TPU v7x, 32 devices: a whole 2x2x4 slice. The times are simulated.
32 devices in a mesh: ctx: 8 (over z, y), head: 4 (over x, core).
Axes of the slice: x: 2, y: 2, z: 4, core: 2. Of those that a mesh axis runs over, the one named last changes fastest.
Arguments:
- query_all: bfloat16 [1024, 1024], P('ctx', 'head'), may hold values from -6 to 6
- key_all: bfloat16 [1024, 1024], P('ctx', 'head'), may hold values from -6 to 6
- value_all: bfloat16 [1024, 1024], P('ctx', 'head'), may hold values from -6 to 6
- cotangent: bfloat16 [1024, 1024], P('ctx', 'head'), may hold values from -6 to 6
- conv_input: bfloat16 [1024, 1024], P('ctx', 'head'), may hold values from -6 to 6
- rec_lengths: int32 [3], replicated, may hold values from 170 to 341
- out_proj: bfloat16 [1024, 1024], P(None, 'head'), may hold values from -0.1875 to 0.1875
- conv_weight: bfloat16 [31, 1024], P(None, 'head'), may hold values from -1 to 1
Outputs:
- q_grad: bfloat16 [1024, 1024], P('ctx', 'head')
- k_grad: bfloat16 [1024, 1024], P('ctx', 'head')
- v_grad: bfloat16 [1024, 1024], P('ctx', 'head')
- x_grad: bfloat16 [1024, 1024], P('ctx', 'head')
- out_proj_grad: float32 [1024, 1024], P('ctx', 'head')
- conv_weight_grad: float32 [31, 1024], P(None, 'head')
Inputs may be any that keep to these rules, and one draw needn't show every extreme that they name: `rec_lengths`: the recordings lie end to end from frame 0; frames from their total on are padding.
All inputs are finite; a program needn't handle non-finite values.
Results may differ from a plain program's by a relative error of at most 0.03.
Values may be sent and summed in bfloat16 or wider, within the bound.
No kernel may reach another device: no remote copies, remote signals or barrier semaphores. Data moves between devices by JAX's collectives and lax.ppermute only.
A program may use at most 64 MiB of HBM per device.

v0:
```python
import jax
import jax.numpy as jnp
from jax import lax
from jax.sharding import PartitionSpec as P

HEAD_DIM = 64


def extended_2(block, sides, width):
    for axis, dim in sides:
        count = lax.axis_size(axis)
        forward = [(i, i + 1) for i in range(count - 1)]
        backward = [(target, source) for source, target in forward]
        low = lax.ppermute(
            lax.slice_in_dim(block, block.shape[dim] - width, None, axis=dim), axis, forward
        )
        high = lax.ppermute(lax.slice_in_dim(block, 0, width, axis=dim), axis, backward)
        block = jnp.concatenate([low, block, high], axis=dim)
    return block


def split_heads(matrix):
    return matrix.reshape(matrix.shape[0], -1, HEAD_DIM)


def join_heads(tensor):
    return jnp.transpose(tensor, (1, 0, 2)).reshape(tensor.shape[1], -1)


def over_blocks(step_fn, running, members):
    row_count = members[0].shape[0]
    blocks = row_count // 512
    stacked = tuple((member.reshape((blocks, 512) + member.shape[1:]) for member in members))

    def inner_step(state, inputs):
        block_members, block_index = inputs
        return (step_fn(state, block_members, block_index * 512), None)

    running, unused = lax.scan(inner_step, running, (stacked, jnp.arange(blocks, dtype=jnp.int32)))
    return running


def conv_forward(extended, taps, frames):
    wide = extended.astype(jnp.float32)
    weights = taps.astype(jnp.float32)
    result = jnp.zeros((frames, extended.shape[1]), jnp.float32)
    for offset in range(taps.shape[0]):
        result = result + weights[offset] * wide[offset : offset + frames]
    return result


def conv_backward(grad_ext, taps, frames):
    wide = grad_ext.astype(jnp.float32)
    weights = taps.astype(jnp.float32)
    reach = taps.shape[0] - 1
    result = jnp.zeros((frames, grad_ext.shape[1]), jnp.float32)
    for offset in range(taps.shape[0]):
        result = result + weights[offset] * wide[reach - offset : reach - offset + frames]
    return result


def tap_products(grad_conv, extended):
    frames = grad_conv.shape[0]
    wide = extended.astype(jnp.float32)
    grad_wide = grad_conv.astype(jnp.float32)
    rows_out = [
        jnp.sum(grad_wide * wide[offset : offset + frames], axis=0)
        for offset in range(extended.shape[0] - frames + 1)
    ]
    return jnp.stack(rows_out)


def gate_slope(conv_out, upstream):
    sigmoid_value = jax.nn.sigmoid(conv_out)
    return (
        upstream.astype(jnp.float32) * sigmoid_value * (1.0 + conv_out * (1.0 - sigmoid_value))
    ).astype(jnp.bfloat16)


def on_device(
    query_all, key_all, value_all, cotangent, conv_input, rec_lengths, out_proj, conv_weight
):
    frames, local_width = query_all.shape
    half_taps = conv_weight.shape[0] // 2
    score_scale = HEAD_DIM ** (-0.5)
    valid_total = jnp.sum(rec_lengths)
    positions = lax.axis_index("ctx") * frames + jnp.arange(frames, dtype=jnp.int32)
    frame_ok = positions < valid_total
    masked = jnp.where(frame_ok[:, None], conv_input, jnp.zeros_like(conv_input))
    input_ext = extended_2(masked, (("ctx", 0),), half_taps)
    conv_out = conv_forward(input_ext, conv_weight, frames)
    grad_conv = gate_slope(conv_out, cotangent)
    grad_ext = extended_2(grad_conv, (("ctx", 0),), half_taps)
    conv_weight_grad = lax.psum(tap_products(grad_conv, input_ext), "ctx")
    grad_input = conv_backward(grad_ext, conv_weight, frames)
    x_grad = (cotangent.astype(jnp.float32) + jnp.where(frame_ok[:, None], grad_input, 0.0)).astype(
        jnp.bfloat16
    )
    full_grad = lax.all_gather(x_grad, "head", axis=1, tiled=True)
    grad_out16 = jnp.dot(full_grad, out_proj, preferred_element_type=jnp.float32).astype(
        jnp.bfloat16
    )
    query_heads = split_heads(query_all)
    grad_heads = split_heads(grad_out16)
    grad_wide = grad_heads.astype(jnp.float32)
    heads_here = query_heads.shape[1]
    start_max = jnp.full((heads_here, frames), -1e30, jnp.float32)
    zeros_sum = jnp.zeros((heads_here, frames), jnp.float32)
    zeros_acc = jnp.zeros((heads_here, frames, HEAD_DIM), jnp.float32)
    zeros_keys = jnp.zeros((frames, heads_here, HEAD_DIM), jnp.float32)

    def masked_scores(key_rows, first_row):
        scores = (
            jnp.einsum(
                "qhd,khd->hqk",
                query_heads,
                split_heads(key_rows),
                preferred_element_type=jnp.float32,
            )
            * score_scale
        )
        key_ok = first_row + jnp.arange(key_rows.shape[0], dtype=jnp.int32) < valid_total
        return jnp.where(key_ok[None, None, :], scores, -jnp.inf)

    def forward_step(running, members, first_row):
        maxima, totals, numer = running
        key_rows, value_rows = members
        scores = masked_scores(key_rows, first_row)
        new_max = jnp.maximum(maxima, jnp.max(scores, axis=-1))
        shrink = jnp.exp(maxima - new_max)
        weights = jnp.exp(scores - new_max[..., None])
        totals = totals * shrink + jnp.sum(weights, axis=-1)
        numer = numer * shrink[..., None] + jnp.einsum(
            "hqk,khd->hqd",
            weights.astype(jnp.bfloat16),
            split_heads(value_rows),
            preferred_element_type=jnp.float32,
        )
        return (new_max, totals, numer)

    maxima, totals, numer = over_blocks(
        forward_step,
        (start_max, zeros_sum, zeros_acc),
        (
            lax.all_gather(key_all, "ctx", axis=0, tiled=True),
            lax.all_gather(value_all, "ctx", axis=0, tiled=True),
        ),
    )
    attn_out = numer / totals[..., None]
    log_total = maxima + jnp.log(totals)
    row_delta = jnp.einsum("qhd,hqd->hq", grad_wide, attn_out)
    query_sum = None

    def query_step(running, members, first_row):
        key_rows, value_rows = members
        scores = masked_scores(key_rows, first_row)
        probs = jnp.exp(scores - log_total[..., None])
        slopes = jnp.einsum(
            "qhd,khd->hqk", grad_heads, split_heads(value_rows), preferred_element_type=jnp.float32
        )
        dscores = probs * (slopes - row_delta[..., None])
        return running + jnp.einsum(
            "hqk,khd->hqd",
            dscores,
            split_heads(key_rows).astype(jnp.float32),
            precision=lax.Precision.HIGHEST,
        )

    query_sum = over_blocks(
        query_step,
        zeros_acc,
        (
            lax.all_gather(key_all, "ctx", axis=0, tiled=True),
            lax.all_gather(value_all, "ctx", axis=0, tiled=True),
        ),
    )
    lse_all, delta_all = (
        lax.all_gather(log_total, "ctx", axis=1, tiled=True),
        lax.all_gather(row_delta, "ctx", axis=1, tiled=True),
    )
    key_heads = split_heads(key_all)
    value_heads = split_heads(value_all)

    def key_step(running, members, first_row):
        key_acc, value_acc = running
        query_rows, grad_rows = members
        rows_here = query_rows.shape[0]
        lse_rows = lax.dynamic_slice_in_dim(lse_all, first_row, rows_here, 1)
        delta_rows = lax.dynamic_slice_in_dim(delta_all, first_row, rows_here, 1)
        scores = (
            jnp.einsum(
                "qhd,khd->hqk",
                split_heads(query_rows),
                key_heads,
                preferred_element_type=jnp.float32,
            )
            * score_scale
        )
        scores = jnp.where(frame_ok[None, None, :], scores, -jnp.inf)
        probs = jnp.exp(scores - lse_rows[..., None])
        probs16 = probs.astype(jnp.bfloat16)
        slopes = jnp.einsum(
            "qhd,khd->hqk", split_heads(grad_rows), value_heads, preferred_element_type=jnp.float32
        )
        dscores16 = (probs * (slopes - delta_rows[..., None])).astype(jnp.bfloat16)
        key_acc = key_acc + jnp.einsum(
            "hqk,qhd->khd", dscores16, split_heads(query_rows), preferred_element_type=jnp.float32
        )
        value_acc = value_acc + jnp.einsum(
            "hqk,qhd->khd", probs16, split_heads(grad_rows), preferred_element_type=jnp.float32
        )
        return (key_acc, value_acc)

    key_sum, value_sum = over_blocks(
        key_step,
        (zeros_keys, zeros_keys),
        (
            lax.all_gather(query_all, "ctx", axis=0, tiled=True),
            lax.all_gather(grad_out16, "ctx", axis=0, tiled=True),
        ),
    )
    q_grad = join_heads(query_sum * score_scale).astype(jnp.bfloat16)
    attn16 = join_heads(attn_out).astype(jnp.bfloat16)
    k_grad = (key_sum * score_scale).reshape(frames, local_width).astype(jnp.bfloat16)
    v_grad = value_sum.reshape(frames, local_width).astype(jnp.bfloat16)
    out_proj_grad = lax.psum_scatter(
        jnp.einsum("ta,tb->ab", full_grad, attn16, preferred_element_type=jnp.float32),
        "ctx",
        scatter_dimension=0,
        tiled=True,
    )
    return (q_grad, k_grad, v_grad, x_grad, out_proj_grad, conv_weight_grad)


def solution(mesh):
    placed = (
        P("ctx", "head"),
        P("ctx", "head"),
        P("ctx", "head"),
        P("ctx", "head"),
        P("ctx", "head"),
        P(),
        P(None, "head"),
        P(None, "head"),
    )
    return jax.shard_map(
        on_device,
        mesh=mesh,
        in_specs=placed,
        out_specs=(
            P("ctx", "head"),
            P("ctx", "head"),
            P("ctx", "head"),
            P("ctx", "head"),
            P("ctx", "head"),
            P(None, "head"),
        ),
        check_vma=False,
    )
```

profile of v0, /device:TPU:0, one launch (start us, length us, event | category | flops | bytes accessed | tf_op | source)
XLA Modules:
  0.0 354.8 jit_solution(6739002948123425645)
XLA Ops:
  10.9 1.3 collective-permute-start.1
  12.2 6.1 %collective-permute-start = (bf16[15,256]{1,0:T(8,128)(2,1)}, bf16[15,256]{1,0:T(8,128)(2,1)}, u32[]{:S(2)}, u32[]{:S(2)}) collective-permute-start(bf16[15,256]{1,0:T(8,128)(2,1)} %get-tuple-element.482), channel_id=1, source_target_pairs={{0,4},{4,8},{8,12},{12,16},{16,20},{20,24},{24,28},{1,5},{5,9},{9,... | collective-permute-start | bytes 23048 | tf_op jit(solution)/shard_map/ppermute | solution.py:14
  20.4 32.4 %all_gather.26 = bf16[1024,256]{1,0:T(8,128)(2,1)S(1)} all-gather(bf16[128,256]{1,0:T(8,128)(2,1)S(1)} %copy-done.13), channel_id=1, replica_groups=mesh['ctx'=8,'head'=4] {'ctx'}, dimensions={0}, use_global_device_ids=true | all-gather | bytes 589824 | tf_op jit(solution)/shard_map/all_gather | solution.py:218
  52.8 31.2 %all_gather.23 = bf16[1024,256]{1,0:T(8,128)(2,1)S(1)} all-gather(bf16[128,256]{1,0:T(8,128)(2,1)S(1)} %copy-done.14), channel_id=1, replica_groups=mesh['ctx'=8,'head'=4] {'ctx'}, dimensions={0}, use_global_device_ids=true | all-gather | bytes 589824 | tf_op jit(solution)/shard_map/all_gather | solution.py:173
  84.8 31.2 %all_gather.24 = bf16[1024,256]{1,0:T(8,128)(2,1)S(1)} all-gather(bf16[128,256]{1,0:T(8,128)(2,1)S(1)} %copy-done.15), channel_id=1, replica_groups=mesh['ctx'=8,'head'=4] {'ctx'}, dimensions={0}, use_global_device_ids=true | all-gather | bytes 589824 | tf_op jit(solution)/shard_map/all_gather | solution.py:174
  116.2 9.9 %while.39 = (s32[]{:T(128)}, f32[4,128]{1,0:T(4,128)S(1)}, f32[4,128]{1,0:T(4,128)S(1)}, f32[4,128,64]{1,2,0:T(8,128)S(1)}, s32[2]{0:T(128)S(1)}, /*index=5*/s32...) while((s32[]{:T(128)}, f32[4,128]{1,0:T(4,128)S(1)}, ...), condition=%wide.region_4.5_spmd.clone, body=%wide.region_1.4_spmd.clone.sunk | while | flops 69045760 | bytes 5080357 | solution.py:39
  126.8 1.6 copy.44
  129.1 26.8 %all_gather.27 = f32[4,1024]{1,0:T(4,128)} all-gather(f32[4,128]{1,0:T(4,128)S(1)} %log_add_fusion), channel_id=1, replica_groups=mesh['ctx'=8,'head'=4] {'ctx'}, dimensions={1}, use_global_device_ids=true | all-gather | bytes 18432 | tf_op jit(solution)/shard_map/all_gather | solution.py:178
  159.0 1.3 collective-permute-start.3
  160.3 4.5 %collective-permute-start.2 = (bf16[15,256]{1,0:T(8,128)(2,1)S(1)}, bf16[15,256]{1,0:T(8,128)(2,1)S(1)}, u32[]{:S(2)}, u32[]{:S(2)}) collective-permute-start(bf16[15,256]{1,0:T(8,128)(2,1)S(1)} %get-tuple-element.480), channel_id=1, source_target_pairs={{0,4},{4,8},{8,12},{12,16},{16,20},{20,24},{24,28},{1,5},{5,9},{9,... | collective-permute-start | bytes 23048 | tf_op jit(solution)/shard_map/ppermute | solution.py:14
  164.9 34.5 %psum.7 = f32[31,256]{1,0:T(8,128)} all-reduce(f32[31,256]{1,0:T(8,128)S(1)} %stack.127), channel_id=1, replica_groups=mesh['ctx'=8,'head'=4] {'ctx'}, use_global_device_ids=true, to_apply=%region_41.42 | all-reduce | flops 7936 | bytes 63488 | tf_op jit(solution)/shard_map/psum | solution.py:94
  201.2 5.8 %all_gather.25 = bf16[128,1024]{1,0:T(8,128)(2,1)S(1)} all-gather(bf16[128,256]{1,0:T(8,128)(2,1)S(1)} %fusion.26), channel_id=1, replica_groups=mesh['ctx'=8,'head'=4] {'head'}, dimensions={1}, use_global_device_ids=true | all-gather | bytes 327680 | tf_op jit(solution)/shard_map/all_gather | solution.py:99
  208.6 33.5 %all_gather.28 = bf16[1024,256]{1,0:T(8,128)(2,1)} all-gather(bf16[128,256]{1,0:T(8,128)(2,1)S(1)} %convolution_convert_fusion), channel_id=1, replica_groups=mesh['ctx'=8,'head'=4] {'ctx'}, dimensions={0}, use_global_device_ids=true | all-gather | bytes 589824 | tf_op jit(solution)/shard_map/all_gather | solution.py:219
  242.2 1.5 fusion.90
  243.6 27.0 %all_gather.29 = f32[4,1024]{1,0:T(4,128)} all-gather(f32[4,128]{1,0:T(4,128)S(1)} %get-tuple-element.773), channel_id=1, replica_groups=mesh['ctx'=8,'head'=4] {'ctx'}, dimensions={1}, use_global_device_ids=true | all-gather | bytes 18432 | tf_op jit(solution)/shard_map/all_gather | solution.py:179
  270.6 12.2 %while.40 = (s32[]{:T(128)}, f32[4,128,64]{1,2,0:T(8,128)}, s32[2]{0:T(128)S(1)}, s32[]{:T(128)}, bf16[2,512,256]{1,2,0:T(8,128)(2,1)S(1)}, /*index=5*/bf16[128,...) while((s32[]{:T(128)}, f32[4,128,64]{1,2,0:T(8,128)}, ...), condition=%wide.region_6.7_spmd.clone, body=%wide.region_5.6_spmd.clone.sunk | while | flops 269812736 | bytes 6427827 | solution.py:39
  280.7 2.1 convolution_add_fusion.5
  284.6 1.3 fusion.97
  287.0 13.6 %while.41 = (s32[]{:T(128)}, f32[128,4,64]{0,2,1:T(8,128)S(1)}, f32[128,4,64]{0,2,1:T(8,128)}, bf16[2,512,256]{2,1,0:T(8,128)(2,1)S(1)}, bf16[128,4,64]{0,2,1:T(...) while((s32[]{:T(128)}, f32[128,4,64]{0,2,1:T(8,128)S(1)}, ...), condition=%wide.region_8.9_spmd.clone, body=%wide.region_7.8_spmd.clone.sunk | while | flops 136184064 | bytes 8045098 | solution.py:39
  289.8 1.3 fusion.164
  291.3 1.5 fusion.165
  296.6 1.3 fusion.164
  298.1 1.6 fusion.165
  302.3 45.7 %reduce-scatter.2.cloned.1.call-done = f32[128,256]{1,0:T(8,128)} async-done(((f32[1024,256]{1,0:T(8,128)}), f32[128,256]{1,0:T(8,128)}) %reduce-scatter.2.cloned.1.call-update) | async-done | bytes 131088 | tf_op jit(solution)/shard_map/reduce_scatter | solution.py:226
  (200 shorter events, 42.3 us)
Async XLA Ops:
  7.2 200.5 %copy-start = (bf16[1024,256]{1,0:T(8,128)(2,1)S(1)}, bf16[1024,256]{1,0:T(8,128)(2,1)}, u32[]{:S(2)}) copy-start(bf16[1024,256]{1,0:T(8,128)(2,1)} %param.20) | copy-start | bytes 1572868
  7.2 340.7 %reduce-scatter.2.cloned.1.call-start = ((), (), s32[]{:S(2)}) async-start(), calls=%async_computation.1 | async-start | bytes 1179648 | tf_op jit(solution)/shard_map/reduce_scatter | solution.py:226
  9.4 9.0 %copy-start.18 = (bf16[31,256]{1,0:T(8,128)(2,1)S(1)}, bf16[31,256]{1,0:T(8,128)(2,1)}, u32[]{:S(2)}) copy-start(bf16[31,256]{1,0:T(8,128)(2,1)} %param.21) | copy-start | bytes 47620
  10.3 9.3 %copy-start.9 = (bf16[128,256]{1,0:T(8,128)(2,1)}, bf16[128,256]{1,0:T(8,128)(2,1)S(1)}, u32[]{:S(2)}) copy-start(bf16[128,256]{1,0:T(8,128)(2,1)S(1)} %broadcast_select_fusion) | copy-start | bytes 196612
  10.3 9.3 %copy-start.13 = (bf16[128,256]{1,0:T(8,128)(2,1)S(1)}, bf16[128,256]{1,0:T(8,128)(2,1)}, u32[]{:S(2)}) copy-start(bf16[128,256]{1,0:T(8,128)(2,1)} %param.14) | copy-start | bytes 196612
  10.9 145.0 %collective-permute-start.1 = (bf16[15,256]{1,0:T(8,128)(2,1)}, bf16[15,256]{1,0:T(8,128)(2,1)}, u32[]{:S(2)}, u32[]{:S(2)}) collective-permute-start(bf16[15,256]{1,0:T(8,128)(2,1)} %get-tuple-element.483), channel_id=1, source_target_pairs={{4,0},{8,4},{12,8},{16,12},{20,16},{24,20},{28,24},{5,1},{9,5},{13... | collective-permute-start | bytes 23048 | tf_op jit(solution)/shard_map/ppermute | solution.py:17
  12.2 143.7 %collective-permute-start = (bf16[15,256]{1,0:T(8,128)(2,1)}, bf16[15,256]{1,0:T(8,128)(2,1)}, u32[]{:S(2)}, u32[]{:S(2)}) collective-permute-start(bf16[15,256]{1,0:T(8,128)(2,1)} %get-tuple-element.482), channel_id=1, source_target_pairs={{0,4},{4,8},{8,12},{12,16},{16,20},{20,24},{24,28},{1,5},{5,9},{9,... | collective-permute-start | bytes 23048 | tf_op jit(solution)/shard_map/ppermute | solution.py:14
  20.4 32.4 %copy-start.14 = (bf16[128,256]{1,0:T(8,128)(2,1)S(1)}, bf16[128,256]{1,0:T(8,128)(2,1)}, u32[]{:S(2)}) copy-start(bf16[128,256]{1,0:T(8,128)(2,1)} %param.15) | copy-start | bytes 196612
  126.8 1.6 copy-start.16
  128.4 27.6 %copy-start.10 = (bf16[128,256]{1,0:T(8,128)(2,1)S(1)}, bf16[128,256]{1,0:T(8,128)(2,1)}, u32[]{:S(2)}) copy-start(bf16[128,256]{1,0:T(8,128)(2,1)} %copy-done.9) | copy-start | bytes 196612
  156.0 1.1 copy-start.20
  156.0 1.1 copy-start.21
  156.0 1.1 copy-start.22
  156.0 1.1 copy-start.23
  156.0 1.1 copy-start.24
  156.0 1.1 copy-start.25
  156.0 1.1 copy-start.26
  156.0 1.1 copy-start.27
  159.0 40.5 %collective-permute-start.3 = (bf16[15,256]{1,0:T(8,128)(2,1)S(1)}, bf16[15,256]{1,0:T(8,128)(2,1)S(1)}, u32[]{:S(2)}, u32[]{:S(2)}) collective-permute-start(bf16[15,256]{1,0:T(8,128)(2,1)S(1)} %get-tuple-element.481), channel_id=1, source_target_pairs={{4,0},{8,4},{12,8},{16,12},{20,16},{24,20},{28,24},{5,1},{9,5},{13... | collective-permute-start | bytes 23048 | tf_op jit(solution)/shard_map/ppermute | solution.py:17
  160.3 39.2 %collective-permute-start.2 = (bf16[15,256]{1,0:T(8,128)(2,1)S(1)}, bf16[15,256]{1,0:T(8,128)(2,1)S(1)}, u32[]{:S(2)}, u32[]{:S(2)}) collective-permute-start(bf16[15,256]{1,0:T(8,128)(2,1)S(1)} %get-tuple-element.480), channel_id=1, source_target_pairs={{0,4},{4,8},{8,12},{12,16},{16,20},{20,24},{24,28},{1,5},{5,9},{9,... | collective-permute-start | bytes 23048 | tf_op jit(solution)/shard_map/ppermute | solution.py:14
  208.6 33.5 %copy-start.6 = (f32[4,128,64]{1,2,0:T(8,128)S(1)}, f32[4,128,64]{1,2,0:T(8,128)}, u32[]{:S(2)}) copy-start(f32[4,128,64]{1,2,0:T(8,128)} %copy-done.5) | copy-start | bytes 393220
  282.8 1.7 copy-start.8
  291.3 1.6 copy-start.2
  298.1 1.6 copy-start.2
  (39 other events, 35.6 us)
Sparse Core Ops, SparseCore 0:
  286.1 61.7 reduce-scatter.1
where the time goes:
time: 356 us; the launch traced here: 355 us
  blocking collectives  222 us (62%)
  waiting for transfers between devices  45.7 us (13%)
  local copies, waits for them, and re-layouts  23.8 us (7%)
  matrix products  19.1 us (5%)
  between operations  14.7 us (4%)
  starting transfers between devices  13.3 us (4%)
  other arithmetic  11.6 us (3%)
  loops' own time  4.23 us (1%)
    reduce_scatter x1, waiting for transfers between devices, on_device(): lax.psum_scatter(jnp.einsum('ta,tb->ab', full_grad, attn16, preferred_ele...  45.7 us
    psum x1, blocking collectives, on_device(): conv_weight_grad = lax.psum(tap_products(grad_conv, input_ext), 'ctx')  34.5 us
    all_gather x1, blocking collectives, on_device(): lax.all_gather(grad_out16, 'ctx', axis=0, tiled=True)  33.5 us
    all_gather x1, blocking collectives, on_device(): lax.all_gather(query_all, 'ctx', axis=0, tiled=True)  32.4 us
    all_gather x1, blocking collectives, on_device(): lax.all_gather(value_all, 'ctx', axis=0, tiled=True)  31.2 us
    all_gather x1, blocking collectives, on_device(): lax.all_gather(key_all, 'ctx', axis=0, tiled=True)  31.2 us
    all_gather x1, blocking collectives, on_device(): lax.all_gather(row_delta, 'ctx', axis=1, tiled=True)  27 us
    all_gather x1, blocking collectives, on_device(): lax.all_gather(log_total, 'ctx', axis=1, tiled=True)  26.8 us
  transfers between devices with their start and end apart: 5, of which 1 were waited for; matrix products, arithmetic and copies ran while one was open for 7% of the time, Pallas kernels for 0%

commit v1 on v0

v1 whole, which is shorter than its diff:
```python
import functools

import jax
import jax.numpy as jnp
from jax import lax
from jax.experimental import pallas as pl
from jax.experimental.pallas import tpu as pltpu
from jax.sharding import PartitionSpec as P

HEAD_DIM = 64
HALO_X = 32
HALO_G = 16
BF = jnp.bfloat16
F32 = jnp.float32
VM = pl.BlockSpec(memory_space=pltpu.VMEM)
SM = pl.BlockSpec(memory_space=pltpu.SMEM)


def dot(a, b, dims):
    return lax.dot_general(a, b, (dims, ((), ())), preferred_element_type=F32)


def call(kernel, out_shape, in_specs, args, scratch=(), flops=1 << 20, limit=None):
    one = not isinstance(out_shape, (tuple, list))
    return pl.pallas_call(
        kernel,
        out_shape=out_shape,
        in_specs=in_specs,
        out_specs=VM if one else tuple(VM for _ in out_shape),
        scratch_shapes=list(scratch),
        compiler_params=pltpu.CompilerParams(vmem_limit_bytes=limit),
        cost_estimate=pl.CostEstimate(flops=flops, bytes_accessed=1 << 20, transcendentals=0),
    )(*args)


def shape(dims, dtype):
    return jax.ShapeDtypeStruct(tuple(dims), dtype)


def pack_kernel(q_ref, k_ref, v_ref, o_ref):
    rows = q_ref.shape[0]
    half = rows // 2
    for m in range(o_ref.shape[0]):
        cols = slice(m * HEAD_DIM, (m + 1) * HEAD_DIM)
        o_ref[m, 0:rows, 0:HEAD_DIM] = k_ref[:, cols]
        o_ref[m, 0:rows, HEAD_DIM:] = v_ref[:, cols]
        o_ref[m, rows:, 0:HEAD_DIM] = q_ref[0:half, cols]
        o_ref[m, rows:, HEAD_DIM:] = q_ref[half:, cols]


def conv_kernel(info_ref, x_ref, g_ref, low_ref, high_ref, w_ref, out_ref, tap_ref, xs, gs):
    rows, width = x_ref.shape
    taps = w_ref.shape[0]
    half = taps // 2
    base, total = info_ref[0], info_ref[1]

    def ok(first, count):
        return (first + lax.broadcasted_iota(jnp.int32, (count, width), 0)) < total

    xs[0:HALO_X] = low_ref[0:HALO_X].astype(F32)
    xs[HALO_X : HALO_X + rows] = x_ref[...].astype(F32)
    xs[HALO_X + rows :] = high_ref[0:HALO_X].astype(F32)
    xs[...] = jnp.where(ok(base - HALO_X, rows + 2 * HALO_X), xs[...], 0.0)
    w = w_ref[...].astype(F32)
    wide = rows + 2 * HALO_G
    shift = HALO_X - HALO_G - half
    acc = jnp.zeros((wide, width), F32)
    for j in range(taps):
        acc = acc + w[j : j + 1] * xs[shift + j : shift + j + wide]
    s = jax.nn.sigmoid(acc)
    slope = s * (1.0 + acc * (1.0 - s))
    gs[0:HALO_G] = low_ref[HALO_X:].astype(F32)
    gs[HALO_G : HALO_G + rows] = g_ref[...].astype(F32)
    gs[HALO_G + rows :] = high_ref[HALO_X:].astype(F32)
    gs[...] = (gs[...] * slope).astype(BF).astype(F32)
    acc = jnp.zeros((rows, width), F32)
    for j in range(taps):
        first = HALO_G + half - j
        acc = acc + w[j : j + 1] * gs[first : first + rows]
    out_ref[...] = (g_ref[...].astype(F32) + jnp.where(ok(base, rows), acc, 0.0)).astype(BF)
    mine = gs[HALO_G : HALO_G + rows]
    for j in range(taps):
        first = HALO_X - half + j
        tap_ref[j : j + 1] = jnp.sum(mine * xs[first : first + rows], axis=0, keepdims=True)
    tap_ref[taps:] = jnp.zeros((tap_ref.shape[0] - taps, width), F32)


def spread_kernel(pieces, full_ref, proj_ref, tap_ref, o_ref):
    rows = full_ref.shape[0]
    half = rows // 2
    go = dot(full_ref[...], proj_ref[...], ((1,), (0,))).astype(BF)
    taps = tap_ref[...].astype(BF)
    n_taps = taps.shape[0]
    for m in range(o_ref.shape[0]):
        cols = slice(m * HEAD_DIM, (m + 1) * HEAD_DIM)
        o_ref[m, 0:half, 0:HEAD_DIM] = go[0:half, cols]
        o_ref[m, 0:half, HEAD_DIM:] = go[half:, cols]
        at = half
        for first in pieces[m]:
            o_ref[m, at : at + rows] = full_ref[:, first : first + 128]
            at += rows
        for side in range(taps.shape[1] // 128):
            o_ref[m, at : at + n_taps] = taps[:, side * 128 : (side + 1) * 128]
            at += n_taps


def widened(x, keep_high):
    x = x.reshape(-1, 128).astype(F32)
    turned = pltpu.roll(x, HEAD_DIM, 1)
    lane = lax.broadcasted_iota(jnp.int32, x.shape, 1)
    used = (lane >= HEAD_DIM) if keep_high else (lane < HEAD_DIM)
    first, second = (turned, x) if keep_high else (x, turned)
    return jnp.concatenate([jnp.where(used, first, 0.0), jnp.where(used, second, 0.0)], 0)


def over(count, body):
    if count <= 2:
        for g in range(count):
            body(g)
    else:
        lax.fori_loop(0, count, lambda g, c: (body(g), c)[1], 0)


def key_block(refs, g):
    if len(refs) == 1:
        block = refs[0][g]
    else:
        block = refs[g][:, 0:128, :]
    return block.reshape(-1, 128)


def forward_kernel(n_keys, scale, start_ref, info_ref, got_ref, *rest):
    kv_refs, (p_ref, a_ref, s_ref, m_ref, l_ref, acc_ref) = rest[:n_keys], rest[n_keys:]
    groups, keys, queries = s_ref.shape
    total = info_ref[1]
    rows = got_ref.shape[1] * 2 // 3
    q = (widened(got_ref[:, rows:, :], False) * scale).astype(BF)
    m_ref[...] = jnp.full(m_ref.shape, -1e30, F32)
    l_ref[...] = jnp.zeros(l_ref.shape, F32)
    acc_ref[...] = jnp.zeros(acc_ref.shape, F32)

    def scores(g):
        s = dot(key_block(kv_refs, g), q, ((1,), (1,)))
        pos = start_ref[g] + lax.broadcasted_iota(jnp.int32, s.shape, 0)
        s = jnp.where(pos < total, s, -1e30)
        s_ref[g] = s
        m_ref[...] = jnp.maximum(m_ref[...], jnp.max(s, axis=0, keepdims=True))

    over(groups, scores)

    def weights(g):
        e = jnp.exp(s_ref[g] - m_ref[...])
        s_ref[g] = e
        l_ref[...] += jnp.sum(e, axis=0, keepdims=True)

    over(groups, weights)
    l_ref[...] = 1.0 / l_ref[...]

    def values(g):
        p = (s_ref[g] * l_ref[...]).astype(BF)
        p_ref[g] = p
        acc_ref[...] += dot(key_block(kv_refs, g), p, ((0,), (0,)))

    over(groups, values)
    attn = acc_ref[HEAD_DIM:, :].T.astype(BF)
    half = queries // 2
    for m in range(a_ref.shape[0]):
        a_ref[m, :, 0:HEAD_DIM] = attn[0:half]
        a_ref[m, :, HEAD_DIM:] = attn[half:]


def backward_kernel(n_keys, scale, p_ref, got_ref, spread_ref, *rest):
    kv_refs, (dkv_ref, dq_ref, s_ref, d_ref, acc_ref) = rest[:n_keys], rest[n_keys:]
    groups, keys, queries = s_ref.shape
    rows = got_ref.shape[1] * 2 // 3
    q = (widened(got_ref[:, rows:, :], False) * scale).astype(BF)
    go = widened(spread_ref[:, 0 : rows // 2, :], True).astype(BF)
    d_ref[...] = jnp.zeros(d_ref.shape, F32)
    acc_ref[...] = jnp.zeros(acc_ref.shape, F32)

    def slopes(g):
        s = dot(key_block(kv_refs, g), go, ((1,), (1,)))
        s_ref[g] = s
        d_ref[...] += jnp.sum(s * p_ref[g].astype(F32), axis=0, keepdims=True)

    over(groups, slopes)

    def grads(g):
        p = p_ref[g]
        ds = (p.astype(F32) * (s_ref[g] - d_ref[...])).astype(BF)
        acc_ref[...] += dot(key_block(kv_refs, g), ds, ((0,), (0,)))
        dkv_ref[g] = (dot(ds, q, ((1,), (0,))) + dot(p, go, ((1,), (0,)))).astype(BF)

    over(groups, grads)
    dq = (acc_ref[0:HEAD_DIM, :] * scale).T.astype(BF)
    half = queries // 2
    dq_ref[:, 0:HEAD_DIM] = dq[0:half]
    dq_ref[:, HEAD_DIM:] = dq[half:]


def project_kernel(spread_ref, attn_ref, o_ref, lhs, rhs):
    members, _, _ = spread_ref.shape
    half = attn_ref.shape[1] // members
    rows = 2 * half
    width = lhs.shape[1]
    acc = jnp.zeros((width, rhs.shape[1]), F32)
    for fold in range(2):
        for i in range(members):
            for side in range(width // 128):
                first = half + side * rows + fold * half
                lhs[i * half : (i + 1) * half, side * 128 : (side + 1) * 128] = spread_ref[
                    i, first : first + half, :
                ]
            rhs[:, i * HEAD_DIM : (i + 1) * HEAD_DIM] = attn_ref[
                i, :, fold * HEAD_DIM : (fold + 1) * HEAD_DIM
            ]
        acc = acc + dot(lhs[...], rhs[...], ((0,), (0,)))
    o_ref[...] = acc


def collect_kernel(kv_ref, dq_ref, o_ref):
    members = o_ref.shape[0]
    rows = o_ref.shape[1] * 2 // 3
    half = rows // 2
    total = kv_ref[0].astype(F32)
    for g in range(1, kv_ref.shape[0]):
        total = total + kv_ref[g].astype(F32)
    total = total.astype(BF)
    for m in range(members):
        o_ref[m, 0:rows, :] = total[m * rows : (m + 1) * rows]
        o_ref[m, rows:, :] = dq_ref[m * half : (m + 1) * half, :]


def unpack_kernel(got_ref, q_ref, k_ref, v_ref):
    rows = q_ref.shape[0]
    half = rows // 2
    for m in range(got_ref.shape[0]):
        cols = slice(m * HEAD_DIM, (m + 1) * HEAD_DIM)
        k_ref[:, cols] = got_ref[m, 0:rows, 0:HEAD_DIM]
        v_ref[:, cols] = got_ref[m, 0:rows, HEAD_DIM:]
        q_ref[0:half, cols] = got_ref[m, rows:, 0:HEAD_DIM]
        q_ref[half:, cols] = got_ref[m, rows:, HEAD_DIM:]


def on_device(
    query_all, key_all, value_all, cotangent, conv_input, rec_lengths, out_proj, conv_weight
):
    rows, width = query_all.shape
    half = rows // 2
    members = width // HEAD_DIM
    n_ctx = lax.axis_size("ctx")
    groups = n_ctx // members
    channels = out_proj.shape[0]
    own_rows = channels // n_ctx
    scale = HEAD_DIM**-0.5
    taps = conv_weight.shape[0]
    tap_rows = -(-taps // 16) * 16
    keys = members * rows
    inside = [[g * members + m for m in range(members)] for g in range(groups)]
    across = [[g * members + m for g in range(groups)] for m in range(members)]
    me = lax.axis_index("ctx")
    group = me // members
    total = jnp.sum(rec_lengths)
    info = jnp.stack([me * rows, total]).astype(jnp.int32)

    def swap(x):
        return lax.all_to_all(x, "ctx", 0, 0, axis_index_groups=inside)

    other = [(i, (i + members) % n_ctx) for i in range(n_ctx)]

    def exchange(parts):
        if groups == 2:
            mine = lax.dynamic_index_in_dim(parts, group, 0, keepdims=False)
            theirs = lax.dynamic_index_in_dim(parts, 1 - group, 0, keepdims=False)
            return jnp.stack([mine, lax.ppermute(theirs, "ctx", other)])
        return lax.all_to_all(parts, "ctx", 0, 0, axis_index_groups=across)

    up = [(i, i + 1) for i in range(n_ctx - 1)]
    down = [(i + 1, i) for i in range(n_ctx - 1)]
    low = lax.ppermute(
        jnp.concatenate([conv_input[rows - HALO_X :], cotangent[rows - HALO_G :]], 0), "ctx", up
    )
    high = lax.ppermute(
        jnp.concatenate([conv_input[:HALO_X], cotangent[:HALO_G]], 0), "ctx", down
    )
    packed = call(
        pack_kernel, shape((members, rows + half, 128), BF), [VM] * 3, (query_all, key_all, value_all)
    )
    got = swap(packed)
    own_kv = got[:, :rows]
    if groups == 2:
        kv = (got, lax.ppermute(own_kv, "ctx", other))
        starts = jnp.stack([group, 1 - group]).astype(jnp.int32) * keys
    else:
        kv = (lax.all_gather(own_kv, "ctx", axis_index_groups=across),)
        starts = jnp.arange(groups, dtype=jnp.int32) * keys
    n_keys = len(kv)
    x_grad, tap_part = call(
        conv_kernel,
        (shape((rows, width), BF), shape((tap_rows, width), F32)),
        [SM] + [VM] * 5,
        (info, conv_input, cotangent, low, high, conv_weight),
        scratch=[pltpu.VMEM((rows + 2 * HALO_X, width), F32), pltpu.VMEM((rows + 2 * HALO_G, width), F32)],
    )
    full = lax.all_gather(x_grad, "head", axis=1, tiled=True)
    slot_channels = groups * own_rows
    if own_rows % 128 == 0:
        ordered = full
        pieces = [
            [(g * members + m) * own_rows + b for g in range(groups) for b in range(0, own_rows, 128)]
            for m in range(members)
        ]
        proj = out_proj
    else:

        def in_order(x, dim):
            split = x.shape[:dim] + (groups, members, own_rows) + x.shape[dim + 1 :]
            return jnp.swapaxes(x.reshape(split), dim, dim + 1).reshape(x.shape)

        ordered = in_order(full, 1)
        proj = in_order(out_proj, 0)
        pieces = [list(range(m * slot_channels, (m + 1) * slot_channels, 128)) for m in range(members)]
    slot_rows = half + slot_channels // 128 * rows + tap_rows * (width // 128)
    spread = swap(
        call(
            functools.partial(spread_kernel, pieces),
            shape((members, slot_rows, 128), BF),
            [VM] * 3,
            (ordered, proj, tap_part),
            flops=2 * rows * channels * width,
        )
    )
    queries = members * rows
    big = 60 << 20
    flops = 2 * queries * keys * groups * 128
    probs, attn = call(
        functools.partial(forward_kernel, n_keys, scale),
        (shape((groups, keys, queries), BF), shape((members, queries // 2, 128), BF)),
        [SM, SM, VM] + [VM] * n_keys,
        (starts, info, got) + kv,
        scratch=[
            pltpu.VMEM((groups, keys, queries), F32),
            pltpu.VMEM((1, queries), F32),
            pltpu.VMEM((1, queries), F32),
            pltpu.VMEM((128, queries), F32),
        ],
        flops=2 * flops,
        limit=big,
    )
    attn_all = swap(attn)
    dkv, dq = call(
        functools.partial(backward_kernel, n_keys, scale),
        (shape((groups, keys, 128), BF), shape((queries // 2, 128), BF)),
        [VM] * (3 + n_keys),
        (probs, got, spread) + kv,
        scratch=[
            pltpu.VMEM((groups, keys, queries), F32),
            pltpu.VMEM((1, queries), F32),
            pltpu.VMEM((128, queries), F32),
        ],
        flops=4 * flops,
        limit=big,
    )
    partial = call(
        project_kernel,
        shape((slot_channels, width), F32),
        [VM] * 2,
        (spread, attn_all),
        scratch=[pltpu.VMEM((members * half, slot_channels), BF), pltpu.VMEM((members * half, width), BF)],
        flops=2 * slot_channels * width * queries,
    ).reshape(groups, own_rows, width)
    out_proj_grad = jnp.sum(exchange(partial.astype(BF)).astype(F32), 0)
    tap_sum = jnp.sum(
        spread[:, half + slot_channels // 128 * rows :].astype(F32), 0
    ).astype(BF)
    tap_all = exchange(jnp.broadcast_to(tap_sum, (groups,) + tap_sum.shape)).astype(F32)
    tap_all = jnp.sum(tap_all, 0).reshape(width // 128, tap_rows, 128)
    conv_weight_grad = jnp.swapaxes(tap_all, 0, 1).reshape(tap_rows, width)[:taps]
    if groups == 2:
        parts = jnp.stack([dkv[0], lax.ppermute(dkv[1], "ctx", other)])
    else:
        parts = exchange(dkv)
    back = swap(
        call(collect_kernel, shape((members, rows + half, 128), BF), [VM] * 2, (parts, dq))
    )
    q_grad, k_grad, v_grad = call(
        unpack_kernel, (shape((rows, width), BF),) * 3, [VM], (back,)
    )
    return (q_grad, k_grad, v_grad, x_grad, out_proj_grad, conv_weight_grad)


def solution(mesh):
    placed = (
        P("ctx", "head"),
        P("ctx", "head"),
        P("ctx", "head"),
        P("ctx", "head"),
        P("ctx", "head"),
        P(),
        P(None, "head"),
        P(None, "head"),
    )
    return jax.shard_map(
        on_device,
        mesh=mesh,
        in_specs=placed,
        out_specs=(
            P("ctx", "head"),
            P("ctx", "head"),
            P("ctx", "head"),
            P("ctx", "head"),
            P("ctx", "head"),
            P(None, "head"),
        ),
        check_vma=False,
    )
```

time: 356 us -> 89.4 us (0.25)
  blocking collectives: 222 us -> 7.39 us
  waiting for transfers between devices: 45.7 us -> 17 us
  Pallas kernels: 0 us -> 20.4 us
  matrix products: 19.1 us -> 0 us
  starting transfers between devices: 13.3 us -> 31.5 us
  local copies, waits for them, and re-layouts: 23.8 us -> 5.75 us
  between operations: 14.7 us -> 0.75 us
  other arithmetic: 11.6 us -> 5.68 us
  loops' own time: 4.23 us -> 0 us
    all_gather x7 -> x1, blocking collectives: 188 us -> 7.39 us  [on_device(): full = lax.all_gather(x_grad, 'head', axis=1, tiled=True)]
    reduce_scatter x1 -> x0, waiting for transfers between devices: 45.7 us -> none  [on_device(): lax.psum_scatter(jnp.einsum('ta,tb->ab', full_grad, attn16, preferred_ele...]
    psum x1 -> x0, blocking collectives: 34.5 us -> none  [on_device(): conv_weight_grad = lax.psum(tap_products(grad_conv, input_ext), 'ctx')]
    pallas_call x0 -> x8, Pallas kernels: none -> 20.4 us  [call(): pl.pallas_call(kernel, out_shape=out_shape, in_specs=in_specs, out_specs=...]
    dot_general x18 -> x0, matrix products: 19.1 us -> none  [the longest x4 5.01 us: masked_scores(): jnp.einsum('qhd,khd->hqk', query_heads, split_heads(key_rows), preferred_...]
    all_to_all x0 -> x4, starting transfers between devices: none -> 19 us  [swap(): return lax.all_to_all(x, 'ctx', 0, 0, axis_index_groups=inside)]
    ppermute x4 -> x6, waiting for transfers between devices: 0.01 us -> 17 us  [the longest x1 7.2 us: on_device(): parts = jnp.stack([dkv[0], lax.ppermute(dkv[1], 'ctx', other)])]
    unnamed x108 -> x18, local copies, waits for them, and re-layouts: 11.6 us -> 3.25 us
  transfers between devices with their start and end apart: 5 -> 10, of which waited for: 1 -> 4; matrix products, arithmetic and copies ran while one was open for 7% -> 8% of each run, Pallas kernels for 0% -> 21%
where the time goes in v1:
time: 89.4 us; the launch traced here: 88.4 us
  starting transfers between devices  31.5 us (35%)
  Pallas kernels  20.4 us (23%)
  waiting for transfers between devices  17 us (19%)
  blocking collectives  7.39 us (8%)
  local copies, waits for them, and re-layouts  5.75 us (6%)
  other arithmetic  5.68 us (6%)
    pallas_call x8, Pallas kernels, call(): pl.pallas_call(kernel, out_shape=out_shape, in_specs=in_specs, out_specs=...  20.4 us
    all_to_all x4, starting transfers between devices, swap(): return lax.all_to_all(x, 'ctx', 0, 0, axis_index_groups=inside)  19 us
    all_gather x1, blocking collectives, on_device(): full = lax.all_gather(x_grad, 'head', axis=1, tiled=True)  7.39 us
    ppermute x1, waiting for transfers between devices, on_device(): parts = jnp.stack([dkv[0], lax.ppermute(dkv[1], 'ctx', other)])  7.2 us
    ppermute x1, waiting for transfers between devices, on_device(): kv = (got, lax.ppermute(own_kv, 'ctx', other))  4.97 us
    ppermute x1, starting transfers between devices, on_device(): lax.ppermute(jnp.concatenate([conv_input[rows - HALO_X:], cotangent[rows...  4.89 us
    unnamed x18, local copies, waits for them, and re-layouts  3.25 us
    ppermute x2, starting transfers between devices, exchange(): return jnp.stack([mine, lax.ppermute(theirs, 'ctx', other)])  3.06 us
  transfers between devices with their start and end apart: 10, of which 4 were waited for; matrix products, arithmetic and copies ran while one was open for 8% of the time, Pallas kernels for 21%

profile of v1, /device:TPU:0, one launch (start us, length us, event | category | flops | bytes accessed | tf_op | source)
XLA Modules:
  0.0 88.4 jit_solution(16556267574643059748)
XLA Ops:
  2.1 4.9 %collective-permute-start.1 = (bf16[48,256]{1,0:T(8,128)(2,1)S(1)}, bf16[48,256]{1,0:T(8,128)(2,1)S(1)}, u32[]{:S(2)}, u32[]{:S(2)}) collective-permute-start(bf16[48,256]{1,0:T(8,128)(2,1)S(1)} %pad_maximum_fusion.1), channel_id=1, source_target_pairs={{0,4},{4,8},{8,12},{12,16},{16,20},{20,24},{24,28},{1,5},{5,9},{9,... | collective-permute-start | bytes 73736 | tf_op jit(solution)/shard_map/ppermute | solution.py:280
  7.0 1.8 %shard_map.127 = bf16[4,192,128]{2,1,0:T(8,128)(2,1)} custom-call(bf16[128,256]{1,0:T(8,128)(2,1)} %q_ref.1, bf16[128,256]{1,0:T(8,128)(2,1)} %k_ref.1, bf16[128,256]{1,0:T(8,128)(2,1)} %v_ref.1), custom_call_target="tpu_custom_call" | custom-call | flops 1048576 | bytes 1048576 | tf_op jit(solution)/shard_map/pallas_call | solution.py:25
  8.7 3.8 %all-to-all-start = ((bf16[4,192,128]{2,1,0:T(8,128)(2,1)}), bf16[4,192,128]{2,1,0:T(8,128)(2,1)S(1)}, u32[]{:S(2)}, u32[]{:S(2)}) async-start(bf16[4,192,128]{2,1,0:T(8,128)(2,1)} %shard_map.127), calls=%async_computation | async-start | bytes 393216 | tf_op jit(solution)/shard_map/all_to_all | solution.py:267
  12.5 1.3 %collective-permute-start.2 = (bf16[48,256]{1,0:T(8,128)(2,1)S(1)}, bf16[48,256]{1,0:T(8,128)(2,1)S(1)}, u32[]{:S(2)}, u32[]{:S(2)}) collective-permute-start(bf16[48,256]{1,0:T(8,128)(2,1)S(1)} %pad_maximum_fusion.2), channel_id=1, source_target_pairs={{4,0},{8,4},{12,8},{16,12},{20,16},{24,20},{28,24},{5,1},{9,5},{13... | collective-permute-start | bytes 73736 | tf_op jit(solution)/shard_map/ppermute | solution.py:283
  15.1 1.2 %pad_add_fusion.info_ref = s32[2]{0:T(128)} fusion(s32[1]{0:T(128)} %bitcast.3, s32[1]{0:T(128)} %bitcast.2), kind=kLoop, calls=%fused_computation.9 | loop fusion | flops 2 | bytes 16 | tf_op jit(solution)/shard_map/stack | solution.py:264
  16.4 1.9 %collective-permute-done.2.high_ref = bf16[48,256]{1,0:T(8,128)(2,1)S(1)} collective-permute-done((bf16[48,256]{1,0:T(8,128)(2,1)S(1)}, bf16[48,256]{1,0:T(8,128)(2,1)S(1)}, u32[]{:S(2)}, u32[]{:S(2)}) %collective-permute-start.2) | collective-permute-done | bytes 24608 | tf_op jit(solution)/shard_map/ppermute | solution.py:283
  18.9 3.6 %shard_map.129 = (bf16[128,256]{1,0:T(8,128)(2,1)}, f32[32,256]{1,0:T(8,128)}) custom-call(s32[2]{0:T(128)} %pad_add_fusion.info_ref, bf16[128,256]{1,0:T(8,128)(2,1)} %x_ref.1, bf16[128,256]{1,0:T(8,128)(2,1)} %g_ref.1, bf16[48,256]{1,0:T(8,128)(2,1)} %copy-done.4, bf16[48,256]{1,0:T(8,128)(2,1)} %copy-done.5, bf16[31,256]{1,0:T(8,128)(2,1)} %w_ref.1), custom_call_target="tpu_custom_call" | custom-call | flops 1048576 | bytes 1048576 | tf_op jit(solution)/shard_map/pallas_call | solution.py:25
  22.5 7.4 %all_gather.3.full_ref = bf16[128,1024]{1,0:T(8,128)(2,1)} all-gather(bf16[128,256]{1,0:T(8,128)(2,1)} %get-tuple-element.12), channel_id=1, replica_groups=mesh['ctx'=8,'head'=4] {'head'}, dimensions={1}, use_global_device_ids=true | all-gather | bytes 327680 | tf_op jit(solution)/shard_map/all_gather | solution.py:305
  29.8 2.2 %shard_map.130 = bf16[4,384,128]{2,1,0:T(8,128)(2,1)} custom-call(bf16[128,1024]{1,0:T(8,128)(2,1)} %all_gather.3.full_ref, bf16[1024,256]{1,0:T(8,128)(2,1)} %proj_ref.1, f32[32,256]{1,0:T(8,128)} %get-tuple-element.17.tap_ref), custom_call_target="tpu_custom_call" | custom-call | flops 67108864 | bytes 1048576 | tf_op jit(solution)/shard_map/pallas_call | solution.py:25
  32.0 5.1 %all-to-all-start.1 = ((bf16[4,384,128]{2,1,0:T(8,128)(2,1)}), bf16[4,384,128]{2,1,0:T(8,128)(2,1)S(1)}, u32[]{:S(2)}, u32[]{:S(2)}) async-start(bf16[4,384,128]{2,1,0:T(8,128)(2,1)} %shard_map.130), calls=%async_computation.1 | async-start | bytes 786432 | tf_op jit(solution)/shard_map/all_to_all | solution.py:267
  37.1 2.2 %collective-permute-start = (bf16[4,128,128]{2,1,0:T(8,128)(2,1)S(1)}, bf16[4,128,128]{2,1,0:T(8,128)(2,1)S(1)}, u32[]{:S(2)}, u32[]{:S(2)}) collective-permute-start(bf16[4,128,128]{2,1,0:T(8,128)(2,1)S(1)} %slice.40), channel_id=1, source_target_pairs={{0,16},{4,20},{8,24},{12,28},{16,0},{20,4},{24,8},{28,12},{1,17},{... | collective-permute-start | bytes 393224 | tf_op jit(solution)/shard_map/ppermute | solution.py:292
  39.9 5.0 %collective-permute-done.rest_1_ = bf16[4,128,128]{2,1,0:T(8,128)(2,1)S(1)} collective-permute-done((bf16[4,128,128]{2,1,0:T(8,128)(2,1)S(1)}, bf16[4,128,128]{2,1,0:T(8,128)(2,1)S(1)}, u32[]{:S(2)}, u32[]{:S(2)}) %collective-permute-start) | collective-permute-done | bytes 131104 | tf_op jit(solution)/shard_map/ppermute | solution.py:292
  45.5 3.3 %shard_map.128 = (bf16[2,512,512]{2,1,0:T(8,128)(2,1)}, bf16[4,256,128]{2,1,0:T(8,128)(2,1)}) custom-call(s32[2]{0:T(128)} %add_multiply_fusion.start_ref, s32[2]{0:T(128)} %pad_add_fusion.info_ref, bf16[4,192,128]{2,1,0:T(8,128)(2,1)} %copy-done.3, bf16[4,192,128]{2,1,0:T(8,128)(2,1)} %copy-done.3, bf16[4,128,128]{2,1,0:T(8,128)(2,1)} %copy-done.6), custom_call_target="tpu_custom_call" | custom-call | flops 268435456 | bytes 1048576 | tf_op jit(solution)/shard_map/pallas_call | solution.py:25
  48.8 6.7 %all-to-all-start.3 = ((bf16[4,256,128]{2,1,0:T(8,128)(2,1)}), bf16[4,256,128]{2,1,0:T(8,128)(2,1)S(1)}, u32[]{:S(2)}, u32[]{:S(2)}) async-start(bf16[4,256,128]{2,1,0:T(8,128)(2,1)} %get-tuple-element.23), calls=%async_computation.3 | async-start | bytes 524288 | tf_op jit(solution)/shard_map/all_to_all | solution.py:267
  55.6 3.8 %shard_map.131 = (bf16[2,512,128]{2,1,0:T(8,128)(2,1)}, bf16[256,128]{1,0:T(8,128)(2,1)}) custom-call(bf16[2,512,512]{2,1,0:T(8,128)(2,1)} %get-tuple-element.15.p_ref, bf16[4,192,128]{2,1,0:T(8,128)(2,1)} %copy-done.3, bf16[4,384,128]{2,1,0:T(8,128)(2,1)} %copy-done, bf16[4,192,128]{2,1,0:T(8,128)(2,1)} %copy-done.3, bf16[4,128,128]{2,1,0:T(8,128)(2,1)} %copy-done.6), custom_call_target="tpu_custom_call" | custom-call | flops 536870912 | bytes 1048576 | tf_op jit(solution)/shard_map/pallas_call | solution.py:25
  59.4 1.0 %fusion = (bf16[1,512,128]{2,1,0:T(8,128)(2,1)S(1)}, bf16[512,128]{1,0:T(8,128)(2,1)S(1)}) fusion(bf16[2,512,128]{2,1,0:T(8,128)(2,1)} %get-tuple-element.18), kind=kLoop, calls=%fused_computation.11 | loop fusion | bytes 524288 | tf_op jit(solution)/shard_map/slice | solution.py:380
  60.4 1.2 %collective-permute-start.3 = (bf16[512,128]{1,0:T(8,128)(2,1)S(1)}, bf16[512,128]{1,0:T(8,128)(2,1)S(1)}, u32[]{:S(2)}, u32[]{:S(2)}) collective-permute-start(bf16[512,128]{1,0:T(8,128)(2,1)S(1)} %get-tuple-element.25), channel_id=1, source_target_pairs={{0,16},{4,20},{8,24},{12,28},{16,0},{20,4},{24,8},{28,12},{1,17},{... | collective-permute-start | bytes 393224 | tf_op jit(solution)/shard_map/ppermute | solution.py:380
  61.5 7.2 %collective-permute-done.3 = bf16[512,128]{1,0:T(8,128)(2,1)S(1)} collective-permute-done((bf16[512,128]{1,0:T(8,128)(2,1)S(1)}, bf16[512,128]{1,0:T(8,128)(2,1)S(1)}, u32[]{:S(2)}, u32[]{:S(2)}) %collective-permute-start.3) | collective-permute-done | bytes 131104 | tf_op jit(solution)/shard_map/ppermute | solution.py:380
  69.5 1.7 %shard_map.132 = bf16[4,192,128]{2,1,0:T(8,128)(2,1)} custom-call(bf16[2,512,128]{2,1,0:T(8,128)(2,1)} %pad_maximum_fusion.kv_ref, bf16[256,128]{1,0:T(8,128)(2,1)} %get-tuple-element.19.dq_ref), custom_call_target="tpu_custom_call" | custom-call | flops 1048576 | bytes 1048576 | tf_op jit(solution)/shard_map/pallas_call | solution.py:25
  71.2 3.4 %all-to-all-start.2 = ((bf16[4,192,128]{2,1,0:T(8,128)(2,1)}), bf16[4,192,128]{2,1,0:T(8,128)(2,1)S(1)}, u32[]{:S(2)}, u32[]{:S(2)}) async-start(bf16[4,192,128]{2,1,0:T(8,128)(2,1)} %shard_map.132), calls=%async_computation.2 | async-start | bytes 393216 | tf_op jit(solution)/shard_map/all_to_all | solution.py:267
  74.6 2.2 %shard_map.134 = f32[256,256]{1,0:T(8,128)} custom-call(bf16[4,384,128]{2,1,0:T(8,128)(2,1)} %copy-done, bf16[4,256,128]{2,1,0:T(8,128)(2,1)} %copy-done.1), custom_call_target="tpu_custom_call" | custom-call | flops 67108864 | bytes 1048576 | tf_op jit(solution)/shard_map/pallas_call | solution.py:25
  79.6 2.1 %collective-permute-start.5 = (bf16[64,128]{1,0:T(8,128)(2,1)S(1)}, bf16[64,128]{1,0:T(8,128)(2,1)S(1)}, u32[]{:S(2)}, u32[]{:S(2)}) collective-permute-start(bf16[64,128]{1,0:T(8,128)(2,1)S(1)} %slice_reduce_fusion), channel_id=1, source_target_pairs={{0,16},{4,20},{8,24},{12,28},{16,0},{20,4},{24,8},{28,12},{1,17},{... | collective-permute-start | bytes 49160 | tf_op jit(solution)/shard_map/ppermute | solution.py:275
  81.7 2.9 %collective-permute-done.5 = bf16[64,128]{1,0:T(8,128)(2,1)S(1)} collective-permute-done((bf16[64,128]{1,0:T(8,128)(2,1)S(1)}, bf16[64,128]{1,0:T(8,128)(2,1)S(1)}, u32[]{:S(2)}, u32[]{:S(2)}) %collective-permute-start.5) | collective-permute-done | bytes 16416 | tf_op jit(solution)/shard_map/ppermute | solution.py:275
  86.7 1.8 %shard_map.133 = (bf16[128,256]{1,0:T(8,128)(2,1)}, bf16[128,256]{1,0:T(8,128)(2,1)}, bf16[128,256]{1,0:T(8,128)(2,1)}) custom-call(bf16[4,192,128]{2,1,0:T(8,128)(2,1)} %copy-done.2), custom_call_target="tpu_custom_call" | custom-call | flops 1048576 | bytes 1048576 | tf_op jit(solution)/shard_map/pallas_call | solution.py:25
  (39 shorter events, 10.2 us)
Async XLA Ops:
  2.1 14.3 %collective-permute-start.1 = (bf16[48,256]{1,0:T(8,128)(2,1)S(1)}, bf16[48,256]{1,0:T(8,128)(2,1)S(1)}, u32[]{:S(2)}, u32[]{:S(2)}) collective-permute-start(bf16[48,256]{1,0:T(8,128)(2,1)S(1)} %pad_maximum_fusion.1), channel_id=1, source_target_pairs={{0,4},{4,8},{8,12},{12,16},{16,20},{20,24},{24,28},{1,5},{5,9},{9,... | collective-permute-start | bytes 73736 | tf_op jit(solution)/shard_map/ppermute | solution.py:280
  8.7 23.3 %all-to-all-start = ((bf16[4,192,128]{2,1,0:T(8,128)(2,1)}), bf16[4,192,128]{2,1,0:T(8,128)(2,1)S(1)}, u32[]{:S(2)}, u32[]{:S(2)}) async-start(bf16[4,192,128]{2,1,0:T(8,128)(2,1)} %shard_map.127), calls=%async_computation | async-start | bytes 393216 | tf_op jit(solution)/shard_map/all_to_all | solution.py:267
  12.5 5.7 %collective-permute-start.2 = (bf16[48,256]{1,0:T(8,128)(2,1)S(1)}, bf16[48,256]{1,0:T(8,128)(2,1)S(1)}, u32[]{:S(2)}, u32[]{:S(2)}) collective-permute-start(bf16[48,256]{1,0:T(8,128)(2,1)S(1)} %pad_maximum_fusion.2), channel_id=1, source_target_pairs={{4,0},{8,4},{12,8},{16,12},{20,16},{24,20},{28,24},{5,1},{9,5},{13... | collective-permute-start | bytes 73736 | tf_op jit(solution)/shard_map/ppermute | solution.py:283
  13.8 0.7 copy-start.7
  16.4 1.9 %copy-start.4 = (bf16[48,256]{1,0:T(8,128)(2,1)}, bf16[48,256]{1,0:T(8,128)(2,1)S(1)}, u32[]{:S(2)}) copy-start(bf16[48,256]{1,0:T(8,128)(2,1)S(1)} %collective-permute-done.1.low_ref) | copy-start | bytes 73732
  18.3 0.6 copy-start.5
  32.0 5.1 %copy-start.3 = (bf16[4,192,128]{2,1,0:T(8,128)(2,1)}, bf16[4,192,128]{2,1,0:T(8,128)(2,1)S(1)}, u32[]{:S(2)}) copy-start(bf16[4,192,128]{2,1,0:T(8,128)(2,1)S(1)} %all-to-all-done.got_ref.rest_0_) | copy-start | bytes 589828
  32.0 16.8 %all-to-all-start.1 = ((bf16[4,384,128]{2,1,0:T(8,128)(2,1)}), bf16[4,384,128]{2,1,0:T(8,128)(2,1)S(1)}, u32[]{:S(2)}, u32[]{:S(2)}) async-start(bf16[4,384,128]{2,1,0:T(8,128)(2,1)} %shard_map.130), calls=%async_computation.1 | async-start | bytes 786432 | tf_op jit(solution)/shard_map/all_to_all | solution.py:267
  37.1 7.7 %collective-permute-start = (bf16[4,128,128]{2,1,0:T(8,128)(2,1)S(1)}, bf16[4,128,128]{2,1,0:T(8,128)(2,1)S(1)}, u32[]{:S(2)}, u32[]{:S(2)}) collective-permute-start(bf16[4,128,128]{2,1,0:T(8,128)(2,1)S(1)} %slice.40), channel_id=1, source_target_pairs={{0,16},{4,20},{8,24},{12,28},{16,0},{20,4},{24,8},{28,12},{1,17},{... | collective-permute-start | bytes 393224 | tf_op jit(solution)/shard_map/ppermute | solution.py:292
  44.9 0.7 copy-start.6
  48.8 6.7 %copy-start = (bf16[4,384,128]{2,1,0:T(8,128)(2,1)}, bf16[4,384,128]{2,1,0:T(8,128)(2,1)S(1)}, u32[]{:S(2)}) copy-start(bf16[4,384,128]{2,1,0:T(8,128)(2,1)S(1)} %all-to-all-done.1.spread_ref) | copy-start | bytes 1179652
  48.8 22.3 %all-to-all-start.3 = ((bf16[4,256,128]{2,1,0:T(8,128)(2,1)}), bf16[4,256,128]{2,1,0:T(8,128)(2,1)S(1)}, u32[]{:S(2)}, u32[]{:S(2)}) async-start(bf16[4,256,128]{2,1,0:T(8,128)(2,1)} %get-tuple-element.23), calls=%async_computation.3 | async-start | bytes 524288 | tf_op jit(solution)/shard_map/all_to_all | solution.py:267
  60.4 8.4 %collective-permute-start.3 = (bf16[512,128]{1,0:T(8,128)(2,1)S(1)}, bf16[512,128]{1,0:T(8,128)(2,1)S(1)}, u32[]{:S(2)}, u32[]{:S(2)}) collective-permute-start(bf16[512,128]{1,0:T(8,128)(2,1)S(1)} %get-tuple-element.25), channel_id=1, source_target_pairs={{0,16},{4,20},{8,24},{12,28},{16,0},{20,4},{24,8},{28,12},{1,17},{... | collective-permute-start | bytes 393224 | tf_op jit(solution)/shard_map/ppermute | solution.py:380
  71.2 3.4 %copy-start.1 = (bf16[4,256,128]{2,1,0:T(8,128)(2,1)}, bf16[4,256,128]{2,1,0:T(8,128)(2,1)S(1)}, u32[]{:S(2)}) copy-start(bf16[4,256,128]{2,1,0:T(8,128)(2,1)S(1)} %all-to-all-done.3.attn_ref) | copy-start | bytes 786436
  71.2 14.8 %all-to-all-start.2 = ((bf16[4,192,128]{2,1,0:T(8,128)(2,1)}), bf16[4,192,128]{2,1,0:T(8,128)(2,1)S(1)}, u32[]{:S(2)}, u32[]{:S(2)}) async-start(bf16[4,192,128]{2,1,0:T(8,128)(2,1)} %shard_map.132), calls=%async_computation.2 | async-start | bytes 393216 | tf_op jit(solution)/shard_map/all_to_all | solution.py:267
  77.8 7.5 %collective-permute-start.4 = (bf16[128,256]{1,0:T(8,128)(2,1)S(1)}, bf16[128,256]{1,0:T(8,128)(2,1)S(1)}, u32[]{:S(2)}, u32[]{:S(2)}) collective-permute-start(bf16[128,256]{1,0:T(8,128)(2,1)S(1)} %get-tuple-element.27), channel_id=1, source_target_pairs={{0,16},{4,20},{8,24},{12,28},{16,0},{20,4},{24,8},{28,12},{1,17},{... | collective-permute-start | bytes 196616 | tf_op jit(solution)/shard_map/ppermute | solution.py:275
  79.6 5.0 %collective-permute-start.5 = (bf16[64,128]{1,0:T(8,128)(2,1)S(1)}, bf16[64,128]{1,0:T(8,128)(2,1)S(1)}, u32[]{:S(2)}, u32[]{:S(2)}) collective-permute-start(bf16[64,128]{1,0:T(8,128)(2,1)S(1)} %slice_reduce_fusion), channel_id=1, source_target_pairs={{0,16},{4,20},{8,24},{12,28},{16,0},{20,4},{24,8},{28,12},{1,17},{... | collective-permute-start | bytes 49160 | tf_op jit(solution)/shard_map/ppermute | solution.py:275
  86.0 0.7 copy-start.2

commit v2 on v1

v2 whole, which is shorter than its diff:
```python
import functools

import jax
import jax.numpy as jnp
from jax import lax
from jax.experimental import pallas as pl
from jax.experimental.pallas import tpu as pltpu
from jax.sharding import PartitionSpec as P

HEAD_DIM = 64
HALO_X = 32
HALO_G = 16
BF = jnp.bfloat16
F32 = jnp.float32
VM = pl.BlockSpec(memory_space=pltpu.VMEM)
SM = pl.BlockSpec(memory_space=pltpu.SMEM)


def dot(a, b, dims):
    return lax.dot_general(a, b, (dims, ((), ())), preferred_element_type=F32)


def call(kernel, out_shape, args, smem=0, scratch=(), flops=1 << 20, limit=None):
    one = not isinstance(out_shape, (tuple, list))
    return pl.pallas_call(
        kernel,
        out_shape=out_shape,
        in_specs=[SM] * smem + [VM] * (len(args) - smem),
        out_specs=VM if one else tuple(VM for _ in out_shape),
        scratch_shapes=list(scratch),
        compiler_params=pltpu.CompilerParams(vmem_limit_bytes=limit),
        cost_estimate=pl.CostEstimate(flops=flops, bytes_accessed=1 << 20, transcendentals=0),
    )(*args)


def shape(dims, dtype):
    return jax.ShapeDtypeStruct(tuple(dims), dtype)


def member(members):
    return lax.rem(lax.axis_index("ctx"), members)


def total_of(lengths_ref):
    total = lengths_ref[0]
    for i in range(1, lengths_ref.shape[0]):
        total = total + lengths_ref[i]
    return total


def halo_kernel(x_ref, g_ref, up_ref, down_ref):
    rows = x_ref.shape[0]
    up_ref[0:HALO_X] = x_ref[rows - HALO_X :]
    up_ref[HALO_X:] = g_ref[rows - HALO_G :]
    down_ref[0:HALO_X] = x_ref[0:HALO_X]
    down_ref[HALO_X:] = g_ref[0:HALO_G]


def pack_kernel(q_ref, k_ref, v_ref, *rest):
    slots, buf = rest[:-1], rest[-1]
    members = len(slots)
    rows = q_ref.shape[0]
    half = rows // 2
    for m in range(members):
        cols = slice(m * HEAD_DIM, (m + 1) * HEAD_DIM)
        buf[m, 0:rows, 0:HEAD_DIM] = k_ref[:, cols]
        buf[m, 0:rows, HEAD_DIM:] = v_ref[:, cols]
        buf[m, rows:, 0:HEAD_DIM] = q_ref[0:half, cols]
        buf[m, rows:, HEAD_DIM:] = q_ref[half:, cols]
    me = member(members)
    for k in range(members):
        slots[k][...] = buf[me ^ k]


def masked_into(xs, len_ref, x_ref, low_ref, high_ref):
    rows = x_ref.shape[0]
    base = lax.axis_index("ctx") * rows - HALO_X
    total = total_of(len_ref)
    xs[0:HALO_X] = low_ref[0:HALO_X].astype(F32)
    xs[HALO_X : HALO_X + rows] = x_ref[...].astype(F32)
    xs[HALO_X + rows :] = high_ref[0:HALO_X].astype(F32)

    @pl.when(base + xs.shape[0] > total)
    def _():
        pos = base + lax.broadcasted_iota(jnp.int32, xs.shape, 0)
        xs[...] = jnp.where(pos < total, xs[...], 0.0)


def conv_kernel(len_ref, x_ref, g_ref, low_ref, high_ref, w_ref, out_ref, mine_ref, xs, gs):
    rows, width = x_ref.shape
    taps = w_ref.shape[0]
    half = taps // 2
    masked_into(xs, len_ref, x_ref, low_ref, high_ref)
    w = w_ref[...].astype(F32)
    wide = rows + 2 * HALO_G
    shift = HALO_X - HALO_G - half
    acc = jnp.zeros((wide, width), F32)
    for j in range(taps):
        acc = acc + w[j : j + 1] * xs[shift + j : shift + j + wide]
    s = jax.nn.sigmoid(acc)
    slope = s * (1.0 + acc * (1.0 - s))
    gs[0:HALO_G] = low_ref[HALO_X:].astype(F32)
    gs[HALO_G : HALO_G + rows] = g_ref[...].astype(F32)
    gs[HALO_G + rows :] = high_ref[HALO_X:].astype(F32)
    gs[...] = (gs[...] * slope).astype(BF).astype(F32)
    acc = jnp.zeros((rows, width), F32)
    for j in range(taps):
        first = HALO_G + half - j
        acc = acc + w[j : j + 1] * gs[first : first + rows]
    pos = lax.axis_index("ctx") * rows + lax.broadcasted_iota(jnp.int32, acc.shape, 0)
    acc = jnp.where(pos < total_of(len_ref), acc, 0.0)
    out_ref[...] = (g_ref[...].astype(F32) + acc).astype(BF)
    mine_ref[...] = gs[HALO_G : HALO_G + rows].astype(BF)


def taps_kernel(taps, len_ref, x_ref, low_ref, high_ref, mine_ref, tap_ref, xs):
    rows, width = x_ref.shape
    half = taps // 2
    sides = width // 128
    tap_rows = tap_ref.shape[0] // sides
    masked_into(xs, len_ref, x_ref, low_ref, high_ref)
    mine = mine_ref[...].astype(F32)
    sums = []
    for j in range(taps):
        first = HALO_X - half + j
        sums.append(jnp.sum(mine * xs[first : first + rows], axis=0, keepdims=True))
    sums.append(jnp.zeros((tap_rows - taps, width), F32))
    out = jnp.concatenate(sums, 0).astype(BF)
    for side in range(sides):
        tap_ref[side * tap_rows : (side + 1) * tap_rows] = out[:, side * 128 : (side + 1) * 128]


def spread_kernel(pieces, members, proj_ref, *rest):
    n_heads = len(rest) - members - 4
    xs, go_refs = rest[:n_heads], rest[n_heads : n_heads + members]
    piece_ref, full, go_buf, piece_buf = rest[n_heads + members :]
    rows, width = xs[0].shape
    half = rows // 2
    mine = lax.axis_index("head")
    for k in range(n_heads):
        full[mine ^ k] = xs[k][...]
    go = jnp.zeros((rows, proj_ref.shape[1]), F32)
    for b in range(n_heads):
        go = go + dot(full[b], proj_ref[b * width : (b + 1) * width], ((1,), (0,)))
    go = go.astype(BF)
    for m in range(members):
        cols = slice(m * HEAD_DIM, (m + 1) * HEAD_DIM)
        go_buf[m, :, 0:HEAD_DIM] = go[0:half, cols]
        go_buf[m, :, HEAD_DIM:] = go[half:, cols]
        for i, first in enumerate(pieces[m]):
            piece_buf[m, i * rows : (i + 1) * rows] = full[first // width][
                :, first % width : first % width + 128
            ]
    me = member(members)
    for k in range(members):
        go_refs[k][...] = go_buf[me ^ k]
        piece_ref[k] = piece_buf[me ^ k]


def widened(x, keep_high):
    x = x.astype(F32)
    turned = pltpu.roll(x, HEAD_DIM, 1)
    lane = lax.broadcasted_iota(jnp.int32, x.shape, 1)
    used = (lane >= HEAD_DIM) if keep_high else (lane < HEAD_DIM)
    first, second = (turned, x) if keep_high else (x, turned)
    return jnp.concatenate([jnp.where(used, first, 0.0), jnp.where(used, second, 0.0)], 0)


def over(count, body):
    if count <= 2:
        for g in range(count):
            body(g)
    else:
        lax.fori_loop(0, count, lambda g, c: (body(g), c)[1], 0)


def key_block(refs, g):
    return refs[0][g] if len(refs) == 1 else refs[g][...]


def queries_of(got_refs, scale):
    rows = got_refs[0].shape[0] * 2 // 3
    q = jnp.concatenate([r[rows:, :] for r in got_refs], 0)
    return (widened(q, False) * scale).astype(BF)


def forward_kernel(n_keys, members, scale, len_ref, piece_ref, tap_ref, *rest):
    got, rest = rest[:members], rest[members:]
    kv, rest = rest[:n_keys], rest[n_keys:]
    p_ref, slots, (s_ref, m_ref, l_ref, acc_ref) = rest[0], rest[1 : 1 + members], rest[1 + members :]
    groups, keys, queries = s_ref.shape
    rows = keys // members
    total = total_of(len_ref)
    ctx = lax.axis_index("ctx")
    me, group = lax.rem(ctx, members), lax.div(ctx, members)
    q = queries_of(got, scale)
    m_ref[...] = jnp.full(m_ref.shape, -1e30, F32)
    l_ref[...] = jnp.zeros(l_ref.shape, F32)
    acc_ref[...] = jnp.zeros(acc_ref.shape, F32)

    def scores(g):
        s = dot(key_block(kv, g), q, ((1,), (1,)))
        start = (lax.rem(group + g, groups) if n_keys > 1 else g) * keys
        s_ref[g] = s

        @pl.when(start + keys > total)
        def _():
            for k in range(members):
                pos = start + (me ^ k) * rows + lax.broadcasted_iota(jnp.int32, (rows, queries), 0)
                part = s_ref[g, k * rows : (k + 1) * rows]
                s_ref[g, k * rows : (k + 1) * rows] = jnp.where(pos < total, part, -1e30)

        m_ref[...] = jnp.maximum(m_ref[...], jnp.max(s_ref[g], axis=0, keepdims=True))

    over(groups, scores)

    def weights(g):
        e = jnp.exp(s_ref[g] - m_ref[...])
        s_ref[g] = e
        l_ref[...] += jnp.sum(e, axis=0, keepdims=True)

    over(groups, weights)
    l_ref[...] = 1.0 / l_ref[...]

    def values(g):
        p = (s_ref[g] * l_ref[...]).astype(BF)
        p_ref[g] = p
        acc_ref[...] += dot(key_block(kv, g), p, ((0,), (0,)))

    over(groups, values)
    attn = acc_ref[HEAD_DIM:, :].T.astype(BF)
    half = queries // 2
    count = piece_ref.shape[1]
    for k in range(members):
        slots[k][0:count] = piece_ref[k]
        slots[k][count : count + half, 0:HEAD_DIM] = attn[0:half]
        slots[k][count : count + half, HEAD_DIM:] = attn[half:]
        slots[k][count + half :] = tap_ref[...]


def backward_kernel(n_keys, members, scale, p_ref, *rest):
    got, rest = rest[:members], rest[members:]
    gos, rest = rest[:members], rest[members:]
    kv, rest = rest[:n_keys], rest[n_keys:]
    dkv, (dq_ref, s_ref, d_ref, acc_ref) = rest[:n_keys], rest[n_keys:]
    groups, keys, queries = s_ref.shape
    q = queries_of(got, scale)
    go = widened(jnp.concatenate([r[...] for r in gos], 0), True).astype(BF)
    d_ref[...] = jnp.zeros(d_ref.shape, F32)
    acc_ref[...] = jnp.zeros(acc_ref.shape, F32)

    def slopes(g):
        s = dot(key_block(kv, g), go, ((1,), (1,)))
        s_ref[g] = s
        d_ref[...] += jnp.sum(s * p_ref[g].astype(F32), axis=0, keepdims=True)

    over(groups, slopes)

    def grads(g):
        p = p_ref[g]
        ds = (p.astype(F32) * (s_ref[g] - d_ref[...])).astype(BF)
        acc_ref[...] += dot(key_block(kv, g), ds, ((0,), (0,)))
        out = (dot(ds, q, ((1,), (0,))) + dot(p, go, ((1,), (0,)))).astype(BF)
        if n_keys > 1:
            dkv[g][...] = out
        else:
            dkv[0][g] = out

    over(groups, grads)
    dq = (acc_ref[0:HEAD_DIM, :] * scale).T.astype(BF)
    half = queries // 2
    dq_ref[:, 0:HEAD_DIM] = dq[0:half]
    dq_ref[:, HEAD_DIM:] = dq[half:]


def project_kernel(tap_rows, *refs):
    members = len(refs) - 5
    slots, (out_ref, tap_ref, lhs, rhs, heads) = refs[:members], refs[members:]
    count, width = lhs.shape[1], rhs.shape[1]
    half = lhs.shape[0] // members
    rows = 2 * half
    me = member(members)
    first = count // 128 * rows
    acc = jnp.zeros((count, width), F32)
    tap = jnp.zeros((slots[0].shape[0] - first - members * half, 128), F32)
    for k in range(members):
        heads[me ^ k] = slots[k][first : first + members * half]
        tap = tap + slots[k][first + members * half :].astype(F32)
    tap_ref[...] = tap.astype(BF)
    for fold in range(2):
        for k in range(members):
            for side in range(count // 128):
                at = side * rows + fold * half
                where = pl.multiple_of((me ^ k) * half, half)
                lhs[pl.ds(where, half), side * 128 : (side + 1) * 128] = slots[k][at : at + half]
        for h in range(members):
            for i in range(members):
                j = h ^ i
                rhs[i * half : (i + 1) * half, h * HEAD_DIM : (h + 1) * HEAD_DIM] = heads[
                    h, j * half : (j + 1) * half, fold * HEAD_DIM : (fold + 1) * HEAD_DIM
                ]
        acc = acc + dot(lhs[...], rhs[...], ((0,), (0,)))
    out_ref[...] = acc


def collect_kernel(members, *refs):
    parts, dq_ref, slots = refs[: -1 - members], refs[-1 - members], refs[-members:]
    rows = slots[0].shape[0] * 2 // 3
    half = rows // 2
    if len(parts) == 1:
        total = parts[0][0].astype(F32)
        for g in range(1, parts[0].shape[0]):
            total = total + parts[0][g].astype(F32)
    else:
        total = parts[0][...].astype(F32) + parts[1][...].astype(F32)
    total = total.astype(BF)
    for k in range(members):
        slots[k][0:rows] = total[k * rows : (k + 1) * rows]
        slots[k][rows:] = dq_ref[k * half : (k + 1) * half]


def unpack_kernel(*refs):
    members = len(refs) - 4
    slots, (q_ref, k_ref, v_ref, buf) = refs[:members], refs[members:]
    rows = q_ref.shape[0]
    half = rows // 2
    me = member(members)
    for k in range(members):
        buf[me ^ k] = slots[k][...]
    for m in range(members):
        cols = slice(m * HEAD_DIM, (m + 1) * HEAD_DIM)
        k_ref[:, cols] = buf[m, 0:rows, 0:HEAD_DIM]
        v_ref[:, cols] = buf[m, 0:rows, HEAD_DIM:]
        q_ref[0:half, cols] = buf[m, rows:, 0:HEAD_DIM]
        q_ref[half:, cols] = buf[m, rows:, HEAD_DIM:]


def split_kernel(own_rows, part_ref, tap_ref, mine_ref, send_ref):
    group = lax.div(lax.axis_index("ctx"), lax.axis_size("ctx") // 2)
    width = part_ref.shape[1]
    mine_ref[...] = part_ref[pl.ds(pl.multiple_of(group * own_rows, own_rows), own_rows), :]
    theirs = part_ref[pl.ds(pl.multiple_of((1 - group) * own_rows, own_rows), own_rows), :].astype(BF)
    for side in range(width // 128):
        send_ref[side * own_rows : (side + 1) * own_rows] = theirs[:, side * 128 : (side + 1) * 128]
    send_ref[width // 128 * own_rows :] = tap_ref[...]


def finish_kernel(mine_ref, tap_ref, got_ref, out_ref, grad_ref):
    own_rows, width = mine_ref.shape
    taps = grad_ref.shape[0]
    sides = width // 128
    tap_rows = tap_ref.shape[0] // sides
    tap = tap_ref[...].astype(F32) + got_ref[sides * own_rows :].astype(F32)
    for side in range(sides):
        cols = slice(side * 128, (side + 1) * 128)
        out_ref[:, cols] = mine_ref[:, cols] + got_ref[
            side * own_rows : (side + 1) * own_rows
        ].astype(F32)
        grad_ref[:, cols] = tap[side * tap_rows : side * tap_rows + taps]


def on_device(
    query_all, key_all, value_all, cotangent, conv_input, rec_lengths, out_proj, conv_weight
):
    rows, width = query_all.shape
    half = rows // 2
    members = width // HEAD_DIM
    n_ctx, n_heads = lax.axis_size("ctx"), lax.axis_size("head")
    groups = n_ctx // members
    channels = out_proj.shape[0]
    own_rows = channels // n_ctx
    scale = HEAD_DIM**-0.5
    taps = conv_weight.shape[0]
    tap_rows = -(-taps // 16) * 16
    sides = width // 128
    keys = members * rows
    queries = members * rows
    pair = groups == 2
    across = [[g * members + m for g in range(groups)] for m in range(members)]
    other = [(i, (i + members) % n_ctx) for i in range(n_ctx)]

    def swap(slots, axis="ctx"):
        n = lax.axis_size(axis)
        return [slots[0]] + [
            lax.ppermute(slots[k], axis, [(i, i ^ k) for i in range(n)]) for k in range(1, len(slots))
        ]

    up, down = call(
        halo_kernel, (shape((HALO_X + HALO_G, width), BF),) * 2, (conv_input, cotangent)
    )
    low = lax.ppermute(up, "ctx", [(i, i + 1) for i in range(n_ctx - 1)])
    high = lax.ppermute(down, "ctx", [(i + 1, i) for i in range(n_ctx - 1)])
    slot = shape((rows + half, 128), BF)
    got = swap(
        call(
            pack_kernel,
            (slot,) * members,
            (query_all, key_all, value_all),
            scratch=[pltpu.VMEM((members, rows + half, 128), BF)],
        )
    )
    own_kv = jnp.concatenate([x[:rows] for x in got], 0)
    if pair:
        kv = (own_kv, lax.ppermute(own_kv, "ctx", other))
    else:
        kv = (lax.all_gather(own_kv, "ctx", axis_index_groups=across),)
    n_keys = len(kv)
    x_grad, grad_conv = call(
        conv_kernel,
        (shape((rows, width), BF),) * 2,
        (rec_lengths, conv_input, cotangent, low, high, conv_weight),
        smem=1,
        scratch=[
            pltpu.VMEM((rows + 2 * HALO_X, width), F32),
            pltpu.VMEM((rows + 2 * HALO_G, width), F32),
        ],
    )
    xs = swap([x_grad] * n_heads, "head")
    tap_part = call(
        functools.partial(taps_kernel, taps),
        shape((sides * tap_rows, 128), BF),
        (rec_lengths, conv_input, low, high, grad_conv),
        smem=1,
        scratch=[pltpu.VMEM((rows + 2 * HALO_X, width), F32)],
    )
    count = groups * own_rows
    if own_rows % 128 == 0:
        pieces = [
            [(g * members + m) * own_rows + b for g in range(groups) for b in range(0, own_rows, 128)]
            for m in range(members)
        ]
    else:
        pieces = [list(range(m * count, (m + 1) * count, 128)) for m in range(members)]
    spread = call(
        functools.partial(spread_kernel, pieces, members),
        (shape((half, 128), BF),) * members + (shape((members, count // 128 * rows, 128), BF),),
        (out_proj, *xs),
        scratch=[
            pltpu.VMEM((n_heads, rows, width), BF),
            pltpu.VMEM((members, half, 128), BF),
            pltpu.VMEM((members, count // 128 * rows, 128), BF),
        ],
        flops=2 * rows * channels * width,
    )
    piece = spread[members]
    gos = swap(spread[:members])
    big = 60 << 20
    flops = 2 * queries * keys * groups * 128
    fwd = call(
        functools.partial(forward_kernel, n_keys, members, scale),
        (shape((groups, keys, queries), BF),)
        + (shape((count // 128 * rows + queries // 2 + sides * tap_rows, 128), BF),) * members,
        (rec_lengths, piece, tap_part, *got, *kv),
        smem=1,
        scratch=[
            pltpu.VMEM((groups, keys, queries), F32),
            pltpu.VMEM((1, queries), F32),
            pltpu.VMEM((1, queries), F32),
            pltpu.VMEM((128, queries), F32),
        ],
        flops=2 * flops,
        limit=big,
    )
    probs = fwd[0]
    bwd = call(
        functools.partial(backward_kernel, n_keys, members, scale),
        (
            (shape((keys, 128), BF),) * 2
            if pair
            else (shape((groups, keys, 128), BF),)
        )
        + (shape((queries // 2, 128), BF),),
        (probs, *got, *gos, *kv),
        scratch=[
            pltpu.VMEM((groups, keys, queries), F32),
            pltpu.VMEM((1, queries), F32),
            pltpu.VMEM((128, queries), F32),
        ],
        flops=4 * flops,
        limit=big,
    )
    dq = bwd[-1]
    if pair:
        parts = (bwd[0], lax.ppermute(bwd[1], "ctx", other))
    else:
        parts = (lax.all_to_all(bwd[0], "ctx", 0, 0, axis_index_groups=across),)
    back = swap(call(functools.partial(collect_kernel, members), (slot,) * members, (*parts, dq)))
    q_grad, k_grad, v_grad = call(
        unpack_kernel,
        (shape((rows, width), BF),) * 3,
        tuple(back),
        scratch=[pltpu.VMEM((members, rows + half, 128), BF)],
    )
    shared = swap(fwd[1:])
    partial, tap_sum = call(
        functools.partial(project_kernel, tap_rows),
        (shape((count, width), F32), shape((sides * tap_rows, 128), BF)),
        tuple(shared),
        scratch=[
            pltpu.VMEM((members * half, count), BF),
            pltpu.VMEM((members * half, width), BF),
            pltpu.VMEM((members, queries // 2, 128), BF),
        ],
        flops=2 * count * width * queries,
    )
    grads = (shape((own_rows, width), F32), shape((taps, width), F32))
    if pair and own_rows % 16 == 0:
        mine, send = call(
            functools.partial(split_kernel, own_rows),
            (shape((own_rows, width), F32), shape((sides * (own_rows + tap_rows), 128), BF)),
            (partial, tap_sum),
        )
        out_proj_grad, conv_weight_grad = call(
            finish_kernel, grads, (mine, tap_sum, lax.ppermute(send, "ctx", other))
        )
    else:
        if own_rows % 128:
            wanted = partial.astype(BF).reshape(1, groups, own_rows, width)
            slots = jnp.zeros((members, groups, own_rows, width), BF)
            slots = lax.dynamic_update_slice(
                slots, wanted, (lax.rem(lax.axis_index("ctx"), members), 0, 0, 0)
            )
            moved = lax.all_to_all(slots.reshape(n_ctx, own_rows, width), "ctx", 0, 0)
        else:
            moved = lax.all_to_all(
                partial.astype(BF).reshape(groups, own_rows, width),
                "ctx",
                0,
                0,
                axis_index_groups=across,
            )
        out_proj_grad = jnp.sum(moved.astype(F32), 0)
        tap_all = jnp.sum(
            lax.all_gather(tap_sum, "ctx", axis_index_groups=across).astype(F32), 0
        ).reshape(sides, tap_rows, 128)
        conv_weight_grad = jnp.swapaxes(tap_all, 0, 1).reshape(tap_rows, width)[:taps]
    return (q_grad, k_grad, v_grad, x_grad, out_proj_grad, conv_weight_grad)


def solution(mesh):
    placed = (
        P("ctx", "head"),
        P("ctx", "head"),
        P("ctx", "head"),
        P("ctx", "head"),
        P("ctx", "head"),
        P(),
        P(None, "head"),
        P(None, "head"),
    )
    return jax.shard_map(
        on_device,
        mesh=mesh,
        in_specs=placed,
        out_specs=(
            P("ctx", "head"),
            P("ctx", "head"),
            P("ctx", "head"),
            P("ctx", "head"),
            P("ctx", "head"),
            P(None, "head"),
        ),
        check_vma=False,
    )
```

time: 89.4 us -> 76.7 us (0.86)
  blocking collectives: 7.39 us -> 0 us
  starting transfers between devices: 31.5 us -> 24.9 us
  Pallas kernels: 20.4 us -> 26.8 us
  other arithmetic: 5.68 us -> 0.01 us
    all_to_all x4 -> x0, starting transfers between devices: 19 us -> none  [swap(): return lax.all_to_all(x, 'ctx', 0, 0, axis_index_groups=inside)]
    ppermute x6 -> x20, starting transfers between devices: 12.6 us -> 24.9 us  [the longest x15 17.2 us: swap(): lax.ppermute(slots[k], axis, [(i, i ^ k) for i in range(n)])]
    all_gather x1 -> x0, blocking collectives: 7.39 us -> none  [on_device(): full = lax.all_gather(x_grad, 'head', axis=1, tiled=True)]
    pallas_call x8 -> x12, Pallas kernels: 20.4 us -> 26.8 us  [call(): pl.pallas_call(kernel, out_shape=out_shape, in_specs=[SM] * smem + [VM] *...]
    reduce_sum x4 -> x0, other arithmetic: 2.16 us -> none  [the longest x1 0.85 us: on_device(): jnp.sum(spread[:, half + slot_channels // 128 * rows:].astype(F32), 0)]
    another operation x2 -> x0, other arithmetic: 1.96 us -> none  [the longest x1 1.23 us: on_device(): info = jnp.stack([me * rows, total]).astype(jnp.int32)]
    unnamed x18 -> x42, local copies, waits for them, and re-layouts: 3.25 us -> 5.09 us
    convert_element_type x1 -> x0, other arithmetic: 0.96 us -> none  [on_device(): out_proj_grad = jnp.sum(exchange(partial.astype(BF)).astype(F32), 0)]
  transfers between devices with their start and end apart: 10 -> 20, of which waited for: 4 -> 12; matrix products, arithmetic and copies ran while one was open for 8% -> 1% of each run, Pallas kernels for 21% -> 31%
where the time goes in v2:
time: 76.7 us; the launch traced here: 76 us
  Pallas kernels  26.8 us (35%)
  starting transfers between devices  24.9 us (32%)
  waiting for transfers between devices  16.9 us (22%)
  local copies, waits for them, and re-layouts  6.61 us (9%)
    pallas_call x12, Pallas kernels, call(): pl.pallas_call(kernel, out_shape=out_shape, in_specs=[SM] * smem + [VM] *...  26.8 us
    ppermute x15, starting transfers between devices, swap(): lax.ppermute(slots[k], axis, [(i, i ^ k) for i in range(n)])  17.2 us
    ppermute x15, waiting for transfers between devices, swap(): lax.ppermute(slots[k], axis, [(i, i ^ k) for i in range(n)])  12 us
    unnamed x42, local copies, waits for them, and re-layouts  5.09 us
    ppermute x1, waiting for transfers between devices, on_device(): high = lax.ppermute(down, 'ctx', [(i + 1, i) for i in range(n_ctx - 1)])  4.22 us
    ppermute x1, starting transfers between devices, on_device(): kv = (own_kv, lax.ppermute(own_kv, 'ctx', other))  2.65 us
    ppermute x1, starting transfers between devices, on_device(): low = lax.ppermute(up, 'ctx', [(i, i + 1) for i in range(n_ctx - 1)])  2.4 us
  transfers between devices with their start and end apart: 20, of which 12 were waited for; matrix products, arithmetic and copies ran while one was open for 1% of the time, Pallas kernels for 31%

profile of v2, /device:TPU:0, one launch (start us, length us, event | category | flops | bytes accessed | tf_op | source)
XLA Modules:
  0.0 76.0 jit_solution(12742799713785253137)
XLA Ops:
  0.6 1.8 %shard_map.131 = (bf16[192,128]{1,0:T(8,128)(2,1)}, bf16[192,128]{1,0:T(8,128)(2,1)}, bf16[192,128]{1,0:T(8,128)(2,1)}, bf16[192,128]{1,0:T(8,128)(2,1)}) custom-call(bf16[128,256]{1,0:T(8,128)(2,1)} %q_ref.1, bf16[128,256]{1,0:T(8,128)(2,1)} %k_ref.1, bf16[128,256]{1,0:T(8,128)(2,1)} %v_ref.1), custom_call_target="tpu_custom_call" | custom-call | flops 1048576 | bytes 1048576 | tf_op jit(solution)/shard_map/pallas_call | solution.py:25
  2.4 3.0 %collective-permute-start.5 = (bf16[192,128]{1,0:T(8,128)(2,1)}, bf16[192,128]{1,0:T(8,128)(2,1)S(1)}, u32[]{:S(2)}, u32[]{:S(2)}) collective-permute-start(bf16[192,128]{1,0:T(8,128)(2,1)} %get-tuple-element.46), channel_id=1, source_target_pairs={{0,4},{4,0},{8,12},{12,8},{16,20},{20,16},{24,28},{28,24},{1,5},{5... | collective-permute-start | bytes 147464 | tf_op jit(solution)/shard_map/ppermute | solution.py:385
  5.4 1.6 %collective-permute-start.6 = (bf16[192,128]{1,0:T(8,128)(2,1)}, bf16[192,128]{1,0:T(8,128)(2,1)S(1)}, u32[]{:S(2)}, u32[]{:S(2)}) collective-permute-start(bf16[192,128]{1,0:T(8,128)(2,1)} %get-tuple-element.47), channel_id=1, source_target_pairs={{0,8},{4,12},{8,0},{12,4},{16,24},{20,28},{24,16},{28,20},{1,9},{5... | collective-permute-start | bytes 147464 | tf_op jit(solution)/shard_map/ppermute | solution.py:385
  7.7 2.3 %collective-permute-done.6.rest_2_ = bf16[192,128]{1,0:T(8,128)(2,1)S(1)} collective-permute-done((bf16[192,128]{1,0:T(8,128)(2,1)}, bf16[192,128]{1,0:T(8,128)(2,1)S(1)}, u32[]{:S(2)}, u32[]{:S(2)}) %collective-permute-start.6) | collective-permute-done | bytes 49184 | tf_op jit(solution)/shard_map/ppermute | solution.py:385
  10.1 2.1 %collective-permute-done.7.rest_3_ = bf16[192,128]{1,0:T(8,128)(2,1)S(1)} collective-permute-done((bf16[192,128]{1,0:T(8,128)(2,1)}, bf16[192,128]{1,0:T(8,128)(2,1)S(1)}, u32[]{:S(2)}, u32[]{:S(2)}) %collective-permute-start.7) | collective-permute-done | bytes 49184 | tf_op jit(solution)/shard_map/ppermute | solution.py:385
  13.0 2.7 %collective-permute-start.8 = (bf16[512,128]{1,0:T(8,128)(2,1)S(1)}, bf16[512,128]{1,0:T(8,128)(2,1)S(1)}, u32[]{:S(2)}, u32[]{:S(2)}) collective-permute-start(bf16[512,128]{1,0:T(8,128)(2,1)S(1)} %pad_maximum_fusion.rest_4_.rest_8_), channel_id=1, source_target_pairs={{0,16},{4,20},{8,24},{12,28},{16,0},{20,4},{24,8},{28,12},{1,17},{... | collective-permute-start | bytes 393224 | tf_op jit(solution)/shard_map/ppermute | solution.py:404
  15.6 1.5 %shard_map.127 = (bf16[48,256]{1,0:T(8,128)(2,1)}, bf16[48,256]{1,0:T(8,128)(2,1)}) custom-call(bf16[128,256]{1,0:T(8,128)(2,1)} %x_ref.5, bf16[128,256]{1,0:T(8,128)(2,1)} %g_ref.3), custom_call_target="tpu_custom_call" | custom-call | flops 1048576 | bytes 1048576 | tf_op jit(solution)/shard_map/pallas_call | solution.py:25
  17.1 2.4 %collective-permute-start = (bf16[48,256]{1,0:T(8,128)(2,1)}, bf16[48,256]{1,0:T(8,128)(2,1)S(1)}, u32[]{:S(2)}, u32[]{:S(2)}) collective-permute-start(bf16[48,256]{1,0:T(8,128)(2,1)} %get-tuple-element.40), channel_id=1, source_target_pairs={{0,4},{4,8},{8,12},{12,16},{16,20},{20,24},{24,28},{1,5},{5,9},{9,... | collective-permute-start | bytes 73736 | tf_op jit(solution)/shard_map/ppermute | solution.py:391
  21.2 4.2 %collective-permute-done.1.high_ref = bf16[48,256]{1,0:T(8,128)(2,1)S(1)} collective-permute-done((bf16[48,256]{1,0:T(8,128)(2,1)}, bf16[48,256]{1,0:T(8,128)(2,1)S(1)}, u32[]{:S(2)}, u32[]{:S(2)}) %collective-permute-start.1) | collective-permute-done | bytes 24608 | tf_op jit(solution)/shard_map/ppermute | solution.py:392
  26.1 3.0 %shard_map.128 = (bf16[128,256]{1,0:T(8,128)(2,1)}, bf16[128,256]{1,0:T(8,128)(2,1)}) custom-call(s32[3]{0:T(128)} %len_ref.5, bf16[128,256]{1,0:T(8,128)(2,1)} %x_ref.5, bf16[128,256]{1,0:T(8,128)(2,1)} %g_ref.3, bf16[48,256]{1,0:T(8,128)(2,1)} %copy-done.6, bf16[48,256]{1,0:T(8,128)(2,1)} %copy-done.7, bf16[31,256]{1,0:T(8,128)(2,1)} %w_ref.1), custom_call_target="tpu_custom_call" | custom-call | flops 1048576 | bytes 1048576 | tf_op jit(solution)/shard_map/pallas_call | solution.py:25
  29.1 1.6 %collective-permute-start.3 = (bf16[128,256]{1,0:T(8,128)(2,1)}, bf16[128,256]{1,0:T(8,128)(2,1)S(1)}, u32[]{:S(2)}, u32[]{:S(2)}) collective-permute-start(bf16[128,256]{1,0:T(8,128)(2,1)} %get-tuple-element.37.rest_0_), channel_id=1, source_target_pairs={{0,2},{1,3},{2,0},{3,1},{4,6},{5,7},{6,4},{7,5},{8,10},{9,11},{10,... | collective-permute-start | bytes 196616 | tf_op jit(solution)/shard_map/ppermute | solution.py:385
  30.9 1.9 %shard_map.130.tap_ref = bf16[64,128]{1,0:T(8,128)(2,1)} custom-call(s32[3]{0:T(128)} %len_ref.5, bf16[128,256]{1,0:T(8,128)(2,1)} %x_ref.5, bf16[48,256]{1,0:T(8,128)(2,1)} %copy-done.6, bf16[48,256]{1,0:T(8,128)(2,1)} %copy-done.7, bf16[128,256]{1,0:T(8,128)(2,1)} %get-tuple-element.44.mine_ref), custom_call_target="tpu_custom_call" | custom-call | flops 1048576 | bytes 1048576 | tf_op jit(solution)/shard_map/pallas_call | solution.py:25
  35.5 2.2 %shard_map.129 = (bf16[64,128]{1,0:T(8,128)(2,1)}, bf16[64,128]{1,0:T(8,128)(2,1)}, bf16[64,128]{1,0:T(8,128)(2,1)}, bf16[64,128]{1,0:T(8,128)(2,1)}, bf16[4,256,128]{2,1,0:T(8,128)(2,1)}) custom-call(bf16[1024,256]{1,0:T(8,128)(2,1)} %proj_ref.1, bf16[128,256]{1,0:T(8,128)(2,1)} %get-tuple-element.37.rest_0_, bf16[128,256]{1,0:T(8,128)(2,1)} %copy-done.9, ...), custom_call_target="tpu_custom_call" | custom-call | flops 67108864 | bytes 1048576 | tf_op jit(solution)/shard_map/pallas_call | solution.py:25
  38.3 3.2 %collective-permute-start.11 = (bf16[64,128]{1,0:T(8,128)(2,1)}, bf16[64,128]{1,0:T(8,128)(2,1)S(1)}, u32[]{:S(2)}, u32[]{:S(2)}) collective-permute-start(bf16[64,128]{1,0:T(8,128)(2,1)} %get-tuple-element.53), channel_id=1, source_target_pairs={{0,12},{4,8},{8,4},{12,0},{16,28},{20,24},{24,20},{28,16},{1,13},{... | collective-permute-start | bytes 49160 | tf_op jit(solution)/shard_map/ppermute | solution.py:385
  42.1 3.7 %shard_map.132 = (bf16[2,512,512]{2,1,0:T(8,128)(2,1)}, bf16[576,128]{1,0:T(8,128)(2,1)}, bf16[576,128]{1,0:T(8,128)(2,1)}, bf16[576,128]{1,0:T(8,128)(2,1)}, bf16[576,128]{1,0:T(8,128)(2,1)}) custom-call(s32[3]{0:T(128)} %len_ref.5, bf16[4,256,128]{2,1,0:T(8,128)(2,1)} %get-tuple-element.43.piece_ref, bf16[64,128]{1,0:T(8,128)(2,1)} %shard_map.130.tap_ref, ...), custom_call_target="tpu_custom_call" | custom-call | flops 268435456 | bytes 1048576 | tf_op jit(solution)/shard_map/pallas_call | solution.py:25
  45.9 2.0 %collective-permute-start.16 = (bf16[576,128]{1,0:T(8,128)(2,1)}, bf16[576,128]{1,0:T(8,128)(2,1)S(1)}, u32[]{:S(2)}, u32[]{:S(2)}) collective-permute-start(bf16[576,128]{1,0:T(8,128)(2,1)} %get-tuple-element.65), channel_id=1, source_target_pairs={{0,4},{4,0},{8,12},{12,8},{16,20},{20,16},{24,28},{28,24},{1,5},{5... | collective-permute-start | bytes 442376 | tf_op jit(solution)/shard_map/ppermute | solution.py:385
  50.0 3.7 %shard_map.133 = (bf16[512,128]{1,0:T(8,128)(2,1)}, bf16[512,128]{1,0:T(8,128)(2,1)}, bf16[256,128]{1,0:T(8,128)(2,1)}) custom-call(bf16[2,512,512]{2,1,0:T(8,128)(2,1)} %get-tuple-element.49.p_ref, bf16[192,128]{1,0:T(8,128)(2,1)} %get-tuple-element.45.rest_0_, bf16[192,128]{1,0:T(8,128)(2,1)} %copy-done.5, bf16[192,128]{1,0:T(8,128)(2,1)} %copy-done.15, ...), custom_call_target="tpu_custom_call" | custom-call | flops 536870912 | bytes 1048576 | tf_op jit(solution)/shard_map/pallas_call | solution.py:25
  56.5 2.4 %shard_map.136 = (f32[256,256]{1,0:T(8,128)}, bf16[64,128]{1,0:T(8,128)(2,1)}) custom-call(bf16[576,128]{1,0:T(8,128)(2,1)} %get-tuple-element.64.refs_0_, bf16[576,128]{1,0:T(8,128)(2,1)} %copy-done, bf16[576,128]{1,0:T(8,128)(2,1)} %copy-done.1, bf16[576,128]{1,0:T(8,128)(2,1)} %copy-done.2), custom_call_target="tpu_custom_call" | custom-call | flops 67108864 | bytes 1048576 | tf_op jit(solution)/shard_map/pallas_call | solution.py:25
  58.9 1.6 %shard_map.137 = (f32[128,256]{1,0:T(8,128)}, bf16[320,128]{1,0:T(8,128)(2,1)}) custom-call(f32[256,256]{1,0:T(8,128)} %get-tuple-element.68.part_ref, bf16[64,128]{1,0:T(8,128)(2,1)} %get-tuple-element.69.tap_ref), custom_call_target="tpu_custom_call" | custom-call | flops 1048576 | bytes 1048576 | tf_op jit(solution)/shard_map/pallas_call | solution.py:25
  62.4 1.6 %shard_map.134 = (bf16[192,128]{1,0:T(8,128)(2,1)}, bf16[192,128]{1,0:T(8,128)(2,1)}, bf16[192,128]{1,0:T(8,128)(2,1)}, bf16[192,128]{1,0:T(8,128)(2,1)}) custom-call(bf16[512,128]{1,0:T(8,128)(2,1)} %get-tuple-element.54.refs_0_, bf16[512,128]{1,0:T(8,128)(2,1)} %copy-done.4, bf16[256,128]{1,0:T(8,128)(2,1)} %get-tuple-element.56.refs_2_), custom_call_target="tpu_custom_call" | custom-call | flops 1048576 | bytes 1048576 | tf_op jit(solution)/shard_map/pallas_call | solution.py:25
  64.1 1.6 %collective-permute-start.13 = (bf16[192,128]{1,0:T(8,128)(2,1)}, bf16[192,128]{1,0:T(8,128)(2,1)S(1)}, u32[]{:S(2)}, u32[]{:S(2)}) collective-permute-start(bf16[192,128]{1,0:T(8,128)(2,1)} %get-tuple-element.58), channel_id=1, source_target_pairs={{0,4},{4,0},{8,12},{12,8},{16,20},{20,16},{24,28},{28,24},{1,5},{5... | collective-permute-start | bytes 147464 | tf_op jit(solution)/shard_map/ppermute | solution.py:385
  66.2 1.4 %collective-permute-start.15 = (bf16[192,128]{1,0:T(8,128)(2,1)}, bf16[192,128]{1,0:T(8,128)(2,1)S(1)}, u32[]{:S(2)}, u32[]{:S(2)}) collective-permute-start(bf16[192,128]{1,0:T(8,128)(2,1)} %get-tuple-element.60), channel_id=1, source_target_pairs={{0,12},{4,8},{8,4},{12,0},{16,28},{20,24},{24,20},{28,16},{1,13},{... | collective-permute-start | bytes 147464 | tf_op jit(solution)/shard_map/ppermute | solution.py:385
  72.0 1.7 %shard_map.135 = (bf16[128,256]{1,0:T(8,128)(2,1)}, bf16[128,256]{1,0:T(8,128)(2,1)}, bf16[128,256]{1,0:T(8,128)(2,1)}) custom-call(bf16[192,128]{1,0:T(8,128)(2,1)} %get-tuple-element.57.refs_0_, bf16[192,128]{1,0:T(8,128)(2,1)} %copy-done.12, bf16[192,128]{1,0:T(8,128)(2,1)} %copy-done.13, bf16[192,128]{1,0:T(8,128)(2,1)} %copy-done.14), custom_call_target="tpu_custom_call" | custom-call | flops 1048576 | bytes 1048576 | tf_op jit(solution)/shard_map/pallas_call | solution.py:25
  74.3 1.6 %shard_map.138 = (f32[128,256]{1,0:T(8,128)}, f32[31,256]{1,0:T(8,128)}) custom-call(f32[128,256]{1,0:T(8,128)} %get-tuple-element.70.mine_ref, bf16[64,128]{1,0:T(8,128)(2,1)} %get-tuple-element.69.tap_ref, bf16[320,128]{1,0:T(8,128)(2,1)} %copy-done.8), custom_call_target="tpu_custom_call" | custom-call | flops 1048576 | bytes 1048576 | tf_op jit(solution)/shard_map/pallas_call | solution.py:25
  (76 shorter events, 20.4 us)
Async XLA Ops:
  2.4 5.3 %collective-permute-start.5 = (bf16[192,128]{1,0:T(8,128)(2,1)}, bf16[192,128]{1,0:T(8,128)(2,1)S(1)}, u32[]{:S(2)}, u32[]{:S(2)}) collective-permute-start(bf16[192,128]{1,0:T(8,128)(2,1)} %get-tuple-element.46), channel_id=1, source_target_pairs={{0,4},{4,0},{8,12},{12,8},{16,20},{20,16},{24,28},{28,24},{1,5},{5... | collective-permute-start | bytes 147464 | tf_op jit(solution)/shard_map/ppermute | solution.py:385
  5.4 4.7 %collective-permute-start.6 = (bf16[192,128]{1,0:T(8,128)(2,1)}, bf16[192,128]{1,0:T(8,128)(2,1)S(1)}, u32[]{:S(2)}, u32[]{:S(2)}) collective-permute-start(bf16[192,128]{1,0:T(8,128)(2,1)} %get-tuple-element.47), channel_id=1, source_target_pairs={{0,8},{4,12},{8,0},{12,4},{16,24},{20,28},{24,16},{28,20},{1,9},{5... | collective-permute-start | bytes 147464 | tf_op jit(solution)/shard_map/ppermute | solution.py:385
  7.0 5.2 %collective-permute-start.7 = (bf16[192,128]{1,0:T(8,128)(2,1)}, bf16[192,128]{1,0:T(8,128)(2,1)S(1)}, u32[]{:S(2)}, u32[]{:S(2)}) collective-permute-start(bf16[192,128]{1,0:T(8,128)(2,1)} %get-tuple-element.48), channel_id=1, source_target_pairs={{0,12},{4,8},{8,4},{12,0},{16,28},{20,24},{24,20},{28,16},{1,13},{... | collective-permute-start | bytes 147464 | tf_op jit(solution)/shard_map/ppermute | solution.py:385
  7.7 2.3 %copy-start.5 = (bf16[192,128]{1,0:T(8,128)(2,1)}, bf16[192,128]{1,0:T(8,128)(2,1)S(1)}, u32[]{:S(2)}) copy-start(bf16[192,128]{1,0:T(8,128)(2,1)S(1)} %collective-permute-done.5.rest_1_) | copy-start | bytes 147460
  13.0 16.1 %copy-start.3 = (bf16[512,128]{1,0:T(8,128)(2,1)}, bf16[512,128]{1,0:T(8,128)(2,1)S(1)}, u32[]{:S(2)}) copy-start(bf16[512,128]{1,0:T(8,128)(2,1)S(1)} %pad_maximum_fusion.rest_4_.rest_8_) | copy-start | bytes 393220
  13.0 28.5 %collective-permute-start.8 = (bf16[512,128]{1,0:T(8,128)(2,1)S(1)}, bf16[512,128]{1,0:T(8,128)(2,1)S(1)}, u32[]{:S(2)}, u32[]{:S(2)}) collective-permute-start(bf16[512,128]{1,0:T(8,128)(2,1)S(1)} %pad_maximum_fusion.rest_4_.rest_8_), channel_id=1, source_target_pairs={{0,16},{4,20},{8,24},{12,28},{16,0},{20,4},{24,8},{28,12},{1,17},{... | collective-permute-start | bytes 393224 | tf_op jit(solution)/shard_map/ppermute | solution.py:404
  17.1 4.1 %collective-permute-start = (bf16[48,256]{1,0:T(8,128)(2,1)}, bf16[48,256]{1,0:T(8,128)(2,1)S(1)}, u32[]{:S(2)}, u32[]{:S(2)}) collective-permute-start(bf16[48,256]{1,0:T(8,128)(2,1)} %get-tuple-element.40), channel_id=1, source_target_pairs={{0,4},{4,8},{8,12},{12,16},{16,20},{20,24},{24,28},{1,5},{5,9},{9,... | collective-permute-start | bytes 73736 | tf_op jit(solution)/shard_map/ppermute | solution.py:391
  19.5 5.9 %collective-permute-start.1 = (bf16[48,256]{1,0:T(8,128)(2,1)}, bf16[48,256]{1,0:T(8,128)(2,1)S(1)}, u32[]{:S(2)}, u32[]{:S(2)}) collective-permute-start(bf16[48,256]{1,0:T(8,128)(2,1)} %get-tuple-element.41), channel_id=1, source_target_pairs={{4,0},{8,4},{12,8},{16,12},{20,16},{24,20},{28,24},{5,1},{9,5},{13... | collective-permute-start | bytes 73736 | tf_op jit(solution)/shard_map/ppermute | solution.py:392
  21.2 4.2 %copy-start.6 = (bf16[48,256]{1,0:T(8,128)(2,1)}, bf16[48,256]{1,0:T(8,128)(2,1)S(1)}, u32[]{:S(2)}) copy-start(bf16[48,256]{1,0:T(8,128)(2,1)S(1)} %collective-permute-done.low_ref) | copy-start | bytes 73732
  29.1 3.8 %collective-permute-start.2 = (bf16[128,256]{1,0:T(8,128)(2,1)}, bf16[128,256]{1,0:T(8,128)(2,1)S(1)}, u32[]{:S(2)}, u32[]{:S(2)}) collective-permute-start(bf16[128,256]{1,0:T(8,128)(2,1)} %get-tuple-element.37.rest_0_), channel_id=1, source_target_pairs={{0,1},{1,0},{2,3},{3,2},{4,5},{5,4},{6,7},{7,6},{8,9},{9,8},{10,11... | collective-permute-start | bytes 196616 | tf_op jit(solution)/shard_map/ppermute | solution.py:385
  29.1 4.7 %collective-permute-start.3 = (bf16[128,256]{1,0:T(8,128)(2,1)}, bf16[128,256]{1,0:T(8,128)(2,1)S(1)}, u32[]{:S(2)}, u32[]{:S(2)}) collective-permute-start(bf16[128,256]{1,0:T(8,128)(2,1)} %get-tuple-element.37.rest_0_), channel_id=1, source_target_pairs={{0,2},{1,3},{2,0},{3,1},{4,6},{5,7},{6,4},{7,5},{8,10},{9,11},{10,... | collective-permute-start | bytes 196616 | tf_op jit(solution)/shard_map/ppermute | solution.py:385
  30.6 4.3 %collective-permute-start.4 = (bf16[128,256]{1,0:T(8,128)(2,1)}, bf16[128,256]{1,0:T(8,128)(2,1)S(1)}, u32[]{:S(2)}, u32[]{:S(2)}) collective-permute-start(bf16[128,256]{1,0:T(8,128)(2,1)} %get-tuple-element.37.rest_0_), channel_id=1, source_target_pairs={{0,3},{1,2},{2,1},{3,0},{4,7},{5,6},{6,5},{7,4},{8,11},{9,10},{10,... | collective-permute-start | bytes 196616 | tf_op jit(solution)/shard_map/ppermute | solution.py:385
  37.7 10.6 %collective-permute-start.10 = (bf16[64,128]{1,0:T(8,128)(2,1)}, bf16[64,128]{1,0:T(8,128)(2,1)S(1)}, u32[]{:S(2)}, u32[]{:S(2)}) collective-permute-start(bf16[64,128]{1,0:T(8,128)(2,1)} %get-tuple-element.52), channel_id=1, source_target_pairs={{0,8},{4,12},{8,0},{12,4},{16,24},{20,28},{24,16},{28,20},{1,9},{5... | collective-permute-start | bytes 49160 | tf_op jit(solution)/shard_map/ppermute | solution.py:385
  38.3 11.1 %collective-permute-start.11 = (bf16[64,128]{1,0:T(8,128)(2,1)}, bf16[64,128]{1,0:T(8,128)(2,1)S(1)}, u32[]{:S(2)}, u32[]{:S(2)}) collective-permute-start(bf16[64,128]{1,0:T(8,128)(2,1)} %get-tuple-element.53), channel_id=1, source_target_pairs={{0,12},{4,8},{8,4},{12,0},{16,28},{20,24},{24,20},{28,16},{1,13},{... | collective-permute-start | bytes 49160 | tf_op jit(solution)/shard_map/ppermute | solution.py:385
  41.5 8.0 %collective-permute-start.9 = (bf16[64,128]{1,0:T(8,128)(2,1)}, bf16[64,128]{1,0:T(8,128)(2,1)S(1)}, u32[]{:S(2)}, u32[]{:S(2)}) collective-permute-start(bf16[64,128]{1,0:T(8,128)(2,1)} %get-tuple-element.51), channel_id=1, source_target_pairs={{0,4},{4,0},{8,12},{12,8},{16,20},{20,16},{24,28},{28,24},{1,5},{5... | collective-permute-start | bytes 49160 | tf_op jit(solution)/shard_map/ppermute | solution.py:385
  45.9 8.2 %collective-permute-start.16 = (bf16[576,128]{1,0:T(8,128)(2,1)}, bf16[576,128]{1,0:T(8,128)(2,1)S(1)}, u32[]{:S(2)}, u32[]{:S(2)}) collective-permute-start(bf16[576,128]{1,0:T(8,128)(2,1)} %get-tuple-element.65), channel_id=1, source_target_pairs={{0,4},{4,0},{8,12},{12,8},{16,20},{20,16},{24,28},{28,24},{1,5},{5... | collective-permute-start | bytes 442376 | tf_op jit(solution)/shard_map/ppermute | solution.py:385
  47.9 6.6 %collective-permute-start.17 = (bf16[576,128]{1,0:T(8,128)(2,1)}, bf16[576,128]{1,0:T(8,128)(2,1)S(1)}, u32[]{:S(2)}, u32[]{:S(2)}) collective-permute-start(bf16[576,128]{1,0:T(8,128)(2,1)} %get-tuple-element.66), channel_id=1, source_target_pairs={{0,8},{4,12},{8,0},{12,4},{16,24},{20,28},{24,16},{28,20},{1,9},{5... | collective-permute-start | bytes 442376 | tf_op jit(solution)/shard_map/ppermute | solution.py:385
  48.3 7.5 %collective-permute-start.18 = (bf16[576,128]{1,0:T(8,128)(2,1)}, bf16[576,128]{1,0:T(8,128)(2,1)S(1)}, u32[]{:S(2)}, u32[]{:S(2)}) collective-permute-start(bf16[576,128]{1,0:T(8,128)(2,1)} %get-tuple-element.67), channel_id=1, source_target_pairs={{0,12},{4,8},{8,4},{12,0},{16,28},{20,24},{24,20},{28,16},{1,13},{... | collective-permute-start | bytes 442376 | tf_op jit(solution)/shard_map/ppermute | solution.py:385
  53.7 8.0 %collective-permute-start.12 = (bf16[512,128]{1,0:T(8,128)(2,1)}, bf16[512,128]{1,0:T(8,128)(2,1)S(1)}, u32[]{:S(2)}, u32[]{:S(2)}) collective-permute-start(bf16[512,128]{1,0:T(8,128)(2,1)} %get-tuple-element.55), channel_id=1, source_target_pairs={{0,16},{4,20},{8,24},{12,28},{16,0},{20,4},{24,8},{28,12},{1,17},{... | collective-permute-start | bytes 393224 | tf_op jit(solution)/shard_map/ppermute | solution.py:484
  60.5 13.2 %collective-permute-start.19 = (bf16[320,128]{1,0:T(8,128)(2,1)}, bf16[320,128]{1,0:T(8,128)(2,1)S(1)}, u32[]{:S(2)}, u32[]{:S(2)}) collective-permute-start(bf16[320,128]{1,0:T(8,128)(2,1)} %get-tuple-element.71), channel_id=1, source_target_pairs={{0,16},{4,20},{8,24},{12,28},{16,0},{20,4},{24,8},{28,12},{1,17},{... | collective-permute-start | bytes 245768 | tf_op jit(solution)/shard_map/ppermute | solution.py:514
  64.1 4.8 %collective-permute-start.13 = (bf16[192,128]{1,0:T(8,128)(2,1)}, bf16[192,128]{1,0:T(8,128)(2,1)S(1)}, u32[]{:S(2)}, u32[]{:S(2)}) collective-permute-start(bf16[192,128]{1,0:T(8,128)(2,1)} %get-tuple-element.58), channel_id=1, source_target_pairs={{0,4},{4,0},{8,12},{12,8},{16,20},{20,16},{24,28},{28,24},{1,5},{5... | collective-permute-start | bytes 147464 | tf_op jit(solution)/shard_map/ppermute | solution.py:385
  65.7 4.3 %collective-permute-start.14 = (bf16[192,128]{1,0:T(8,128)(2,1)}, bf16[192,128]{1,0:T(8,128)(2,1)S(1)}, u32[]{:S(2)}, u32[]{:S(2)}) collective-permute-start(bf16[192,128]{1,0:T(8,128)(2,1)} %get-tuple-element.59), channel_id=1, source_target_pairs={{0,8},{4,12},{8,0},{12,4},{16,24},{20,28},{24,16},{28,20},{1,9},{5... | collective-permute-start | bytes 147464 | tf_op jit(solution)/shard_map/ppermute | solution.py:385
  66.2 5.2 %collective-permute-start.15 = (bf16[192,128]{1,0:T(8,128)(2,1)}, bf16[192,128]{1,0:T(8,128)(2,1)S(1)}, u32[]{:S(2)}, u32[]{:S(2)}) collective-permute-start(bf16[192,128]{1,0:T(8,128)(2,1)} %get-tuple-element.60), channel_id=1, source_target_pairs={{0,12},{4,8},{8,4},{12,0},{16,28},{20,24},{24,20},{28,16},{1,13},{... | collective-permute-start | bytes 147464 | tf_op jit(solution)/shard_map/ppermute | solution.py:385
  68.9 2.5 %copy-start.12 = (bf16[192,128]{1,0:T(8,128)(2,1)}, bf16[192,128]{1,0:T(8,128)(2,1)S(1)}, u32[]{:S(2)}) copy-start(bf16[192,128]{1,0:T(8,128)(2,1)S(1)} %collective-permute-done.13.refs_1_) | copy-start | bytes 147460
  (18 other events, 18.1 us)

commit v3 on v2

--- a/solution.py
+++ b/solution.py
@@ -6,6 +6,7 @@
 from jax.experimental import pallas as pl
 from jax.experimental.pallas import tpu as pltpu
 from jax.sharding import PartitionSpec as P
+
 
 HEAD_DIM = 64
 HALO_X = 32
@@ -28,7 +29,7 @@
         in_specs=[SM] * smem + [VM] * (len(args) - smem),
         out_specs=VM if one else tuple(VM for _ in out_shape),
         scratch_shapes=list(scratch),
-        compiler_params=pltpu.CompilerParams(vmem_limit_bytes=limit),
+        compiler_params=pltpu.CompilerParams(vmem_limit_bytes=limit or (4 << 20)),
         cost_estimate=pl.CostEstimate(flops=flops, bytes_accessed=1 << 20, transcendentals=0),
     )(*args)
 
@@ -56,7 +57,7 @@
     down_ref[HALO_X:] = g_ref[0:HALO_G]
 
 
-def pack_kernel(q_ref, k_ref, v_ref, *rest):
+def pack_kernel(q_ref, k_ref, v_ref, after_ref, *rest):
     slots, buf = rest[:-1], rest[-1]
     members = len(slots)
     rows = q_ref.shape[0]
@@ -72,6 +73,13 @@
         slots[k][...] = buf[me ^ k]
 
 
+def join_kernel(after_ref, *refs):
+    out_ref = refs[-1]
+    rows = out_ref.shape[0] // (len(refs) - 1)
+    for k, ref in enumerate(refs[:-1]):
+        out_ref[k * rows : (k + 1) * rows] = ref[0:rows]
+
+
 def masked_into(xs, len_ref, x_ref, low_ref, high_ref):
     rows = x_ref.shape[0]
     base = lax.axis_index("ctx") * rows - HALO_X
@@ -86,7 +94,9 @@
         xs[...] = jnp.where(pos < total, xs[...], 0.0)
 
 
-def conv_kernel(len_ref, x_ref, g_ref, low_ref, high_ref, w_ref, out_ref, mine_ref, xs, gs):
+def conv_kernel(
+    len_ref, x_ref, g_ref, low_ref, high_ref, w_ref, out_ref, send_ref, mine_ref, xs, gs
+):
     rows, width = x_ref.shape
     taps = w_ref.shape[0]
     half = taps // 2
@@ -109,7 +119,9 @@
         acc = acc + w[j : j + 1] * gs[first : first + rows]
     pos = lax.axis_index("ctx") * rows + lax.broadcasted_iota(jnp.int32, acc.shape, 0)
     acc = jnp.where(pos < total_of(len_ref), acc, 0.0)
-    out_ref[...] = (g_ref[...].astype(F32) + acc).astype(BF)
+    out = (g_ref[...].astype(F32) + acc).astype(BF)
+    out_ref[...] = out
+    send_ref[...] = out
     mine_ref[...] = gs[HALO_G : HALO_G + rows].astype(BF)
 
 
@@ -243,7 +255,7 @@
     gos, rest = rest[:members], rest[members:]
     kv, rest = rest[:n_keys], rest[n_keys:]
     dkv, (dq_ref, s_ref, d_ref, acc_ref) = rest[:n_keys], rest[n_keys:]
-    groups, keys, queries = s_ref.shape
+    groups, _, queries = s_ref.shape
     q = queries_of(got, scale)
     go = widened(jnp.concatenate([r[...] for r in gos], 0), True).astype(BF)
     d_ref[...] = jnp.zeros(d_ref.shape, F32)
@@ -273,9 +285,9 @@
     dq_ref[:, HEAD_DIM:] = dq[half:]
 
 
-def project_kernel(tap_rows, *refs):
-    members = len(refs) - 5
-    slots, (out_ref, tap_ref, lhs, rhs, heads) = refs[:members], refs[members:]
+def project_kernel(own_rows, members, *refs):
+    slots, outs, (lhs, rhs, heads) = refs[:members], refs[members:-3], refs[-3:]
+    out_ref, tap_ref = outs[:2]
     count, width = lhs.shape[1], rhs.shape[1]
     half = lhs.shape[0] // members
     rows = 2 * half
@@ -300,7 +312,17 @@
                     h, j * half : (j + 1) * half, fold * HEAD_DIM : (fold + 1) * HEAD_DIM
                 ]
         acc = acc + dot(lhs[...], rhs[...], ((0,), (0,)))
-    out_ref[...] = acc
+    if len(outs) == 2:
+        out_ref[...] = acc
+        return
+    send_ref = outs[2]
+    first = lax.axis_index("ctx") < lax.axis_size("ctx") // 2
+    low, high = acc[:own_rows], acc[own_rows:]
+    out_ref[...] = jnp.where(first, low, high)
+    theirs = jnp.where(first, high, low).astype(BF)
+    for side in range(width // 128):
+        send_ref[side * own_rows : (side + 1) * own_rows] = theirs[:, side * 128 : (side + 1) * 128]
+    send_ref[width // 128 * own_rows :] = tap.astype(BF)
 
 
 def collect_kernel(members, *refs):
@@ -333,16 +355,6 @@
         v_ref[:, cols] = buf[m, 0:rows, HEAD_DIM:]
         q_ref[0:half, cols] = buf[m, rows:, 0:HEAD_DIM]
         q_ref[half:, cols] = buf[m, rows:, HEAD_DIM:]
-
-
-def split_kernel(own_rows, part_ref, tap_ref, mine_ref, send_ref):
-    group = lax.div(lax.axis_index("ctx"), lax.axis_size("ctx") // 2)
-    width = part_ref.shape[1]
-    mine_ref[...] = part_ref[pl.ds(pl.multiple_of(group * own_rows, own_rows), own_rows), :]
-    theirs = part_ref[pl.ds(pl.multiple_of((1 - group) * own_rows, own_rows), own_rows), :].astype(BF)
-    for side in range(width // 128):
-        send_ref[side * own_rows : (side + 1) * own_rows] = theirs[:, side * 128 : (side + 1) * 128]
-    send_ref[width // 128 * own_rows :] = tap_ref[...]
 
 
 def finish_kernel(mine_ref, tap_ref, got_ref, out_ref, grad_ref):
@@ -382,32 +394,29 @@
     def swap(slots, axis="ctx"):
         n = lax.axis_size(axis)
         return [slots[0]] + [
-            lax.ppermute(slots[k], axis, [(i, i ^ k) for i in range(n)]) for k in range(1, len(slots))
+            move(slots[k], [(i, i ^ k) for i in range(n)], axis) for k in range(1, len(slots))
         ]
+
+    def move(x, pairs, axis="ctx"):
+        return lax.ppermute(x, axis, pairs)
 
     up, down = call(
         halo_kernel, (shape((HALO_X + HALO_G, width), BF),) * 2, (conv_input, cotangent)
     )
-    low = lax.ppermute(up, "ctx", [(i, i + 1) for i in range(n_ctx - 1)])
-    high = lax.ppermute(down, "ctx", [(i + 1, i) for i in range(n_ctx - 1)])
+    low = move(up, [(i, i + 1) for i in range(n_ctx - 1)])
+    high = move(down, [(i + 1, i) for i in range(n_ctx - 1)])
     slot = shape((rows + half, 128), BF)
     got = swap(
         call(
             pack_kernel,
             (slot,) * members,
-            (query_all, key_all, value_all),
+            (query_all, key_all, value_all, up),
             scratch=[pltpu.VMEM((members, rows + half, 128), BF)],
-        )
-    )
-    own_kv = jnp.concatenate([x[:rows] for x in got], 0)
-    if pair:
-        kv = (own_kv, lax.ppermute(own_kv, "ctx", other))
-    else:
-        kv = (lax.all_gather(own_kv, "ctx", axis_index_groups=across),)
-    n_keys = len(kv)
-    x_grad, grad_conv = call(
+        ),
+    )
+    x_grad, x_send, grad_conv = call(
         conv_kernel,
-        (shape((rows, width), BF),) * 2,
+        (shape((rows, width), BF),) * 3,
         (rec_lengths, conv_input, cotangent, low, high, conv_weight),
         smem=1,
         scratch=[
@@ -415,7 +424,13 @@
             pltpu.VMEM((rows + 2 * HALO_G, width), F32),
         ],
     )
-    xs = swap([x_grad] * n_heads, "head")
+    xs = swap([x_send] * n_heads, "head")
+    own_kv = call(join_kernel, shape((keys, 128), BF), (grad_conv, *got))
+    if pair:
+        kv = (own_kv, move(own_kv, other))
+    else:
+        kv = (lax.all_gather(own_kv, "ctx", axis_index_groups=across),)
+    n_keys = len(kv)
     tap_part = call(
         functools.partial(taps_kernel, taps),
         shape((sides * tap_rows, 128), BF),
@@ -444,7 +459,7 @@
     )
     piece = spread[members]
     gos = swap(spread[:members])
-    big = 60 << 20
+    big = (12 << 20) if groups <= 2 else (60 << 20)
     flops = 2 * queries * keys * groups * 128
     fwd = call(
         functools.partial(forward_kernel, n_keys, members, scale),
@@ -481,7 +496,7 @@
     )
     dq = bwd[-1]
     if pair:
-        parts = (bwd[0], lax.ppermute(bwd[1], "ctx", other))
+        parts = (bwd[0], move(bwd[1], other))
     else:
         parts = (lax.all_to_all(bwd[0], "ctx", 0, 0, axis_index_groups=across),)
     back = swap(call(functools.partial(collect_kernel, members), (slot,) * members, (*parts, dq)))
@@ -492,9 +507,16 @@
         scratch=[pltpu.VMEM((members, rows + half, 128), BF)],
     )
     shared = swap(fwd[1:])
-    partial, tap_sum = call(
-        functools.partial(project_kernel, tap_rows),
-        (shape((count, width), F32), shape((sides * tap_rows, 128), BF)),
+    merged = pair and own_rows % 16 == 0
+    tap_shape = shape((sides * tap_rows, 128), BF)
+    outs = (
+        (shape((own_rows, width), F32), tap_shape, shape((sides * (own_rows + tap_rows), 128), BF))
+        if merged
+        else (shape((count, width), F32), tap_shape)
+    )
+    partial, tap_sum, *send = call(
+        functools.partial(project_kernel, own_rows, members),
+        outs,
         tuple(shared),
         scratch=[
             pltpu.VMEM((members * half, count), BF),
@@ -504,14 +526,9 @@
         flops=2 * count * width * queries,
     )
     grads = (shape((own_rows, width), F32), shape((taps, width), F32))
-    if pair and own_rows % 16 == 0:
-        mine, send = call(
-            functools.partial(split_kernel, own_rows),
-            (shape((own_rows, width), F32), shape((sides * (own_rows + tap_rows), 128), BF)),
-            (partial, tap_sum),
-        )
+    if merged:
         out_proj_grad, conv_weight_grad = call(
-            finish_kernel, grads, (mine, tap_sum, lax.ppermute(send, "ctx", other))
+            finish_kernel, grads, (partial, tap_sum, move(send[0], other))
         )
     else:
         if own_rows % 128:
@@ -548,6 +565,7 @@
         P(None, "head"),
         P(None, "head"),
     )
+
     return jax.shard_map(
         on_device,
         mesh=mesh,

time: 76.7 us -> 61.3 us (0.80)
  Pallas kernels: 26.8 us -> 10.1 us
  starting transfers between devices: 24.9 us -> 27.3 us
  local copies, waits for them, and re-layouts: 6.61 us -> 4.91 us
  waiting for transfers between devices: 16.9 us -> 17.8 us
    pallas_call x12, Pallas kernels: 26.8 us -> 10.1 us  [call(): pl.pallas_call(kernel, out_shape=out_shape, in_specs=[SM] * smem + [VM] *...]
    ppermute x20, starting transfers between devices: 24.9 us -> 27.3 us  [move(): return lax.ppermute(x, axis, pairs)]
    slice x5 -> x0, local copies, waits for them, and re-layouts: 1.53 us -> none  [on_device(): own_kv = jnp.concatenate([x[:rows] for x in got], 0)]
    ppermute x20, waiting for transfers between devices: 16.9 us -> 17.8 us  [move(): return lax.ppermute(x, axis, pairs)]
    unnamed x42 -> x20, local copies, waits for them, and re-layouts: 5.09 us -> 4.91 us
  transfers between devices with their start and end apart: 20 -> 20, of which waited for: 12 -> 11; matrix products, arithmetic and copies ran while one was open for 1% -> 0% of each run, Pallas kernels for 31% -> 15%
where the time goes in v3:
time: 61.3 us; the launch traced here: 60.8 us
  starting transfers between devices  27.3 us (45%)
  waiting for transfers between devices  17.8 us (29%)
  Pallas kernels  10.1 us (16%)
  local copies, waits for them, and re-layouts  4.91 us (8%)
  between operations  0.76 us (1%)
    ppermute x20, starting transfers between devices, move(): return lax.ppermute(x, axis, pairs)  27.3 us
    ppermute x20, waiting for transfers between devices, move(): return lax.ppermute(x, axis, pairs)  17.8 us
    pallas_call x12, Pallas kernels, call(): pl.pallas_call(kernel, out_shape=out_shape, in_specs=[SM] * smem + [VM] *...  10.1 us
    unnamed x20, local copies, waits for them, and re-layouts  4.91 us
  transfers between devices with their start and end apart: 20, of which 11 were waited for; matrix products, arithmetic and copies ran while one was open for 0% of the time, Pallas kernels for 15%

profile of v3, /device:TPU:0, one launch (start us, length us, event | category | flops | bytes accessed | tf_op | source)
XLA Modules:
  0.0 60.8 jit_solution(10248102929318408564)
XLA Ops:
  5.0 3.1 %collective-permute-start.5 = (bf16[192,128]{1,0:T(8,128)(2,1)S(1)}, bf16[192,128]{1,0:T(8,128)(2,1)S(1)}, u32[]{:S(2)}, u32[]{:S(2)}) collective-permute-start(bf16[192,128]{1,0:T(8,128)(2,1)S(1)} %get-tuple-element.46), channel_id=1, source_target_pairs={{0,4},{4,0},{8,12},{12,8},{16,20},{20,16},{24,28},{28,24},{1,5},{5... | collective-permute-start | bytes 147464 | tf_op jit(solution)/shard_map/ppermute | solution.py:401
  8.1 1.6 %collective-permute-start.6 = (bf16[192,128]{1,0:T(8,128)(2,1)S(1)}, bf16[192,128]{1,0:T(8,128)(2,1)S(1)}, u32[]{:S(2)}, u32[]{:S(2)}) collective-permute-start(bf16[192,128]{1,0:T(8,128)(2,1)S(1)} %get-tuple-element.47), channel_id=1, source_target_pairs={{0,8},{4,12},{8,0},{12,4},{16,24},{20,28},{24,16},{28,20},{1,9},{5... | collective-permute-start | bytes 147464 | tf_op jit(solution)/shard_map/ppermute | solution.py:401
  9.7 3.8 %collective-permute-start = (bf16[48,256]{1,0:T(8,128)(2,1)S(1)}, bf16[48,256]{1,0:T(8,128)(2,1)S(1)}, u32[]{:S(2)}, u32[]{:S(2)}) collective-permute-start(bf16[48,256]{1,0:T(8,128)(2,1)S(1)} %get-tuple-element.40.after_ref), channel_id=1, source_target_pairs={{0,4},{4,8},{8,12},{12,16},{16,20},{20,24},{24,28},{1,5},{5,9},{9,... | collective-permute-start | bytes 73736 | tf_op jit(solution)/shard_map/ppermute | solution.py:401
  13.5 1.3 %collective-permute-start.1 = (bf16[48,256]{1,0:T(8,128)(2,1)S(1)}, bf16[48,256]{1,0:T(8,128)(2,1)S(1)}, u32[]{:S(2)}, u32[]{:S(2)}) collective-permute-start(bf16[48,256]{1,0:T(8,128)(2,1)S(1)} %get-tuple-element.41), channel_id=1, source_target_pairs={{4,0},{8,4},{12,8},{16,12},{20,16},{24,20},{28,24},{5,1},{9,5},{13... | collective-permute-start | bytes 73736 | tf_op jit(solution)/shard_map/ppermute | solution.py:401
  15.0 4.2 %collective-permute-done.1.high_ref = bf16[48,256]{1,0:T(8,128)(2,1)S(1)} collective-permute-done((bf16[48,256]{1,0:T(8,128)(2,1)S(1)}, bf16[48,256]{1,0:T(8,128)(2,1)S(1)}, u32[]{:S(2)}, u32[]{:S(2)}) %collective-permute-start.1) | collective-permute-done | bytes 24608 | tf_op jit(solution)/shard_map/ppermute | solution.py:401
  19.9 2.6 %shard_map.128 = (bf16[128,256]{1,0:T(8,128)(2,1)}, bf16[128,256]{1,0:T(8,128)(2,1)S(1)}, bf16[128,256]{1,0:T(8,128)(2,1)S(1)}) custom-call(s32[3]{0:T(128)S(1)} %copy-done.9, bf16[128,256]{1,0:T(8,128)(2,1)S(1)} %copy-done.1, bf16[128,256]{1,0:T(8,128)(2,1)S(1)} %copy-done.4, bf16[48,256]{1,0:T(8,128)(2,1)S(1)} %collective-permute-done.low_ref, ...), custom_call_target="tpu_custom_call" | custom-call | flops 1048576 | bytes 1048576 | tf_op jit(solution)/shard_map/pallas_call | solution.py:26
  22.6 2.7 %collective-permute-start.8 = (bf16[512,128]{1,0:T(8,128)(2,1)S(1)}, bf16[512,128]{1,0:T(8,128)(2,1)S(1)}, u32[]{:S(2)}, u32[]{:S(2)}) collective-permute-start(bf16[512,128]{1,0:T(8,128)(2,1)S(1)} %shard_map.132.rest_4_.rest_8_), channel_id=1, source_target_pairs={{0,16},{4,20},{8,24},{12,28},{16,0},{20,4},{24,8},{28,12},{1,17},{... | collective-permute-start | bytes 393224 | tf_op jit(solution)/shard_map/ppermute | solution.py:401
  25.2 1.5 %collective-permute-start.3 = (bf16[128,256]{1,0:T(8,128)(2,1)S(1)}, bf16[128,256]{1,0:T(8,128)(2,1)S(1)}, u32[]{:S(2)}, u32[]{:S(2)}) collective-permute-start(bf16[128,256]{1,0:T(8,128)(2,1)S(1)} %get-tuple-element.42.rest_0_), channel_id=1, source_target_pairs={{0,2},{1,3},{2,0},{3,1},{4,6},{5,7},{6,4},{7,5},{8,10},{9,11},{10,... | collective-permute-start | bytes 196616 | tf_op jit(solution)/shard_map/ppermute | solution.py:401
  28.1 1.7 %collective-permute-done.3.rest_2_ = bf16[128,256]{1,0:T(8,128)(2,1)S(1)} collective-permute-done((bf16[128,256]{1,0:T(8,128)(2,1)S(1)}, bf16[128,256]{1,0:T(8,128)(2,1)S(1)}, u32[]{:S(2)}, u32[]{:S(2)}) %collective-permute-start.3) | collective-permute-done | bytes 65568 | tf_op jit(solution)/shard_map/ppermute | solution.py:401
  29.8 1.0 %collective-permute-done.4.rest_3_ = bf16[128,256]{1,0:T(8,128)(2,1)S(1)} collective-permute-done((bf16[128,256]{1,0:T(8,128)(2,1)S(1)}, bf16[128,256]{1,0:T(8,128)(2,1)S(1)}, u32[]{:S(2)}, u32[]{:S(2)}) %collective-permute-start.4) | collective-permute-done | bytes 65568 | tf_op jit(solution)/shard_map/ppermute | solution.py:401
  31.1 1.6 %collective-permute-start.10 = (bf16[64,128]{1,0:T(8,128)(2,1)S(1)}, bf16[64,128]{1,0:T(8,128)(2,1)S(1)}, u32[]{:S(2)}, u32[]{:S(2)}) collective-permute-start(bf16[64,128]{1,0:T(8,128)(2,1)S(1)} %get-tuple-element.52), channel_id=1, source_target_pairs={{0,8},{4,12},{8,0},{12,4},{16,24},{20,28},{24,16},{28,20},{1,9},{5... | collective-permute-start | bytes 49160 | tf_op jit(solution)/shard_map/ppermute | solution.py:401
  32.8 2.3 %collective-permute-start.11 = (bf16[64,128]{1,0:T(8,128)(2,1)S(1)}, bf16[64,128]{1,0:T(8,128)(2,1)S(1)}, u32[]{:S(2)}, u32[]{:S(2)}) collective-permute-start(bf16[64,128]{1,0:T(8,128)(2,1)S(1)} %get-tuple-element.53), channel_id=1, source_target_pairs={{0,12},{4,8},{8,4},{12,0},{16,28},{20,24},{24,20},{28,16},{1,13},{... | collective-permute-start | bytes 49160 | tf_op jit(solution)/shard_map/ppermute | solution.py:401
  35.1 2.2 %shard_map.133 = (bf16[2,512,512]{2,1,0:T(8,128)(2,1)S(1)}, bf16[576,128]{1,0:T(8,128)(2,1)S(1)}, bf16[576,128]{1,0:T(8,128)(2,1)S(1)}, bf16[576,128]{1,0:T(8,128)(2,1)S(1)}, bf16[576,128]{1,0:T(8,128)(2,1)S(1)}) custom-call(s32[3]{0:T(128)S(1)} %copy-done.9, bf16[4,256,128]{2,1,0:T(8,128)(2,1)S(1)} %get-tuple-element.43.piece_ref, ...), custom_call_target="tpu_custom_call" | custom-call | flops 268435456 | bytes 1048576 | tf_op jit(solution)/shard_map/pallas_call | solution.py:26
  37.3 2.1 %collective-permute-start.16 = (bf16[576,128]{1,0:T(8,128)(2,1)S(1)}, bf16[576,128]{1,0:T(8,128)(2,1)S(1)}, u32[]{:S(2)}, u32[]{:S(2)}) collective-permute-start(bf16[576,128]{1,0:T(8,128)(2,1)S(1)} %get-tuple-element.66), channel_id=1, source_target_pairs={{0,4},{4,0},{8,12},{12,8},{16,20},{20,16},{24,28},{28,24},{1,5},{5... | collective-permute-start | bytes 442376 | tf_op jit(solution)/shard_map/ppermute | solution.py:401
  39.5 1.5 %collective-permute-start.18 = (bf16[576,128]{1,0:T(8,128)(2,1)S(1)}, bf16[576,128]{1,0:T(8,128)(2,1)S(1)}, u32[]{:S(2)}, u32[]{:S(2)}) collective-permute-start(bf16[576,128]{1,0:T(8,128)(2,1)S(1)} %get-tuple-element.68), channel_id=1, source_target_pairs={{0,12},{4,8},{8,4},{12,0},{16,28},{20,24},{24,20},{28,16},{1,13},{... | collective-permute-start | bytes 442376 | tf_op jit(solution)/shard_map/ppermute | solution.py:401
  40.9 1.7 %shard_map.134 = (bf16[512,128]{1,0:T(8,128)(2,1)S(1)}, bf16[512,128]{1,0:T(8,128)(2,1)S(1)}, bf16[256,128]{1,0:T(8,128)(2,1)S(1)}) custom-call(bf16[2,512,512]{2,1,0:T(8,128)(2,1)S(1)} %get-tuple-element.49.p_ref, bf16[192,128]{1,0:T(8,128)(2,1)S(1)} %get-tuple-element.45.refs_0_.rest_0_, bf16[192,128]{1,0:T(8,128)(2,1)S(1)} %collective-permute-done.5.refs_1_.rest_1_, ...), custom_call_target="tpu_custom_call" | custom-call | flops 536870912 | bytes 1048576 | tf_op jit(solution)/shard_map/pallas_call | solution.py:26
  43.1 3.9 %collective-permute-done.17.refs_2_ = bf16[576,128]{1,0:T(8,128)(2,1)S(1)} collective-permute-done((bf16[576,128]{1,0:T(8,128)(2,1)S(1)}, bf16[576,128]{1,0:T(8,128)(2,1)S(1)}, u32[]{:S(2)}, u32[]{:S(2)}) %collective-permute-start.17) | collective-permute-done | bytes 147488 | tf_op jit(solution)/shard_map/ppermute | solution.py:401
  47.0 1.3 %collective-permute-done.18.refs_3_ = bf16[576,128]{1,0:T(8,128)(2,1)S(1)} collective-permute-done((bf16[576,128]{1,0:T(8,128)(2,1)S(1)}, bf16[576,128]{1,0:T(8,128)(2,1)S(1)}, u32[]{:S(2)}, u32[]{:S(2)}) %collective-permute-start.18) | collective-permute-done | bytes 147488 | tf_op jit(solution)/shard_map/ppermute | solution.py:401
  48.8 1.5 %collective-permute-start.19 = (bf16[320,128]{1,0:T(8,128)(2,1)S(1)}, bf16[320,128]{1,0:T(8,128)(2,1)S(1)}, u32[]{:S(2)}, u32[]{:S(2)}) collective-permute-start(bf16[320,128]{1,0:T(8,128)(2,1)S(1)} %get-tuple-element.71), channel_id=1, source_target_pairs={{0,16},{4,20},{8,24},{12,28},{16,0},{20,4},{24,8},{28,12},{1,17},{... | collective-permute-start | bytes 245768 | tf_op jit(solution)/shard_map/ppermute | solution.py:401
  50.3 1.7 %collective-permute-done.12.refs_1_ = bf16[512,128]{1,0:T(8,128)(2,1)S(1)} collective-permute-done((bf16[512,128]{1,0:T(8,128)(2,1)S(1)}, bf16[512,128]{1,0:T(8,128)(2,1)S(1)}, u32[]{:S(2)}, u32[]{:S(2)}) %collective-permute-start.12) | collective-permute-done | bytes 131104 | tf_op jit(solution)/shard_map/ppermute | solution.py:401
  52.0 2.0 %collective-permute-start.13 = (bf16[192,128]{1,0:T(8,128)(2,1)S(1)}, bf16[192,128]{1,0:T(8,128)(2,1)S(1)}, u32[]{:S(2)}, u32[]{:S(2)}) collective-permute-start(bf16[192,128]{1,0:T(8,128)(2,1)S(1)} %get-tuple-element.58), channel_id=1, source_target_pairs={{0,4},{4,0},{8,12},{12,8},{16,20},{20,16},{24,28},{28,24},{1,5},{5... | collective-permute-start | bytes 147464 | tf_op jit(solution)/shard_map/ppermute | solution.py:401
  54.3 1.2 %collective-permute-start.15 = (bf16[192,128]{1,0:T(8,128)(2,1)S(1)}, bf16[192,128]{1,0:T(8,128)(2,1)S(1)}, u32[]{:S(2)}, u32[]{:S(2)}) collective-permute-start(bf16[192,128]{1,0:T(8,128)(2,1)S(1)} %get-tuple-element.60), channel_id=1, source_target_pairs={{0,12},{4,8},{8,4},{12,0},{16,28},{20,24},{24,20},{28,16},{1,13},{... | collective-permute-start | bytes 147464 | tf_op jit(solution)/shard_map/ppermute | solution.py:401
  56.1 1.9 %collective-permute-done.14.refs_2_ = bf16[192,128]{1,0:T(8,128)(2,1)S(1)} collective-permute-done((bf16[192,128]{1,0:T(8,128)(2,1)S(1)}, bf16[192,128]{1,0:T(8,128)(2,1)S(1)}, u32[]{:S(2)}, u32[]{:S(2)}) %collective-permute-start.14) | collective-permute-done | bytes 49184 | tf_op jit(solution)/shard_map/ppermute | solution.py:401
  58.1 1.2 %collective-permute-done.15.refs_3_ = bf16[192,128]{1,0:T(8,128)(2,1)S(1)} collective-permute-done((bf16[192,128]{1,0:T(8,128)(2,1)S(1)}, bf16[192,128]{1,0:T(8,128)(2,1)S(1)}, u32[]{:S(2)}, u32[]{:S(2)}) %collective-permute-start.15) | collective-permute-done | bytes 49184 | tf_op jit(solution)/shard_map/ppermute | solution.py:401
  (48 shorter events, 10.6 us)
Async XLA Ops:
  2.3 16.9 %copy-start.4 = (bf16[128,256]{1,0:T(8,128)(2,1)S(1)}, bf16[128,256]{1,0:T(8,128)(2,1)}, u32[]{:S(2)}) copy-start(bf16[128,256]{1,0:T(8,128)(2,1)} %g_ref.3) | copy-start | bytes 196612
  2.3 16.9 %copy-start.9 = (s32[3]{0:T(128)S(1)}, s32[3]{0:T(128)}, u32[]{:S(2)}) copy-start(s32[3]{0:T(128)} %len_ref.5) | copy-start | bytes 40
  4.8 14.4 %copy-start.1 = (bf16[128,256]{1,0:T(8,128)(2,1)S(1)}, bf16[128,256]{1,0:T(8,128)(2,1)}, u32[]{:S(2)}) copy-start(bf16[128,256]{1,0:T(8,128)(2,1)} %x_ref.5) | copy-start | bytes 196612
  4.8 25.9 %copy-start.2 = (bf16[1024,256]{1,0:T(8,128)(2,1)S(1)}, bf16[1024,256]{1,0:T(8,128)(2,1)}, u32[]{:S(2)}) copy-start(bf16[1024,256]{1,0:T(8,128)(2,1)} %proj_ref.1) | copy-start | bytes 1572868
  5.0 17.5 %collective-permute-start.5 = (bf16[192,128]{1,0:T(8,128)(2,1)S(1)}, bf16[192,128]{1,0:T(8,128)(2,1)S(1)}, u32[]{:S(2)}, u32[]{:S(2)}) collective-permute-start(bf16[192,128]{1,0:T(8,128)(2,1)S(1)} %get-tuple-element.46), channel_id=1, source_target_pairs={{0,4},{4,0},{8,12},{12,8},{16,20},{20,16},{24,28},{28,24},{1,5},{5... | collective-permute-start | bytes 147464 | tf_op jit(solution)/shard_map/ppermute | solution.py:401
  8.1 14.5 %collective-permute-start.6 = (bf16[192,128]{1,0:T(8,128)(2,1)S(1)}, bf16[192,128]{1,0:T(8,128)(2,1)S(1)}, u32[]{:S(2)}, u32[]{:S(2)}) collective-permute-start(bf16[192,128]{1,0:T(8,128)(2,1)S(1)} %get-tuple-element.47), channel_id=1, source_target_pairs={{0,8},{4,12},{8,0},{12,4},{16,24},{20,28},{24,16},{28,20},{1,9},{5... | collective-permute-start | bytes 147464 | tf_op jit(solution)/shard_map/ppermute | solution.py:401
  9.7 12.9 %collective-permute-start.7 = (bf16[192,128]{1,0:T(8,128)(2,1)S(1)}, bf16[192,128]{1,0:T(8,128)(2,1)S(1)}, u32[]{:S(2)}, u32[]{:S(2)}) collective-permute-start(bf16[192,128]{1,0:T(8,128)(2,1)S(1)} %get-tuple-element.48), channel_id=1, source_target_pairs={{0,12},{4,8},{8,4},{12,0},{16,28},{20,24},{24,20},{28,16},{1,13},{... | collective-permute-start | bytes 147464 | tf_op jit(solution)/shard_map/ppermute | solution.py:401
  9.7 5.3 %collective-permute-start = (bf16[48,256]{1,0:T(8,128)(2,1)S(1)}, bf16[48,256]{1,0:T(8,128)(2,1)S(1)}, u32[]{:S(2)}, u32[]{:S(2)}) collective-permute-start(bf16[48,256]{1,0:T(8,128)(2,1)S(1)} %get-tuple-element.40.after_ref), channel_id=1, source_target_pairs={{0,4},{4,8},{8,12},{12,16},{16,20},{20,24},{24,28},{1,5},{5,9},{9,... | collective-permute-start | bytes 73736 | tf_op jit(solution)/shard_map/ppermute | solution.py:401
  13.5 5.7 %collective-permute-start.1 = (bf16[48,256]{1,0:T(8,128)(2,1)S(1)}, bf16[48,256]{1,0:T(8,128)(2,1)S(1)}, u32[]{:S(2)}, u32[]{:S(2)}) collective-permute-start(bf16[48,256]{1,0:T(8,128)(2,1)S(1)} %get-tuple-element.41), channel_id=1, source_target_pairs={{4,0},{8,4},{12,8},{16,12},{20,16},{24,20},{28,24},{5,1},{9,5},{13... | collective-permute-start | bytes 73736 | tf_op jit(solution)/shard_map/ppermute | solution.py:401
  22.6 12.5 %collective-permute-start.8 = (bf16[512,128]{1,0:T(8,128)(2,1)S(1)}, bf16[512,128]{1,0:T(8,128)(2,1)S(1)}, u32[]{:S(2)}, u32[]{:S(2)}) collective-permute-start(bf16[512,128]{1,0:T(8,128)(2,1)S(1)} %shard_map.132.rest_4_.rest_8_), channel_id=1, source_target_pairs={{0,16},{4,20},{8,24},{12,28},{16,0},{20,4},{24,8},{28,12},{1,17},{... | collective-permute-start | bytes 393224 | tf_op jit(solution)/shard_map/ppermute | solution.py:401
  25.2 2.8 %collective-permute-start.2 = (bf16[128,256]{1,0:T(8,128)(2,1)S(1)}, bf16[128,256]{1,0:T(8,128)(2,1)S(1)}, u32[]{:S(2)}, u32[]{:S(2)}) collective-permute-start(bf16[128,256]{1,0:T(8,128)(2,1)S(1)} %get-tuple-element.42.rest_0_), channel_id=1, source_target_pairs={{0,1},{1,0},{2,3},{3,2},{4,5},{5,4},{6,7},{7,6},{8,9},{9,8},{10,11... | collective-permute-start | bytes 196616 | tf_op jit(solution)/shard_map/ppermute | solution.py:401
  25.2 4.5 %collective-permute-start.3 = (bf16[128,256]{1,0:T(8,128)(2,1)S(1)}, bf16[128,256]{1,0:T(8,128)(2,1)S(1)}, u32[]{:S(2)}, u32[]{:S(2)}) collective-permute-start(bf16[128,256]{1,0:T(8,128)(2,1)S(1)} %get-tuple-element.42.rest_0_), channel_id=1, source_target_pairs={{0,2},{1,3},{2,0},{3,1},{4,6},{5,7},{6,4},{7,5},{8,10},{9,11},{10,... | collective-permute-start | bytes 196616 | tf_op jit(solution)/shard_map/ppermute | solution.py:401
  26.7 4.0 %collective-permute-start.4 = (bf16[128,256]{1,0:T(8,128)(2,1)S(1)}, bf16[128,256]{1,0:T(8,128)(2,1)S(1)}, u32[]{:S(2)}, u32[]{:S(2)}) collective-permute-start(bf16[128,256]{1,0:T(8,128)(2,1)S(1)} %get-tuple-element.42.rest_0_), channel_id=1, source_target_pairs={{0,3},{1,2},{2,1},{3,0},{4,7},{5,6},{6,5},{7,4},{8,11},{9,10},{10,... | collective-permute-start | bytes 196616 | tf_op jit(solution)/shard_map/ppermute | solution.py:401
  31.1 8.4 %collective-permute-start.10 = (bf16[64,128]{1,0:T(8,128)(2,1)S(1)}, bf16[64,128]{1,0:T(8,128)(2,1)S(1)}, u32[]{:S(2)}, u32[]{:S(2)}) collective-permute-start(bf16[64,128]{1,0:T(8,128)(2,1)S(1)} %get-tuple-element.52), channel_id=1, source_target_pairs={{0,8},{4,12},{8,0},{12,4},{16,24},{20,28},{24,16},{28,20},{1,9},{5... | collective-permute-start | bytes 49160 | tf_op jit(solution)/shard_map/ppermute | solution.py:401
  32.8 8.2 %collective-permute-start.11 = (bf16[64,128]{1,0:T(8,128)(2,1)S(1)}, bf16[64,128]{1,0:T(8,128)(2,1)S(1)}, u32[]{:S(2)}, u32[]{:S(2)}) collective-permute-start(bf16[64,128]{1,0:T(8,128)(2,1)S(1)} %get-tuple-element.53), channel_id=1, source_target_pairs={{0,12},{4,8},{8,4},{12,0},{16,28},{20,24},{24,20},{28,16},{1,13},{... | collective-permute-start | bytes 49160 | tf_op jit(solution)/shard_map/ppermute | solution.py:401
  35.1 5.9 %collective-permute-start.9 = (bf16[64,128]{1,0:T(8,128)(2,1)S(1)}, bf16[64,128]{1,0:T(8,128)(2,1)S(1)}, u32[]{:S(2)}, u32[]{:S(2)}) collective-permute-start(bf16[64,128]{1,0:T(8,128)(2,1)S(1)} %get-tuple-element.51), channel_id=1, source_target_pairs={{0,4},{4,0},{8,12},{12,8},{16,20},{20,16},{24,28},{28,24},{1,5},{5... | collective-permute-start | bytes 49160 | tf_op jit(solution)/shard_map/ppermute | solution.py:401
  37.3 5.8 %collective-permute-start.16 = (bf16[576,128]{1,0:T(8,128)(2,1)S(1)}, bf16[576,128]{1,0:T(8,128)(2,1)S(1)}, u32[]{:S(2)}, u32[]{:S(2)}) collective-permute-start(bf16[576,128]{1,0:T(8,128)(2,1)S(1)} %get-tuple-element.66), channel_id=1, source_target_pairs={{0,4},{4,0},{8,12},{12,8},{16,20},{20,16},{24,28},{28,24},{1,5},{5... | collective-permute-start | bytes 442376 | tf_op jit(solution)/shard_map/ppermute | solution.py:401
  39.4 7.6 %collective-permute-start.17 = (bf16[576,128]{1,0:T(8,128)(2,1)S(1)}, bf16[576,128]{1,0:T(8,128)(2,1)S(1)}, u32[]{:S(2)}, u32[]{:S(2)}) collective-permute-start(bf16[576,128]{1,0:T(8,128)(2,1)S(1)} %get-tuple-element.67), channel_id=1, source_target_pairs={{0,8},{4,12},{8,0},{12,4},{16,24},{20,28},{24,16},{28,20},{1,9},{5... | collective-permute-start | bytes 442376 | tf_op jit(solution)/shard_map/ppermute | solution.py:401
  39.5 8.8 %collective-permute-start.18 = (bf16[576,128]{1,0:T(8,128)(2,1)S(1)}, bf16[576,128]{1,0:T(8,128)(2,1)S(1)}, u32[]{:S(2)}, u32[]{:S(2)}) collective-permute-start(bf16[576,128]{1,0:T(8,128)(2,1)S(1)} %get-tuple-element.68), channel_id=1, source_target_pairs={{0,12},{4,8},{8,4},{12,0},{16,28},{20,24},{24,20},{28,16},{1,13},{... | collective-permute-start | bytes 442376 | tf_op jit(solution)/shard_map/ppermute | solution.py:401
  42.6 9.4 %collective-permute-start.12 = (bf16[512,128]{1,0:T(8,128)(2,1)S(1)}, bf16[512,128]{1,0:T(8,128)(2,1)S(1)}, u32[]{:S(2)}, u32[]{:S(2)}) collective-permute-start(bf16[512,128]{1,0:T(8,128)(2,1)S(1)} %get-tuple-element.55), channel_id=1, source_target_pairs={{0,16},{4,20},{8,24},{12,28},{16,0},{20,4},{24,8},{28,12},{1,17},{... | collective-permute-start | bytes 393224 | tf_op jit(solution)/shard_map/ppermute | solution.py:401
  48.8 11.4 %collective-permute-start.19 = (bf16[320,128]{1,0:T(8,128)(2,1)S(1)}, bf16[320,128]{1,0:T(8,128)(2,1)S(1)}, u32[]{:S(2)}, u32[]{:S(2)}) collective-permute-start(bf16[320,128]{1,0:T(8,128)(2,1)S(1)} %get-tuple-element.71), channel_id=1, source_target_pairs={{0,16},{4,20},{8,24},{12,28},{16,0},{20,4},{24,8},{28,12},{1,17},{... | collective-permute-start | bytes 245768 | tf_op jit(solution)/shard_map/ppermute | solution.py:401
  52.0 4.2 %collective-permute-start.13 = (bf16[192,128]{1,0:T(8,128)(2,1)S(1)}, bf16[192,128]{1,0:T(8,128)(2,1)S(1)}, u32[]{:S(2)}, u32[]{:S(2)}) collective-permute-start(bf16[192,128]{1,0:T(8,128)(2,1)S(1)} %get-tuple-element.58), channel_id=1, source_target_pairs={{0,4},{4,0},{8,12},{12,8},{16,20},{20,16},{24,28},{28,24},{1,5},{5... | collective-permute-start | bytes 147464 | tf_op jit(solution)/shard_map/ppermute | solution.py:401
  54.0 4.1 %collective-permute-start.14 = (bf16[192,128]{1,0:T(8,128)(2,1)S(1)}, bf16[192,128]{1,0:T(8,128)(2,1)S(1)}, u32[]{:S(2)}, u32[]{:S(2)}) collective-permute-start(bf16[192,128]{1,0:T(8,128)(2,1)S(1)} %get-tuple-element.59), channel_id=1, source_target_pairs={{0,8},{4,12},{8,0},{12,4},{16,24},{20,28},{24,16},{28,20},{1,9},{5... | collective-permute-start | bytes 147464 | tf_op jit(solution)/shard_map/ppermute | solution.py:401
  54.3 5.0 %collective-permute-start.15 = (bf16[192,128]{1,0:T(8,128)(2,1)S(1)}, bf16[192,128]{1,0:T(8,128)(2,1)S(1)}, u32[]{:S(2)}, u32[]{:S(2)}) collective-permute-start(bf16[192,128]{1,0:T(8,128)(2,1)S(1)} %get-tuple-element.60), channel_id=1, source_target_pairs={{0,12},{4,8},{8,4},{12,0},{16,28},{20,24},{24,20},{28,16},{1,13},{... | collective-permute-start | bytes 147464 | tf_op jit(solution)/shard_map/ppermute | solution.py:401
  (6 other events, 4.9 us)

commit v4 on v3

--- a/solution.py
+++ b/solution.py
@@ -14,6 +14,7 @@
 BF = jnp.bfloat16
 F32 = jnp.float32
 VM = pl.BlockSpec(memory_space=pltpu.VMEM)
+HB = pl.BlockSpec(memory_space=pltpu.HBM)
 SM = pl.BlockSpec(memory_space=pltpu.SMEM)
 
 
@@ -21,12 +22,12 @@
     return lax.dot_general(a, b, (dims, ((), ())), preferred_element_type=F32)
 
 
-def call(kernel, out_shape, args, smem=0, scratch=(), flops=1 << 20, limit=None):
+def call(kernel, out_shape, args, smem=0, hbm=0, scratch=(), flops=1 << 20, limit=None):
     one = not isinstance(out_shape, (tuple, list))
     return pl.pallas_call(
         kernel,
         out_shape=out_shape,
-        in_specs=[SM] * smem + [VM] * (len(args) - smem),
+        in_specs=[SM] * smem + [HB] * hbm + [VM] * (len(args) - smem - hbm),
         out_specs=VM if one else tuple(VM for _ in out_shape),
         scratch_shapes=list(scratch),
         compiler_params=pltpu.CompilerParams(vmem_limit_bytes=limit or (4 << 20)),
@@ -38,8 +39,21 @@
     return jax.ShapeDtypeStruct(tuple(dims), dtype)
 
 
-def member(members):
-    return lax.rem(lax.axis_index("ctx"), members)
+OUTER = False
+
+
+def ctx_of(m, g, members, groups):
+    return m * groups + g if OUTER else g * members + m
+
+
+def member(members, ctx=None):
+    ctx = lax.axis_index("ctx") if ctx is None else ctx
+    return ctx // (lax.axis_size("ctx") // members) if OUTER else ctx % members
+
+
+def group_of(members, ctx=None):
+    ctx = lax.axis_index("ctx") if ctx is None else ctx
+    return ctx % (lax.axis_size("ctx") // members) if OUTER else ctx // members
 
 
 def total_of(lengths_ref):
@@ -49,19 +63,28 @@
     return total
 
 
-def halo_kernel(x_ref, g_ref, up_ref, down_ref):
-    rows = x_ref.shape[0]
+def start_kernel(members, *refs):
+    q_hbm, k_hbm, v_hbm, x_hbm, g_hbm, w_hbm, x_ref, g_ref, w_ref, up_ref, down_ref, *rest = refs
+    slots, (q_ref, k_ref, v_ref, buf, sems) = rest[:members], rest[members:]
+    rows = q_ref.shape[0]
+    half = rows // 2
+    moves = (
+        (x_hbm, x_ref),
+        (g_hbm, g_ref),
+        (k_hbm, k_ref),
+        (v_hbm, v_ref),
+        (q_hbm, q_ref),
+        (w_hbm, w_ref),
+    )
+    copies = [pltpu.make_async_copy(a, b, sems.at[i]) for i, (a, b) in enumerate(moves)]
+    for copy in copies:
+        copy.start()
+    for copy in copies:
+        copy.wait()
     up_ref[0:HALO_X] = x_ref[rows - HALO_X :]
     up_ref[HALO_X:] = g_ref[rows - HALO_G :]
     down_ref[0:HALO_X] = x_ref[0:HALO_X]
     down_ref[HALO_X:] = g_ref[0:HALO_G]
-
-
-def pack_kernel(q_ref, k_ref, v_ref, after_ref, *rest):
-    slots, buf = rest[:-1], rest[-1]
-    members = len(slots)
-    rows = q_ref.shape[0]
-    half = rows // 2
     for m in range(members):
         cols = slice(m * HEAD_DIM, (m + 1) * HEAD_DIM)
         buf[m, 0:rows, 0:HEAD_DIM] = k_ref[:, cols]
@@ -84,68 +107,72 @@
     rows = x_ref.shape[0]
     base = lax.axis_index("ctx") * rows - HALO_X
     total = total_of(len_ref)
-    xs[0:HALO_X] = low_ref[0:HALO_X].astype(F32)
-    xs[HALO_X : HALO_X + rows] = x_ref[...].astype(F32)
-    xs[HALO_X + rows :] = high_ref[0:HALO_X].astype(F32)
-
-    @pl.when(base + xs.shape[0] > total)
+    for c in range(xs.shape[0]):
+        cols = slice(c * 128, (c + 1) * 128)
+        xs[c, 0:HALO_X] = low_ref[0:HALO_X, cols].astype(F32)
+        xs[c, HALO_X : HALO_X + rows] = x_ref[:, cols].astype(F32)
+        xs[c, HALO_X + rows :] = high_ref[0:HALO_X, cols].astype(F32)
+
+    @pl.when(base + xs.shape[1] > total)
     def _():
-        pos = base + lax.broadcasted_iota(jnp.int32, xs.shape, 0)
-        xs[...] = jnp.where(pos < total, xs[...], 0.0)
+        for c in range(xs.shape[0]):
+            pos = base + lax.broadcasted_iota(jnp.int32, xs.shape[1:], 0)
+            xs[c] = jnp.where(pos < total, xs[c], 0.0)
 
 
 def conv_kernel(
     len_ref, x_ref, g_ref, low_ref, high_ref, w_ref, out_ref, send_ref, mine_ref, xs, gs
 ):
-    rows, width = x_ref.shape
+    rows = x_ref.shape[0]
     taps = w_ref.shape[0]
     half = taps // 2
-    masked_into(xs, len_ref, x_ref, low_ref, high_ref)
-    w = w_ref[...].astype(F32)
     wide = rows + 2 * HALO_G
     shift = HALO_X - HALO_G - half
-    acc = jnp.zeros((wide, width), F32)
-    for j in range(taps):
-        acc = acc + w[j : j + 1] * xs[shift + j : shift + j + wide]
-    s = jax.nn.sigmoid(acc)
-    slope = s * (1.0 + acc * (1.0 - s))
-    gs[0:HALO_G] = low_ref[HALO_X:].astype(F32)
-    gs[HALO_G : HALO_G + rows] = g_ref[...].astype(F32)
-    gs[HALO_G + rows :] = high_ref[HALO_X:].astype(F32)
-    gs[...] = (gs[...] * slope).astype(BF).astype(F32)
-    acc = jnp.zeros((rows, width), F32)
-    for j in range(taps):
-        first = HALO_G + half - j
-        acc = acc + w[j : j + 1] * gs[first : first + rows]
-    pos = lax.axis_index("ctx") * rows + lax.broadcasted_iota(jnp.int32, acc.shape, 0)
-    acc = jnp.where(pos < total_of(len_ref), acc, 0.0)
-    out = (g_ref[...].astype(F32) + acc).astype(BF)
-    out_ref[...] = out
-    send_ref[...] = out
-    mine_ref[...] = gs[HALO_G : HALO_G + rows].astype(BF)
-
-
-def taps_kernel(taps, len_ref, x_ref, low_ref, high_ref, mine_ref, tap_ref, xs):
-    rows, width = x_ref.shape
+    total = total_of(len_ref)
+    masked_into(xs, len_ref, x_ref, low_ref, high_ref)
+    for c in range(xs.shape[0]):
+        cols = slice(c * 128, (c + 1) * 128)
+        w = w_ref[:, cols].astype(F32)
+        acc = jnp.zeros((wide, 128), F32)
+        for j in range(taps):
+            acc = acc + w[j : j + 1] * xs[c, shift + j : shift + j + wide]
+        s = jax.nn.sigmoid(acc)
+        slope = s * (1.0 + acc * (1.0 - s))
+        gs[c, 0:HALO_G] = low_ref[HALO_X:, cols].astype(F32)
+        gs[c, HALO_G : HALO_G + rows] = g_ref[:, cols].astype(F32)
+        gs[c, HALO_G + rows :] = high_ref[HALO_X:, cols].astype(F32)
+        gs[c] = (gs[c] * slope).astype(BF).astype(F32)
+        acc = jnp.zeros((rows, 128), F32)
+        for j in range(taps):
+            first = HALO_G + half - j
+            acc = acc + w[j : j + 1] * gs[c, first : first + rows]
+        pos = lax.axis_index("ctx") * rows + lax.broadcasted_iota(jnp.int32, acc.shape, 0)
+        acc = jnp.where(pos < total, acc, 0.0)
+        out = (g_ref[:, cols].astype(F32) + acc).astype(BF)
+        out_ref[:, cols] = out
+        send_ref[:, cols] = out
+        mine_ref[:, cols] = gs[c, HALO_G : HALO_G + rows].astype(BF)
+
+
+def taps_kernel(taps, len_ref, x_ref, low_ref, high_ref, mine_ref, after_ref, tap_ref, xs):
+    rows = x_ref.shape[0]
     half = taps // 2
-    sides = width // 128
+    sides = xs.shape[0]
     tap_rows = tap_ref.shape[0] // sides
     masked_into(xs, len_ref, x_ref, low_ref, high_ref)
-    mine = mine_ref[...].astype(F32)
-    sums = []
-    for j in range(taps):
-        first = HALO_X - half + j
-        sums.append(jnp.sum(mine * xs[first : first + rows], axis=0, keepdims=True))
-    sums.append(jnp.zeros((tap_rows - taps, width), F32))
-    out = jnp.concatenate(sums, 0).astype(BF)
-    for side in range(sides):
-        tap_ref[side * tap_rows : (side + 1) * tap_rows] = out[:, side * 128 : (side + 1) * 128]
+    for c in range(sides):
+        mine = mine_ref[:, c * 128 : (c + 1) * 128].astype(F32)
+        sums = []
+        for j in range(taps):
+            first = HALO_X - half + j
+            sums.append(jnp.sum(mine * xs[c, first : first + rows], axis=0, keepdims=True))
+        sums.append(jnp.zeros((tap_rows - taps, 128), F32))
+        tap_ref[c * tap_rows : (c + 1) * tap_rows] = jnp.concatenate(sums, 0).astype(BF)
 
 
 def spread_kernel(pieces, members, proj_ref, *rest):
-    n_heads = len(rest) - members - 4
-    xs, go_refs = rest[:n_heads], rest[n_heads : n_heads + members]
-    piece_ref, full, go_buf, piece_buf = rest[n_heads + members :]
+    n_heads = len(rest) - members - 2
+    xs, slots, (full, buf) = rest[:n_heads], rest[n_heads:-2], rest[-2:]
     rows, width = xs[0].shape
     half = rows // 2
     mine = lax.axis_index("head")
@@ -157,16 +184,15 @@
     go = go.astype(BF)
     for m in range(members):
         cols = slice(m * HEAD_DIM, (m + 1) * HEAD_DIM)
-        go_buf[m, :, 0:HEAD_DIM] = go[0:half, cols]
-        go_buf[m, :, HEAD_DIM:] = go[half:, cols]
+        buf[m, 0:half, 0:HEAD_DIM] = go[0:half, cols]
+        buf[m, 0:half, HEAD_DIM:] = go[half:, cols]
         for i, first in enumerate(pieces[m]):
-            piece_buf[m, i * rows : (i + 1) * rows] = full[first // width][
+            buf[m, half + i * rows : half + (i + 1) * rows] = full[first // width][
                 :, first % width : first % width + 128
             ]
     me = member(members)
     for k in range(members):
-        go_refs[k][...] = go_buf[me ^ k]
-        piece_ref[k] = piece_buf[me ^ k]
+        slots[k][...] = buf[me ^ k]
 
 
 def widened(x, keep_high):
@@ -196,15 +222,14 @@
     return (widened(q, False) * scale).astype(BF)
 
 
-def forward_kernel(n_keys, members, scale, len_ref, piece_ref, tap_ref, *rest):
+def forward_kernel(n_keys, members, scale, len_ref, tap_ref, *rest):
     got, rest = rest[:members], rest[members:]
     kv, rest = rest[:n_keys], rest[n_keys:]
-    p_ref, slots, (s_ref, m_ref, l_ref, acc_ref) = rest[0], rest[1 : 1 + members], rest[1 + members :]
+    p_ref, slot_ref, s_ref, m_ref, l_ref, acc_ref = rest
     groups, keys, queries = s_ref.shape
     rows = keys // members
     total = total_of(len_ref)
-    ctx = lax.axis_index("ctx")
-    me, group = lax.rem(ctx, members), lax.div(ctx, members)
+    me, group = member(members), group_of(members)
     q = queries_of(got, scale)
     m_ref[...] = jnp.full(m_ref.shape, -1e30, F32)
     l_ref[...] = jnp.zeros(l_ref.shape, F32)
@@ -212,13 +237,14 @@
 
     def scores(g):
         s = dot(key_block(kv, g), q, ((1,), (1,)))
-        start = (lax.rem(group + g, groups) if n_keys > 1 else g) * keys
+        from_group = lax.rem(group + g, groups) if n_keys > 1 else g
         s_ref[g] = s
 
-        @pl.when(start + keys > total)
+        @pl.when((ctx_of(members - 1, from_group, members, groups) + 1) * rows > total)
         def _():
             for k in range(members):
-                pos = start + (me ^ k) * rows + lax.broadcasted_iota(jnp.int32, (rows, queries), 0)
+                start = ctx_of(me ^ k, from_group, members, groups) * rows
+                pos = start + lax.broadcasted_iota(jnp.int32, (rows, queries), 0)
                 part = s_ref[g, k * rows : (k + 1) * rows]
                 s_ref[g, k * rows : (k + 1) * rows] = jnp.where(pos < total, part, -1e30)
 
@@ -242,12 +268,9 @@
     over(groups, values)
     attn = acc_ref[HEAD_DIM:, :].T.astype(BF)
     half = queries // 2
-    count = piece_ref.shape[1]
-    for k in range(members):
-        slots[k][0:count] = piece_ref[k]
-        slots[k][count : count + half, 0:HEAD_DIM] = attn[0:half]
-        slots[k][count : count + half, HEAD_DIM:] = attn[half:]
-        slots[k][count + half :] = tap_ref[...]
+    slot_ref[0:half, 0:HEAD_DIM] = attn[0:half]
+    slot_ref[0:half, HEAD_DIM:] = attn[half:]
+    slot_ref[half:] = tap_ref[...]
 
 
 def backward_kernel(n_keys, members, scale, p_ref, *rest):
@@ -257,7 +280,8 @@
     dkv, (dq_ref, s_ref, d_ref, acc_ref) = rest[:n_keys], rest[n_keys:]
     groups, _, queries = s_ref.shape
     q = queries_of(got, scale)
-    go = widened(jnp.concatenate([r[...] for r in gos], 0), True).astype(BF)
+    half = queries // members // 2
+    go = widened(jnp.concatenate([r[0:half] for r in gos], 0), True).astype(BF)
     d_ref[...] = jnp.zeros(d_ref.shape, F32)
     acc_ref[...] = jnp.zeros(acc_ref.shape, F32)
 
@@ -286,25 +310,25 @@
 
 
 def project_kernel(own_rows, members, *refs):
-    slots, outs, (lhs, rhs, heads) = refs[:members], refs[members:-3], refs[-3:]
+    gos, slots = refs[:members], refs[members : 2 * members]
+    outs, (lhs, rhs, heads) = refs[2 * members : -3], refs[-3:]
     out_ref, tap_ref = outs[:2]
     count, width = lhs.shape[1], rhs.shape[1]
     half = lhs.shape[0] // members
     rows = 2 * half
     me = member(members)
-    first = count // 128 * rows
     acc = jnp.zeros((count, width), F32)
-    tap = jnp.zeros((slots[0].shape[0] - first - members * half, 128), F32)
+    tap = jnp.zeros(tap_ref.shape, F32)
     for k in range(members):
-        heads[me ^ k] = slots[k][first : first + members * half]
-        tap = tap + slots[k][first + members * half :].astype(F32)
+        heads[me ^ k] = slots[k][0 : members * half]
+        tap = tap + slots[k][members * half :].astype(F32)
     tap_ref[...] = tap.astype(BF)
     for fold in range(2):
         for k in range(members):
             for side in range(count // 128):
-                at = side * rows + fold * half
+                at = half + side * rows + fold * half
                 where = pl.multiple_of((me ^ k) * half, half)
-                lhs[pl.ds(where, half), side * 128 : (side + 1) * 128] = slots[k][at : at + half]
+                lhs[pl.ds(where, half), side * 128 : (side + 1) * 128] = gos[k][at : at + half]
         for h in range(members):
             for i in range(members):
                 j = h ^ i
@@ -316,7 +340,7 @@
         out_ref[...] = acc
         return
     send_ref = outs[2]
-    first = lax.axis_index("ctx") < lax.axis_size("ctx") // 2
+    first = group_of(members) == 0
     low, high = acc[:own_rows], acc[own_rows:]
     out_ref[...] = jnp.where(first, low, high)
     theirs = jnp.where(first, high, low).astype(BF)
@@ -339,6 +363,11 @@
     for k in range(members):
         slots[k][0:rows] = total[k * rows : (k + 1) * rows]
         slots[k][rows:] = dq_ref[k * half : (k + 1) * half]
+
+
+def end_kernel(members, *refs):
+    finish_kernel(*refs[members : members + 3], *refs[members + 6 : members + 8])
+    unpack_kernel(*refs[:members], *refs[members + 3 : members + 6], refs[-1])
 
 
 def unpack_kernel(*refs):
@@ -388,40 +417,51 @@
     keys = members * rows
     queries = members * rows
     pair = groups == 2
-    across = [[g * members + m for g in range(groups)] for m in range(members)]
-    other = [(i, (i + members) % n_ctx) for i in range(n_ctx)]
+    across = [[ctx_of(m, g, members, groups) for g in range(groups)] for m in range(members)]
+
+    def partners(change):
+        return [
+            (i, ctx_of(*change(member(members, i), group_of(members, i)), members, groups))
+            for i in range(n_ctx)
+        ]
+
+    other = partners(lambda m, g: (m, (g + 1) % groups))
 
     def swap(slots, axis="ctx"):
-        n = lax.axis_size(axis)
-        return [slots[0]] + [
-            move(slots[k], [(i, i ^ k) for i in range(n)], axis) for k in range(1, len(slots))
-        ]
+        def by_xor(k):
+            if axis == "ctx":
+                return partners(lambda m, g: (m ^ k, g))
+            return [(i, i ^ k) for i in range(n_heads)]
+
+        return [slots[0]] + [move(slots[k], by_xor(k), axis) for k in range(1, len(slots))]
 
     def move(x, pairs, axis="ctx"):
         return lax.ppermute(x, axis, pairs)
 
-    up, down = call(
-        halo_kernel, (shape((HALO_X + HALO_G, width), BF),) * 2, (conv_input, cotangent)
+    slot = shape((rows + half, 128), BF)
+    halo = shape((HALO_X + HALO_G, width), BF)
+    given = (query_all, key_all, value_all, conv_input, cotangent, conv_weight)
+    x_in, g_in, w_in, up, down, *slots = call(
+        functools.partial(start_kernel, members),
+        (shape((rows, width), BF),) * 2
+        + (shape(conv_weight.shape, BF), halo, halo)
+        + (slot,) * members,
+        tuple(pltpu.with_memory_space_constraint(x, pltpu.HBM) for x in given),
+        hbm=len(given),
+        scratch=[pltpu.VMEM((rows, width), BF)] * 3
+        + [pltpu.VMEM((members, rows + half, 128), BF), pltpu.SemaphoreType.DMA((len(given),))],
     )
     low = move(up, [(i, i + 1) for i in range(n_ctx - 1)])
     high = move(down, [(i + 1, i) for i in range(n_ctx - 1)])
-    slot = shape((rows + half, 128), BF)
-    got = swap(
-        call(
-            pack_kernel,
-            (slot,) * members,
-            (query_all, key_all, value_all, up),
-            scratch=[pltpu.VMEM((members, rows + half, 128), BF)],
-        ),
-    )
+    got = swap(slots)
     x_grad, x_send, grad_conv = call(
         conv_kernel,
         (shape((rows, width), BF),) * 3,
-        (rec_lengths, conv_input, cotangent, low, high, conv_weight),
+        (rec_lengths, x_in, g_in, low, high, w_in),
         smem=1,
         scratch=[
-            pltpu.VMEM((rows + 2 * HALO_X, width), F32),
-            pltpu.VMEM((rows + 2 * HALO_G, width), F32),
+            pltpu.VMEM((sides, rows + 2 * HALO_X, 128), F32),
+            pltpu.VMEM((sides, rows + 2 * HALO_G, 128), F32),
         ],
     )
     xs = swap([x_send] * n_heads, "head")
@@ -431,41 +471,42 @@
     else:
         kv = (lax.all_gather(own_kv, "ctx", axis_index_groups=across),)
     n_keys = len(kv)
+    count = groups * own_rows
+    aligned = OUTER or own_rows % 128 == 0
+    pieces = [
+        [ctx_of(m, g, members, groups) * own_rows + b for g in range(groups) for b in range(0, own_rows, 128)]
+        if own_rows % 128 == 0
+        else list(range(m * count, (m + 1) * count, 128))
+        for m in range(members)
+    ]
+    gradient_rows = half + count // 128 * rows
+    spread = call(
+        functools.partial(spread_kernel, pieces, members),
+        (shape((gradient_rows, 128), BF),) * members,
+        (out_proj, *xs),
+        scratch=[
+            pltpu.VMEM((n_heads, rows, width), BF),
+            pltpu.VMEM((members, gradient_rows, 128), BF),
+        ],
+        flops=2 * rows * channels * width,
+    )
+    gos = swap(spread)
     tap_part = call(
         functools.partial(taps_kernel, taps),
         shape((sides * tap_rows, 128), BF),
-        (rec_lengths, conv_input, low, high, grad_conv),
+        (rec_lengths, x_in, low, high, grad_conv, spread[0]),
         smem=1,
-        scratch=[pltpu.VMEM((rows + 2 * HALO_X, width), F32)],
-    )
-    count = groups * own_rows
-    if own_rows % 128 == 0:
-        pieces = [
-            [(g * members + m) * own_rows + b for g in range(groups) for b in range(0, own_rows, 128)]
-            for m in range(members)
-        ]
-    else:
-        pieces = [list(range(m * count, (m + 1) * count, 128)) for m in range(members)]
-    spread = call(
-        functools.partial(spread_kernel, pieces, members),
-        (shape((half, 128), BF),) * members + (shape((members, count // 128 * rows, 128), BF),),
-        (out_proj, *xs),
-        scratch=[
-            pltpu.VMEM((n_heads, rows, width), BF),
-            pltpu.VMEM((members, half, 128), BF),
-            pltpu.VMEM((members, count // 128 * rows, 128), BF),
-        ],
-        flops=2 * rows * channels * width,
-    )
-    piece = spread[members]
-    gos = swap(spread[:members])
+        scratch=[pltpu.VMEM((sides, rows + 2 * HALO_X, 128), F32)],
+    )
     big = (12 << 20) if groups <= 2 else (60 << 20)
     flops = 2 * queries * keys * groups * 128
     fwd = call(
         functools.partial(forward_kernel, n_keys, members, scale),
-        (shape((groups, keys, queries), BF),)
-        + (shape((count // 128 * rows + queries // 2 + sides * tap_rows, 128), BF),) * members,
-        (rec_lengths, piece, tap_part, *got, *kv),
+        (
+            shape((groups, keys, queries), BF),
+            shape((queries // 2 + sides * tap_rows, 128), BF),
+        ),
+        (rec_lengths, tap_part, *got, *kv),
         smem=1,
         scratch=[
             pltpu.VMEM((groups, keys, queries), F32),
@@ -500,13 +541,7 @@
     else:
         parts = (lax.all_to_all(bwd[0], "ctx", 0, 0, axis_index_groups=across),)
     back = swap(call(functools.partial(collect_kernel, members), (slot,) * members, (*parts, dq)))
-    q_grad, k_grad, v_grad = call(
-        unpack_kernel,
-        (shape((rows, width), BF),) * 3,
-        tuple(back),
-        scratch=[pltpu.VMEM((members, rows + half, 128), BF)],
-    )
-    shared = swap(fwd[1:])
+    shared = swap([fwd[1]] * members)
     merged = pair and own_rows % 16 == 0
     tap_shape = shape((sides * tap_rows, 128), BF)
     outs = (
@@ -517,7 +552,7 @@
     partial, tap_sum, *send = call(
         functools.partial(project_kernel, own_rows, members),
         outs,
-        tuple(shared),
+        (*gos, *shared),
         scratch=[
             pltpu.VMEM((members * half, count), BF),
             pltpu.VMEM((members * half, width), BF),
@@ -525,17 +560,22 @@
         ],
         flops=2 * count * width * queries,
     )
-    grads = (shape((own_rows, width), F32), shape((taps, width), F32))
+    grads = (shape((rows, width), BF),) * 3
+    buf = [pltpu.VMEM((members, rows + half, 128), BF)]
     if merged:
-        out_proj_grad, conv_weight_grad = call(
-            finish_kernel, grads, (partial, tap_sum, move(send[0], other))
+        q_grad, k_grad, v_grad, out_proj_grad, conv_weight_grad = call(
+            functools.partial(end_kernel, members),
+            grads + (shape((own_rows, width), F32), shape((taps, width), F32)),
+            (*back, partial, tap_sum, move(send[0], other)),
+            scratch=buf,
         )
     else:
-        if own_rows % 128:
+        q_grad, k_grad, v_grad = call(unpack_kernel, grads, tuple(back), scratch=buf)
+        if not aligned:
             wanted = partial.astype(BF).reshape(1, groups, own_rows, width)
             slots = jnp.zeros((members, groups, own_rows, width), BF)
             slots = lax.dynamic_update_slice(
-                slots, wanted, (lax.rem(lax.axis_index("ctx"), members), 0, 0, 0)
+                slots, wanted, (member(members), 0, 0, 0)
             )
             moved = lax.all_to_all(slots.reshape(n_ctx, own_rows, width), "ctx", 0, 0)
         else:

time: 61.3 us -> 56.8 us (0.927)
  local copies, waits for them, and re-layouts: 4.91 us -> 0.66 us
  starting transfers between devices: 27.3 us -> 28.6 us
  waiting for transfers between devices: 17.8 us -> 17 us
    unnamed x20 -> x6, local copies, waits for them, and re-layouts: 4.91 us -> 0.66 us
    ppermute x20, starting transfers between devices: 27.3 us -> 28.6 us  [move(): return lax.ppermute(x, axis, pairs)]
    ppermute x20, waiting for transfers between devices: 17.8 us -> 17 us  [move(): return lax.ppermute(x, axis, pairs)]
    pallas_call x12 -> x10, Pallas kernels: 10.1 us -> 9.63 us  [call(): pl.pallas_call(kernel, out_shape=out_shape, in_specs=[SM] * smem + [HB] *...]
  transfers between devices with their start and end apart: 20 -> 20, of which waited for: 11 -> 11; matrix products, arithmetic and copies ran while one was open for 0% -> 0% of each run, Pallas kernels for 15% -> 10%
where the time goes in v4:
time: 56.8 us; the launch traced here: 56.6 us
  starting transfers between devices  28.6 us (50%)
  waiting for transfers between devices  17 us (30%)
  Pallas kernels  9.63 us (17%)
  between operations  0.74 us (1%)
  local copies, waits for them, and re-layouts  0.66 us (1%)
    ppermute x20, starting transfers between devices, move(): return lax.ppermute(x, axis, pairs)  28.6 us
    ppermute x20, waiting for transfers between devices, move(): return lax.ppermute(x, axis, pairs)  17 us
    pallas_call x10, Pallas kernels, call(): pl.pallas_call(kernel, out_shape=out_shape, in_specs=[SM] * smem + [HB] *...  9.63 us
  transfers between devices with their start and end apart: 20, of which 11 were waited for; matrix products, arithmetic and copies ran while one was open for 0% of the time, Pallas kernels for 10%

profile of v4, /device:TPU:0, one launch (start us, length us, event | category | flops | bytes accessed | tf_op | source)
XLA Modules:
  0.0 56.6 jit_solution(7564683750433197370)
XLA Ops:
  0.6 1.3 %shard_map.127 = (bf16[128,256]{1,0:T(8,128)(2,1)S(1)}, bf16[128,256]{1,0:T(8,128)(2,1)S(1)}, bf16[31,256]{1,0:T(8,128)(2,1)S(1)}, bf16[48,256]{1,0:T(8,128)(2,1...) custom-call(bf16[128,256]{1,0:T(8,128)(2,1)} %refs_0_.1, ...), custom_call_target="tpu_custom_call" | custom-call | flops 1048576 | bytes 1048576 | tf_op jit(solution)/shard_map/pallas_call | solution.py:27
  1.9 3.1 %collective-permute-start.5 = (bf16[192,128]{1,0:T(8,128)(2,1)S(1)}, bf16[192,128]{1,0:T(8,128)(2,1)S(1)}, u32[]{:S(2)}, u32[]{:S(2)}) collective-permute-start(bf16[192,128]{1,0:T(8,128)(2,1)S(1)} %get-tuple-element.48), channel_id=1, source_target_pairs={{0,4},{4,0},{8,12},{12,8},{16,20},{20,16},{24,28},{28,24},{1,5},{5... | collective-permute-start | bytes 147464 | tf_op jit(solution)/shard_map/ppermute | solution.py:439
  5.0 1.6 %collective-permute-start.6 = (bf16[192,128]{1,0:T(8,128)(2,1)S(1)}, bf16[192,128]{1,0:T(8,128)(2,1)S(1)}, u32[]{:S(2)}, u32[]{:S(2)}) collective-permute-start(bf16[192,128]{1,0:T(8,128)(2,1)S(1)} %get-tuple-element.49), channel_id=1, source_target_pairs={{0,8},{4,12},{8,0},{12,4},{16,24},{20,28},{24,16},{28,20},{1,9},{5... | collective-permute-start | bytes 147464 | tf_op jit(solution)/shard_map/ppermute | solution.py:439
  6.6 3.8 %collective-permute-start = (bf16[48,256]{1,0:T(8,128)(2,1)S(1)}, bf16[48,256]{1,0:T(8,128)(2,1)S(1)}, u32[]{:S(2)}, u32[]{:S(2)}) collective-permute-start(bf16[48,256]{1,0:T(8,128)(2,1)S(1)} %get-tuple-element.40), channel_id=1, source_target_pairs={{0,4},{4,8},{8,12},{12,16},{16,20},{20,24},{24,28},{1,5},{5,9},{9,... | collective-permute-start | bytes 73736 | tf_op jit(solution)/shard_map/ppermute | solution.py:439
  10.4 1.3 %collective-permute-start.1 = (bf16[48,256]{1,0:T(8,128)(2,1)S(1)}, bf16[48,256]{1,0:T(8,128)(2,1)S(1)}, u32[]{:S(2)}, u32[]{:S(2)}) collective-permute-start(bf16[48,256]{1,0:T(8,128)(2,1)S(1)} %get-tuple-element.41), channel_id=1, source_target_pairs={{4,0},{8,4},{12,8},{16,12},{20,16},{24,20},{28,24},{5,1},{9,5},{13... | collective-permute-start | bytes 73736 | tf_op jit(solution)/shard_map/ppermute | solution.py:439
  11.9 4.2 %collective-permute-done.1.high_ref = bf16[48,256]{1,0:T(8,128)(2,1)S(1)} collective-permute-done((bf16[48,256]{1,0:T(8,128)(2,1)S(1)}, bf16[48,256]{1,0:T(8,128)(2,1)S(1)}, u32[]{:S(2)}, u32[]{:S(2)}) %collective-permute-start.1) | collective-permute-done | bytes 24608 | tf_op jit(solution)/shard_map/ppermute | solution.py:439
  16.7 1.9 %shard_map.128 = (bf16[128,256]{1,0:T(8,128)(2,1)}, bf16[128,256]{1,0:T(8,128)(2,1)S(1)}, bf16[128,256]{1,0:T(8,128)(2,1)S(1)}) custom-call(s32[3]{0:T(128)S(1)} %copy-done.1, bf16[128,256]{1,0:T(8,128)(2,1)S(1)} %get-tuple-element.39.x_ref, bf16[128,256]{1,0:T(8,128)(2,1)S(1)} %get-tuple-element.42.g_ref, bf16[48,256]{1,0:T(8,128)(2,1)S(1)} %collective-permute-done.low_ref, ...), custom_call_target="tpu_custom_call" | custom-call | flops 1048576 | bytes 1048576 | tf_op jit(solution)/shard_map/pallas_call | solution.py:27
  18.7 2.7 %collective-permute-start.8 = (bf16[512,128]{1,0:T(8,128)(2,1)S(1)}, bf16[512,128]{1,0:T(8,128)(2,1)S(1)}, u32[]{:S(2)}, u32[]{:S(2)}) collective-permute-start(bf16[512,128]{1,0:T(8,128)(2,1)S(1)} %shard_map.131.rest_4_.rest_8_), channel_id=1, source_target_pairs={{0,16},{4,20},{8,24},{12,28},{16,0},{20,4},{24,8},{28,12},{1,17},{... | collective-permute-start | bytes 393224 | tf_op jit(solution)/shard_map/ppermute | solution.py:439
  21.3 1.5 %collective-permute-start.3 = (bf16[128,256]{1,0:T(8,128)(2,1)S(1)}, bf16[128,256]{1,0:T(8,128)(2,1)S(1)}, u32[]{:S(2)}, u32[]{:S(2)}) collective-permute-start(bf16[128,256]{1,0:T(8,128)(2,1)S(1)} %get-tuple-element.45.rest_0_), channel_id=1, source_target_pairs={{0,2},{1,3},{2,0},{3,1},{4,6},{5,7},{6,4},{7,5},{8,10},{9,11},{10,... | collective-permute-start | bytes 196616 | tf_op jit(solution)/shard_map/ppermute | solution.py:439
  23.2 2.5 %collective-permute-done.4.rest_3_ = bf16[128,256]{1,0:T(8,128)(2,1)S(1)} collective-permute-done((bf16[128,256]{1,0:T(8,128)(2,1)S(1)}, bf16[128,256]{1,0:T(8,128)(2,1)S(1)}, u32[]{:S(2)}, u32[]{:S(2)}) %collective-permute-start.4) | collective-permute-done | bytes 65568 | tf_op jit(solution)/shard_map/ppermute | solution.py:439
  25.7 1.4 %collective-permute-done.3.rest_2_ = bf16[128,256]{1,0:T(8,128)(2,1)S(1)} collective-permute-done((bf16[128,256]{1,0:T(8,128)(2,1)S(1)}, bf16[128,256]{1,0:T(8,128)(2,1)S(1)}, u32[]{:S(2)}, u32[]{:S(2)}) %collective-permute-start.3) | collective-permute-done | bytes 65568 | tf_op jit(solution)/shard_map/ppermute | solution.py:439
  27.5 2.5 %collective-permute-start.9 = (bf16[320,128]{1,0:T(8,128)(2,1)S(1)}, bf16[320,128]{1,0:T(8,128)(2,1)S(1)}, u32[]{:S(2)}, u32[]{:S(2)}) collective-permute-start(bf16[320,128]{1,0:T(8,128)(2,1)S(1)} %get-tuple-element.52), channel_id=1, source_target_pairs={{0,4},{4,0},{8,12},{12,8},{16,20},{20,16},{24,28},{28,24},{1,5},{5... | collective-permute-start | bytes 245768 | tf_op jit(solution)/shard_map/ppermute | solution.py:439
  30.0 1.5 %collective-permute-start.11 = (bf16[320,128]{1,0:T(8,128)(2,1)S(1)}, bf16[320,128]{1,0:T(8,128)(2,1)S(1)}, u32[]{:S(2)}, u32[]{:S(2)}) collective-permute-start(bf16[320,128]{1,0:T(8,128)(2,1)S(1)} %get-tuple-element.54), channel_id=1, source_target_pairs={{0,12},{4,8},{8,4},{12,0},{16,28},{20,24},{24,20},{28,16},{1,13},{... | collective-permute-start | bytes 245768 | tf_op jit(solution)/shard_map/ppermute | solution.py:439
  32.4 2.2 %shard_map.132 = (bf16[2,512,512]{2,1,0:T(8,128)(2,1)S(1)}, bf16[320,128]{1,0:T(8,128)(2,1)S(1)}) custom-call(s32[3]{0:T(128)S(1)} %copy-done.2, bf16[64,128]{1,0:T(8,128)(2,1)S(1)} %shard_map.130.tap_ref, bf16[192,128]{1,0:T(8,128)(2,1)S(1)} %get-tuple-element.47.refs_0_.rest_0_, bf16[192,128]{1,0:T(8,128)(2,1)S(1)} %collective-permute-done.5.refs_1_.rest_1_, ...), custom_call_target="tpu_custom_call" | custom-call | flops 268435456 | bytes 1048576 | tf_op jit(solution)/shard_map/pallas_call | solution.py:27
  35.7 1.6 %shard_map.133 = (bf16[512,128]{1,0:T(8,128)(2,1)S(1)}, bf16[512,128]{1,0:T(8,128)(2,1)S(1)}, bf16[256,128]{1,0:T(8,128)(2,1)S(1)}) custom-call(bf16[2,512,512]{2,1,0:T(8,128)(2,1)S(1)} %get-tuple-element.51.p_ref, bf16[192,128]{1,0:T(8,128)(2,1)S(1)} %get-tuple-element.47.refs_0_.rest_0_, bf16[192,128]{1,0:T(8,128)(2,1)S(1)} %collective-permute-done.5.refs_1_.rest_1_, ...), custom_call_target="tpu_custom_call" | custom-call | flops 536870912 | bytes 1048576 | tf_op jit(solution)/shard_map/pallas_call | solution.py:27
  37.3 1.6 %collective-permute-start.12 = (bf16[512,128]{1,0:T(8,128)(2,1)S(1)}, bf16[512,128]{1,0:T(8,128)(2,1)S(1)}, u32[]{:S(2)}, u32[]{:S(2)}) collective-permute-start(bf16[512,128]{1,0:T(8,128)(2,1)S(1)} %get-tuple-element.56), channel_id=1, source_target_pairs={{0,16},{4,20},{8,24},{12,28},{16,0},{20,4},{24,8},{28,12},{1,17},{... | collective-permute-start | bytes 393224 | tf_op jit(solution)/shard_map/ppermute | solution.py:439
  38.9 1.5 %collective-permute-start.18 = (bf16[320,128]{1,0:T(8,128)(2,1)S(1)}, bf16[320,128]{1,0:T(8,128)(2,1)S(1)}, u32[]{:S(2)}, u32[]{:S(2)}) collective-permute-start(bf16[320,128]{1,0:T(8,128)(2,1)S(1)} %get-tuple-element.62.refs_4_), channel_id=1, source_target_pairs={{0,12},{4,8},{8,4},{12,0},{16,28},{20,24},{24,20},{28,16},{1,13},{... | collective-permute-start | bytes 245768 | tf_op jit(solution)/shard_map/ppermute | solution.py:439
  41.0 1.4 %collective-permute-start.16 = (bf16[320,128]{1,0:T(8,128)(2,1)S(1)}, bf16[320,128]{1,0:T(8,128)(2,1)S(1)}, u32[]{:S(2)}, u32[]{:S(2)}) collective-permute-start(bf16[320,128]{1,0:T(8,128)(2,1)S(1)} %get-tuple-element.62.refs_4_), channel_id=1, source_target_pairs={{0,4},{4,0},{8,12},{12,8},{16,20},{20,16},{24,28},{28,24},{1,5},{5... | collective-permute-start | bytes 245768 | tf_op jit(solution)/shard_map/ppermute | solution.py:439
  42.4 2.7 %collective-permute-done.18.refs_7_ = bf16[320,128]{1,0:T(8,128)(2,1)S(1)} collective-permute-done((bf16[320,128]{1,0:T(8,128)(2,1)S(1)}, bf16[320,128]{1,0:T(8,128)(2,1)S(1)}, u32[]{:S(2)}, u32[]{:S(2)}) %collective-permute-start.18) | collective-permute-done | bytes 81952 | tf_op jit(solution)/shard_map/ppermute | solution.py:439
  45.1 1.4 %collective-permute-done.17.refs_6_ = bf16[320,128]{1,0:T(8,128)(2,1)S(1)} collective-permute-done((bf16[320,128]{1,0:T(8,128)(2,1)S(1)}, bf16[320,128]{1,0:T(8,128)(2,1)S(1)}, u32[]{:S(2)}, u32[]{:S(2)}) %collective-permute-start.17) | collective-permute-done | bytes 81952 | tf_op jit(solution)/shard_map/ppermute | solution.py:439
  47.0 1.6 %collective-permute-start.19 = (bf16[320,128]{1,0:T(8,128)(2,1)S(1)}, bf16[320,128]{1,0:T(8,128)(2,1)S(1)}, u32[]{:S(2)}, u32[]{:S(2)}) collective-permute-start(bf16[320,128]{1,0:T(8,128)(2,1)S(1)} %get-tuple-element.65), channel_id=1, source_target_pairs={{0,16},{4,20},{8,24},{12,28},{16,0},{20,4},{24,8},{28,12},{1,17},{... | collective-permute-start | bytes 245768 | tf_op jit(solution)/shard_map/ppermute | solution.py:439
  49.4 1.3 %collective-permute-start.14 = (bf16[192,128]{1,0:T(8,128)(2,1)S(1)}, bf16[192,128]{1,0:T(8,128)(2,1)S(1)}, u32[]{:S(2)}, u32[]{:S(2)}) collective-permute-start(bf16[192,128]{1,0:T(8,128)(2,1)S(1)} %get-tuple-element.60), channel_id=1, source_target_pairs={{0,8},{4,12},{8,0},{12,4},{16,24},{20,28},{24,16},{28,20},{1,9},{5... | collective-permute-start | bytes 147464 | tf_op jit(solution)/shard_map/ppermute | solution.py:439
  50.8 1.5 %collective-permute-start.15 = (bf16[192,128]{1,0:T(8,128)(2,1)S(1)}, bf16[192,128]{1,0:T(8,128)(2,1)S(1)}, u32[]{:S(2)}, u32[]{:S(2)}) collective-permute-start(bf16[192,128]{1,0:T(8,128)(2,1)S(1)} %get-tuple-element.61), channel_id=1, source_target_pairs={{0,12},{4,8},{8,4},{12,0},{16,28},{20,24},{24,20},{28,16},{1,13},{... | collective-permute-start | bytes 147464 | tf_op jit(solution)/shard_map/ppermute | solution.py:439
  54.1 1.6 %collective-permute-done.15.refs_3_ = bf16[192,128]{1,0:T(8,128)(2,1)S(1)} collective-permute-done((bf16[192,128]{1,0:T(8,128)(2,1)S(1)}, bf16[192,128]{1,0:T(8,128)(2,1)S(1)}, u32[]{:S(2)}, u32[]{:S(2)}) %collective-permute-start.15) | collective-permute-done | bytes 49184 | tf_op jit(solution)/shard_map/ppermute | solution.py:439
  (32 shorter events, 8.2 us)
Async XLA Ops:
  0.6 26.5 %copy-start = (bf16[1024,256]{1,0:T(8,128)(2,1)S(1)}, bf16[1024,256]{1,0:T(8,128)(2,1)}, u32[]{:S(2)}) copy-start(bf16[1024,256]{1,0:T(8,128)(2,1)} %proj_ref.1) | copy-start | bytes 1572868
  1.9 16.7 %collective-permute-start.5 = (bf16[192,128]{1,0:T(8,128)(2,1)S(1)}, bf16[192,128]{1,0:T(8,128)(2,1)S(1)}, u32[]{:S(2)}, u32[]{:S(2)}) collective-permute-start(bf16[192,128]{1,0:T(8,128)(2,1)S(1)} %get-tuple-element.48), channel_id=1, source_target_pairs={{0,4},{4,0},{8,12},{12,8},{16,20},{20,16},{24,28},{28,24},{1,5},{5... | collective-permute-start | bytes 147464 | tf_op jit(solution)/shard_map/ppermute | solution.py:439
  5.0 13.7 %collective-permute-start.6 = (bf16[192,128]{1,0:T(8,128)(2,1)S(1)}, bf16[192,128]{1,0:T(8,128)(2,1)S(1)}, u32[]{:S(2)}, u32[]{:S(2)}) collective-permute-start(bf16[192,128]{1,0:T(8,128)(2,1)S(1)} %get-tuple-element.49), channel_id=1, source_target_pairs={{0,8},{4,12},{8,0},{12,4},{16,24},{20,28},{24,16},{28,20},{1,9},{5... | collective-permute-start | bytes 147464 | tf_op jit(solution)/shard_map/ppermute | solution.py:439
  6.6 12.1 %collective-permute-start.7 = (bf16[192,128]{1,0:T(8,128)(2,1)S(1)}, bf16[192,128]{1,0:T(8,128)(2,1)S(1)}, u32[]{:S(2)}, u32[]{:S(2)}) collective-permute-start(bf16[192,128]{1,0:T(8,128)(2,1)S(1)} %get-tuple-element.50), channel_id=1, source_target_pairs={{0,12},{4,8},{8,4},{12,0},{16,28},{20,24},{24,20},{28,16},{1,13},{... | collective-permute-start | bytes 147464 | tf_op jit(solution)/shard_map/ppermute | solution.py:439
  6.6 5.3 %collective-permute-start = (bf16[48,256]{1,0:T(8,128)(2,1)S(1)}, bf16[48,256]{1,0:T(8,128)(2,1)S(1)}, u32[]{:S(2)}, u32[]{:S(2)}) collective-permute-start(bf16[48,256]{1,0:T(8,128)(2,1)S(1)} %get-tuple-element.40), channel_id=1, source_target_pairs={{0,4},{4,8},{8,12},{12,16},{16,20},{20,24},{24,28},{1,5},{5,9},{9,... | collective-permute-start | bytes 73736 | tf_op jit(solution)/shard_map/ppermute | solution.py:439
  10.4 5.7 %collective-permute-start.1 = (bf16[48,256]{1,0:T(8,128)(2,1)S(1)}, bf16[48,256]{1,0:T(8,128)(2,1)S(1)}, u32[]{:S(2)}, u32[]{:S(2)}) collective-permute-start(bf16[48,256]{1,0:T(8,128)(2,1)S(1)} %get-tuple-element.41), channel_id=1, source_target_pairs={{4,0},{8,4},{12,8},{16,12},{20,16},{24,20},{28,24},{5,1},{9,5},{13... | collective-permute-start | bytes 73736 | tf_op jit(solution)/shard_map/ppermute | solution.py:439
  16.1 0.7 %copy-start.1 = (s32[3]{0:T(128)S(1)}, s32[3]{0:T(128)}, u32[]{:S(2)}) copy-start(s32[3]{0:T(128)} %len_ref.5) | copy-start | bytes 40
  18.7 13.7 %collective-permute-start.8 = (bf16[512,128]{1,0:T(8,128)(2,1)S(1)}, bf16[512,128]{1,0:T(8,128)(2,1)S(1)}, u32[]{:S(2)}, u32[]{:S(2)}) collective-permute-start(bf16[512,128]{1,0:T(8,128)(2,1)S(1)} %shard_map.131.rest_4_.rest_8_), channel_id=1, source_target_pairs={{0,16},{4,20},{8,24},{12,28},{16,0},{20,4},{24,8},{28,12},{1,17},{... | collective-permute-start | bytes 393224 | tf_op jit(solution)/shard_map/ppermute | solution.py:439
  21.3 4.3 %collective-permute-start.4 = (bf16[128,256]{1,0:T(8,128)(2,1)S(1)}, bf16[128,256]{1,0:T(8,128)(2,1)S(1)}, u32[]{:S(2)}, u32[]{:S(2)}) collective-permute-start(bf16[128,256]{1,0:T(8,128)(2,1)S(1)} %get-tuple-element.45.rest_0_), channel_id=1, source_target_pairs={{0,3},{1,2},{2,1},{3,0},{4,7},{5,6},{6,5},{7,4},{8,11},{9,10},{10,... | collective-permute-start | bytes 196616 | tf_op jit(solution)/shard_map/ppermute | solution.py:439
  21.3 5.8 %collective-permute-start.3 = (bf16[128,256]{1,0:T(8,128)(2,1)S(1)}, bf16[128,256]{1,0:T(8,128)(2,1)S(1)}, u32[]{:S(2)}, u32[]{:S(2)}) collective-permute-start(bf16[128,256]{1,0:T(8,128)(2,1)S(1)} %get-tuple-element.45.rest_0_), channel_id=1, source_target_pairs={{0,2},{1,3},{2,0},{3,1},{4,6},{5,7},{6,4},{7,5},{8,10},{9,11},{10,... | collective-permute-start | bytes 196616 | tf_op jit(solution)/shard_map/ppermute | solution.py:439
  22.8 4.3 %collective-permute-start.2 = (bf16[128,256]{1,0:T(8,128)(2,1)S(1)}, bf16[128,256]{1,0:T(8,128)(2,1)S(1)}, u32[]{:S(2)}, u32[]{:S(2)}) collective-permute-start(bf16[128,256]{1,0:T(8,128)(2,1)S(1)} %get-tuple-element.45.rest_0_), channel_id=1, source_target_pairs={{0,1},{1,0},{2,3},{3,2},{4,5},{5,4},{6,7},{7,6},{8,9},{9,8},{10,11... | collective-permute-start | bytes 196616 | tf_op jit(solution)/shard_map/ppermute | solution.py:439
  27.5 7.1 %collective-permute-start.9 = (bf16[320,128]{1,0:T(8,128)(2,1)S(1)}, bf16[320,128]{1,0:T(8,128)(2,1)S(1)}, u32[]{:S(2)}, u32[]{:S(2)}) collective-permute-start(bf16[320,128]{1,0:T(8,128)(2,1)S(1)} %get-tuple-element.52), channel_id=1, source_target_pairs={{0,4},{4,0},{8,12},{12,8},{16,20},{20,16},{24,28},{28,24},{1,5},{5... | collective-permute-start | bytes 245768 | tf_op jit(solution)/shard_map/ppermute | solution.py:439
  29.9 5.0 %collective-permute-start.10 = (bf16[320,128]{1,0:T(8,128)(2,1)S(1)}, bf16[320,128]{1,0:T(8,128)(2,1)S(1)}, u32[]{:S(2)}, u32[]{:S(2)}) collective-permute-start(bf16[320,128]{1,0:T(8,128)(2,1)S(1)} %get-tuple-element.53), channel_id=1, source_target_pairs={{0,8},{4,12},{8,0},{12,4},{16,24},{20,28},{24,16},{28,20},{1,9},{5... | collective-permute-start | bytes 245768 | tf_op jit(solution)/shard_map/ppermute | solution.py:439
  29.9 1.5 %copy-start.2 = (s32[3]{0:T(128)S(1)}, s32[3]{0:T(128)}, u32[]{:S(2)}) copy-start(s32[3]{0:T(128)} %len_ref.5) | copy-start | bytes 40
  30.0 5.7 %collective-permute-start.11 = (bf16[320,128]{1,0:T(8,128)(2,1)S(1)}, bf16[320,128]{1,0:T(8,128)(2,1)S(1)}, u32[]{:S(2)}, u32[]{:S(2)}) collective-permute-start(bf16[320,128]{1,0:T(8,128)(2,1)S(1)} %get-tuple-element.54), channel_id=1, source_target_pairs={{0,12},{4,8},{8,4},{12,0},{16,28},{20,24},{24,20},{28,16},{1,13},{... | collective-permute-start | bytes 245768 | tf_op jit(solution)/shard_map/ppermute | solution.py:439
  37.3 11.3 %collective-permute-start.12 = (bf16[512,128]{1,0:T(8,128)(2,1)S(1)}, bf16[512,128]{1,0:T(8,128)(2,1)S(1)}, u32[]{:S(2)}, u32[]{:S(2)}) collective-permute-start(bf16[512,128]{1,0:T(8,128)(2,1)S(1)} %get-tuple-element.56), channel_id=1, source_target_pairs={{0,16},{4,20},{8,24},{12,28},{16,0},{20,4},{24,8},{28,12},{1,17},{... | collective-permute-start | bytes 393224 | tf_op jit(solution)/shard_map/ppermute | solution.py:439
  38.9 6.2 %collective-permute-start.18 = (bf16[320,128]{1,0:T(8,128)(2,1)S(1)}, bf16[320,128]{1,0:T(8,128)(2,1)S(1)}, u32[]{:S(2)}, u32[]{:S(2)}) collective-permute-start(bf16[320,128]{1,0:T(8,128)(2,1)S(1)} %get-tuple-element.62.refs_4_), channel_id=1, source_target_pairs={{0,12},{4,8},{8,4},{12,0},{16,28},{20,24},{24,20},{28,16},{1,13},{... | collective-permute-start | bytes 245768 | tf_op jit(solution)/shard_map/ppermute | solution.py:439
  40.4 6.1 %collective-permute-start.17 = (bf16[320,128]{1,0:T(8,128)(2,1)S(1)}, bf16[320,128]{1,0:T(8,128)(2,1)S(1)}, u32[]{:S(2)}, u32[]{:S(2)}) collective-permute-start(bf16[320,128]{1,0:T(8,128)(2,1)S(1)} %get-tuple-element.62.refs_4_), channel_id=1, source_target_pairs={{0,8},{4,12},{8,0},{12,4},{16,24},{20,28},{24,16},{28,20},{1,9},{5... | collective-permute-start | bytes 245768 | tf_op jit(solution)/shard_map/ppermute | solution.py:439
  41.0 5.5 %collective-permute-start.16 = (bf16[320,128]{1,0:T(8,128)(2,1)S(1)}, bf16[320,128]{1,0:T(8,128)(2,1)S(1)}, u32[]{:S(2)}, u32[]{:S(2)}) collective-permute-start(bf16[320,128]{1,0:T(8,128)(2,1)S(1)} %get-tuple-element.62.refs_4_), channel_id=1, source_target_pairs={{0,4},{4,0},{8,12},{12,8},{16,20},{20,16},{24,28},{28,24},{1,5},{5... | collective-permute-start | bytes 245768 | tf_op jit(solution)/shard_map/ppermute | solution.py:439
  47.0 6.1 %collective-permute-start.19 = (bf16[320,128]{1,0:T(8,128)(2,1)S(1)}, bf16[320,128]{1,0:T(8,128)(2,1)S(1)}, u32[]{:S(2)}, u32[]{:S(2)}) collective-permute-start(bf16[320,128]{1,0:T(8,128)(2,1)S(1)} %get-tuple-element.65), channel_id=1, source_target_pairs={{0,16},{4,20},{8,24},{12,28},{16,0},{20,4},{24,8},{28,12},{1,17},{... | collective-permute-start | bytes 245768 | tf_op jit(solution)/shard_map/ppermute | solution.py:439
  48.7 4.4 %collective-permute-start.13 = (bf16[192,128]{1,0:T(8,128)(2,1)S(1)}, bf16[192,128]{1,0:T(8,128)(2,1)S(1)}, u32[]{:S(2)}, u32[]{:S(2)}) collective-permute-start(bf16[192,128]{1,0:T(8,128)(2,1)S(1)} %get-tuple-element.59), channel_id=1, source_target_pairs={{0,4},{4,0},{8,12},{12,8},{16,20},{20,16},{24,28},{28,24},{1,5},{5... | collective-permute-start | bytes 147464 | tf_op jit(solution)/shard_map/ppermute | solution.py:439
  49.4 4.7 %collective-permute-start.14 = (bf16[192,128]{1,0:T(8,128)(2,1)S(1)}, bf16[192,128]{1,0:T(8,128)(2,1)S(1)}, u32[]{:S(2)}, u32[]{:S(2)}) collective-permute-start(bf16[192,128]{1,0:T(8,128)(2,1)S(1)} %get-tuple-element.60), channel_id=1, source_target_pairs={{0,8},{4,12},{8,0},{12,4},{16,24},{20,28},{24,16},{28,20},{1,9},{5... | collective-permute-start | bytes 147464 | tf_op jit(solution)/shard_map/ppermute | solution.py:439
  50.8 5.0 %collective-permute-start.15 = (bf16[192,128]{1,0:T(8,128)(2,1)S(1)}, bf16[192,128]{1,0:T(8,128)(2,1)S(1)}, u32[]{:S(2)}, u32[]{:S(2)}) collective-permute-start(bf16[192,128]{1,0:T(8,128)(2,1)S(1)} %get-tuple-element.61), channel_id=1, source_target_pairs={{0,12},{4,8},{8,4},{12,0},{16,28},{20,24},{24,20},{28,16},{1,13},{... | collective-permute-start | bytes 147464 | tf_op jit(solution)/shard_map/ppermute | solution.py:439

commit v5 on v4

v5 whole, which is shorter than its diff:
```python
import functools

import jax
import jax.numpy as jnp
from jax import lax
from jax.experimental import pallas as pl
from jax.experimental.pallas import tpu as pltpu
from jax.sharding import PartitionSpec as P


HEAD_DIM = 64
HALO_X = 32
HALO_G = 16
BF = jnp.bfloat16
F32 = jnp.float32
VM = pl.BlockSpec(memory_space=pltpu.VMEM)
HB = pl.BlockSpec(memory_space=pltpu.HBM)
SM = pl.BlockSpec(memory_space=pltpu.SMEM)


def dot(a, b, dims):
    return lax.dot_general(a, b, (dims, ((), ())), preferred_element_type=F32)


def call(kernel, out_shape, args, smem=0, hbm=0, scratch=(), flops=1 << 20, limit=None):
    one = not isinstance(out_shape, (tuple, list))
    return pl.pallas_call(
        kernel,
        out_shape=out_shape,
        in_specs=[SM] * smem + [HB] * hbm + [VM] * (len(args) - smem - hbm),
        out_specs=VM if one else tuple(VM for _ in out_shape),
        scratch_shapes=list(scratch),
        compiler_params=pltpu.CompilerParams(vmem_limit_bytes=limit or (4 << 20)),
        cost_estimate=pl.CostEstimate(flops=flops, bytes_accessed=1 << 20, transcendentals=0),
    )(*args)


def shape(dims, dtype):
    return jax.ShapeDtypeStruct(tuple(dims), dtype)


MEMBERS = 4


def member():
    return lax.axis_index("ctx") % MEMBERS


def group_of():
    return lax.axis_index("ctx") // MEMBERS


def start_kernel(*refs):
    q_hbm, k_hbm, v_hbm, x_hbm, g_hbm, w_hbm, len_hbm, *refs = refs
    x_ref, g_ref, w_ref, total_ref, edge_ref, *refs = refs
    slots, (q_ref, k_ref, v_ref, len_ref, buf, sems) = refs[:-6], refs[-6:]
    rows, width = q_ref.shape
    half = rows // 2
    moves = (
        (x_hbm, x_ref),
        (g_hbm, g_ref),
        (k_hbm, k_ref),
        (v_hbm, v_ref),
        (q_hbm, q_ref),
        (w_hbm, w_ref),
        (len_hbm, len_ref),
    )
    copies = [pltpu.make_async_copy(a, b, sems.at[i]) for i, (a, b) in enumerate(moves)]
    for copy in copies:
        copy.start()
    for copy in copies:
        copy.wait()
    total = len_ref[0]
    for i in range(1, len_ref.shape[0]):
        total = total + len_ref[i]
    total_ref[...] = jnp.full(total_ref.shape, total, jnp.int32)
    for m in range(MEMBERS):
        cols = slice(m * HEAD_DIM, (m + 1) * HEAD_DIM)
        buf[m, 0:rows, 0:HEAD_DIM] = k_ref[:, cols]
        buf[m, 0:rows, HEAD_DIM:] = v_ref[:, cols]
        buf[m, rows:, 0:HEAD_DIM] = q_ref[0:half, cols]
        buf[m, rows:, HEAD_DIM:] = q_ref[half:, cols]
    me = member()
    for k in range(MEMBERS):
        slots[k][0 : rows + half] = buf[me ^ k]
    for ref, at, upward in (
        (slots[1], rows + half, me % 2 == 0),
        (slots[3], rows + half, me == 1),
        (edge_ref, 0, me == MEMBERS - 1),
    ):
        for c in range(width // 128):
            cols = slice(c * 128, (c + 1) * 128)
            for first, count, src in ((0, HALO_X, x_ref), (HALO_X, HALO_G, g_ref)):
                last = src[rows - count :, cols].astype(F32)
                chosen = jnp.where(upward, last, src[0:count, cols].astype(F32))
                to = at + c * (HALO_X + HALO_G) + first
                ref[to : to + count] = chosen.astype(BF)


def join_kernel(*refs):
    out_ref = refs[-1]
    rows = out_ref.shape[0] // MEMBERS
    for k, ref in enumerate(refs[:-1]):
        out_ref[k * rows : (k + 1) * rows] = ref[0:rows]


def conv_kernel(
    total_ref,
    x_ref,
    g_ref,
    w_ref,
    one_ref,
    three_ref,
    edge_ref,
    out_ref,
    send_ref,
    mine_ref,
    xs,
    gs,
):
    rows = x_ref.shape[0]
    taps = w_ref.shape[0]
    half = taps // 2
    wide = rows + 2 * HALO_G
    shift = HALO_X - HALO_G - half
    size = edge_ref.shape[0]
    start = one_ref.shape[0] - size
    me = member()
    one, three, edge = (
        one_ref[start:].astype(F32),
        three_ref[start:].astype(F32),
        edge_ref[...].astype(F32),
    )
    low = jnp.where(me == 0, edge, jnp.where(me == 2, three, one))
    high = jnp.where(me == 3, edge, jnp.where(me == 1, three, one))
    first = lax.axis_index("ctx") * rows
    for c in range(xs.shape[0]):
        cols = slice(c * 128, (c + 1) * 128)
        at = c * (HALO_X + HALO_G)
        xs[c, 0:HALO_X] = low[at : at + HALO_X]
        xs[c, HALO_X : HALO_X + rows] = x_ref[:, cols].astype(F32)
        xs[c, HALO_X + rows :] = high[at : at + HALO_X]
        pos = first - HALO_X + lax.broadcasted_iota(jnp.int32, xs.shape[1:], 0)
        xs[c] = jnp.where(pos < total_ref[0:1], xs[c], 0.0)
        w = w_ref[:, cols].astype(F32)
        acc = jnp.zeros((wide, 128), F32)
        for j in range(taps):
            acc = acc + w[j : j + 1] * xs[c, shift + j : shift + j + wide]
        s = jax.nn.sigmoid(acc)
        slope = s * (1.0 + acc * (1.0 - s))
        gs[c, 0:HALO_G] = low[at + HALO_X : at + HALO_X + HALO_G]
        gs[c, HALO_G : HALO_G + rows] = g_ref[:, cols].astype(F32)
        gs[c, HALO_G + rows :] = high[at + HALO_X : at + HALO_X + HALO_G]
        gs[c] = (gs[c] * slope).astype(BF).astype(F32)
        acc = jnp.zeros((rows, 128), F32)
        for j in range(taps):
            to = HALO_G + half - j
            acc = acc + w[j : j + 1] * gs[c, to : to + rows]
        pos = first + lax.broadcasted_iota(jnp.int32, acc.shape, 0)
        acc = jnp.where(pos < total_ref[0:1], acc, 0.0)
        out = (g_ref[:, cols].astype(F32) + acc).astype(BF)
        out_ref[:, cols] = out
        send_ref[:, cols] = out
        mine_ref[:, cols] = gs[c, HALO_G : HALO_G + rows].astype(BF)


def taps_kernel(taps, xs, mine_ref, after_ref, tap_ref):
    rows = mine_ref.shape[0]
    half = taps // 2
    sides = xs.shape[0]
    tap_rows = tap_ref.shape[0] // sides
    for c in range(sides):
        mine = mine_ref[:, c * 128 : (c + 1) * 128].astype(F32)
        sums = []
        for j in range(taps):
            first = HALO_X - half + j
            sums.append(jnp.sum(mine * xs[c, first : first + rows], axis=0, keepdims=True))
        sums.append(jnp.zeros((tap_rows - taps, 128), F32))
        tap_ref[c * tap_rows : (c + 1) * tap_rows] = jnp.concatenate(sums, 0).astype(BF)


def spread_kernel(pieces, proj_ref, *rest):
    n_heads = len(rest) - MEMBERS - 2
    xs, slots, (full, buf) = rest[:n_heads], rest[n_heads:-2], rest[-2:]
    rows, width = xs[0].shape
    half = rows // 2
    mine = lax.axis_index("head")
    for k in range(n_heads):
        full[mine ^ k] = xs[k][...]
    go = jnp.zeros((rows, proj_ref.shape[1]), F32)
    for b in range(n_heads):
        go = go + dot(full[b], proj_ref[b * width : (b + 1) * width], ((1,), (0,)))
    go = go.astype(BF)
    for m in range(MEMBERS):
        cols = slice(m * HEAD_DIM, (m + 1) * HEAD_DIM)
        buf[m, 0:half, 0:HEAD_DIM] = go[0:half, cols]
        buf[m, 0:half, HEAD_DIM:] = go[half:, cols]
        for i, first in enumerate(pieces[m]):
            buf[m, half + i * rows : half + (i + 1) * rows] = full[first // width][
                :, first % width : first % width + 128
            ]
    me = member()
    for k in range(MEMBERS):
        slots[k][...] = buf[me ^ k]


def widened(x, keep_high):
    x = x.astype(F32)
    turned = pltpu.roll(x, HEAD_DIM, 1)
    lane = lax.broadcasted_iota(jnp.int32, x.shape, 1)
    used = (lane >= HEAD_DIM) if keep_high else (lane < HEAD_DIM)
    first, second = (turned, x) if keep_high else (x, turned)
    return jnp.concatenate([jnp.where(used, first, 0.0), jnp.where(used, second, 0.0)], 0)


def over(count, body):
    if count <= 2:
        for g in range(count):
            body(g)
    else:
        lax.fori_loop(0, count, lambda g, c: (body(g), c)[1], 0)


def key_block(refs, g):
    return refs[0][g] if len(refs) == 1 else refs[g][...]


def queries_of(got_refs, scale):
    rows = got_refs[0].shape[0] * 2 // 3
    q = jnp.concatenate([r[rows : rows + rows // 2, :] for r in got_refs], 0)
    return (widened(q, False) * scale).astype(BF)


def forward_kernel(n_keys, scale, total_ref, tap_ref, *rest):
    got, rest = rest[:MEMBERS], rest[MEMBERS:]
    kv, rest = rest[:n_keys], rest[n_keys:]
    p_ref, slot_ref, s_ref, m_ref, l_ref, acc_ref = rest
    groups, keys, queries = s_ref.shape
    rows = keys // MEMBERS
    total = jnp.concatenate([total_ref[0:1]] * (queries // 128), 1)
    me, group = member(), group_of()
    q = queries_of(got, scale)
    m_ref[...] = jnp.full(m_ref.shape, -1e30, F32)
    l_ref[...] = jnp.zeros(l_ref.shape, F32)
    acc_ref[...] = jnp.zeros(acc_ref.shape, F32)

    def scores(g):
        s = dot(key_block(kv, g), q, ((1,), (1,)))
        from_group = lax.rem(group + g, groups) if n_keys > 1 else g
        for k in range(MEMBERS):
            start = (from_group * MEMBERS + (me ^ k)) * rows
            pos = start + lax.broadcasted_iota(jnp.int32, (rows, queries), 0)
            part = slice(k * rows, (k + 1) * rows)
            s_ref[g, part] = jnp.where(pos < total, s[part], -1e30)
        m_ref[...] = jnp.maximum(m_ref[...], jnp.max(s_ref[g], axis=0, keepdims=True))

    over(groups, scores)

    def weights(g):
        e = jnp.exp(s_ref[g] - m_ref[...])
        s_ref[g] = e
        l_ref[...] += jnp.sum(e, axis=0, keepdims=True)

    over(groups, weights)
    l_ref[...] = 1.0 / l_ref[...]

    def values(g):
        p = (s_ref[g] * l_ref[...]).astype(BF)
        p_ref[g] = p
        acc_ref[...] += dot(key_block(kv, g), p, ((0,), (0,)))

    over(groups, values)
    attn = acc_ref[HEAD_DIM:, :].T.astype(BF)
    half = queries // 2
    slot_ref[0:half, 0:HEAD_DIM] = attn[0:half]
    slot_ref[0:half, HEAD_DIM:] = attn[half:]
    slot_ref[half:] = tap_ref[...]


HALVES = ((1, 3), (0, 2))


def backward_kernel(n_keys, scale, p_ref, *rest):
    got, gos, rest = rest[:MEMBERS], rest[MEMBERS : 2 * MEMBERS], rest[2 * MEMBERS :]
    kv, rest = rest[:n_keys], rest[n_keys:]
    dkv, (dq_ref, s_ref, d_ref, acc_ref) = rest[:-4], rest[-4:]
    groups, keys, queries = s_ref.shape
    q = queries_of(got, scale)
    half = queries // MEMBERS // 2
    go = widened(jnp.concatenate([r[0:half] for r in gos], 0), True).astype(BF)
    d_ref[...] = jnp.zeros(d_ref.shape, F32)
    acc_ref[...] = jnp.zeros(acc_ref.shape, F32)

    def slopes(g):
        s = dot(key_block(kv, g), go, ((1,), (1,)))
        s_ref[g] = s
        d_ref[...] += jnp.sum(s * p_ref[g].astype(F32), axis=0, keepdims=True)

    over(groups, slopes)

    def grads(g):
        p = p_ref[g]
        ds = (p.astype(F32) * (s_ref[g] - d_ref[...])).astype(BF)
        acc_ref[...] += dot(key_block(kv, g), ds, ((0,), (0,)))
        out = (dot(ds, q, ((1,), (0,))) + dot(p, go, ((1,), (0,)))).astype(BF)
        if len(dkv) == 1:
            dkv[0][g] = out
        elif g == 0:
            dkv[0][...] = out
        else:
            rows = keys // MEMBERS
            for half, ref in zip(HALVES, dkv[1:]):
                for i, k in enumerate(half):
                    ref[i * rows : (i + 1) * rows] = out[k * rows : (k + 1) * rows]

    over(groups, grads)
    dq = (acc_ref[0:HEAD_DIM, :] * scale).T.astype(BF)
    half = queries // 2
    dq_ref[:, 0:HEAD_DIM] = dq[0:half]
    dq_ref[:, HEAD_DIM:] = dq[half:]


def project_kernel(own_rows, *refs):
    gos, slots, outs = refs[:MEMBERS], refs[MEMBERS : 2 * MEMBERS], refs[2 * MEMBERS : -3]
    out_ref, tap_ref = outs[:2]
    lhs, rhs, heads = refs[-3:]
    members = MEMBERS
    count, width = lhs.shape[1], rhs.shape[1]
    half = lhs.shape[0] // members
    rows = 2 * half
    me = member()
    acc = jnp.zeros((count, width), F32)
    tap = jnp.zeros(tap_ref.shape, F32)
    for k in range(members):
        heads[me ^ k] = slots[k][0 : members * half]
        tap = tap + slots[k][members * half :].astype(F32)
    tap_ref[...] = tap.astype(BF)
    for fold in range(2):
        for k in range(members):
            for side in range(count // 128):
                at = half + side * rows + fold * half
                where = pl.multiple_of((me ^ k) * half, half)
                lhs[pl.ds(where, half), side * 128 : (side + 1) * 128] = gos[k][at : at + half]
        for h in range(members):
            for i in range(members):
                j = h ^ i
                rhs[i * half : (i + 1) * half, h * HEAD_DIM : (h + 1) * HEAD_DIM] = heads[
                    h, j * half : (j + 1) * half, fold * HEAD_DIM : (fold + 1) * HEAD_DIM
                ]
        acc = acc + dot(lhs[...], rhs[...], ((0,), (0,)))
    if len(outs) == 2:
        out_ref[...] = acc
        return
    send_ref = outs[2]
    first = group_of() == 0
    low, high = acc[:own_rows], acc[own_rows:]
    out_ref[...] = jnp.where(first, low, high)
    theirs = jnp.where(first, high, low).astype(BF)
    for side in range(width // 128):
        send_ref[side * own_rows : (side + 1) * own_rows] = theirs[:, side * 128 : (side + 1) * 128]
    send_ref[width // 128 * own_rows :] = tap.astype(BF)


def collect_kernel(blocks, own_ref, *refs):
    slots, refs = refs[-len(blocks) :], refs[: -len(blocks)]
    dq_ref = refs[-1]
    rows = slots[0].shape[0] * 2 // 3
    half = rows // 2
    for i, (k, slot) in enumerate(zip(blocks, slots)):
        total = own_ref[k * rows : (k + 1) * rows]
        if len(refs) == 2:
            theirs = refs[0][i * rows : (i + 1) * rows].astype(F32)
            total = (total.astype(F32) + theirs).astype(BF)
        slot[0:rows] = total
        slot[rows:] = dq_ref[k * half : (k + 1) * half]


def end_kernel(*refs):
    n = MEMBERS
    finish_kernel(*refs[n : n + 3], *refs[-3:-1])
    unpack_kernel(*refs[:n], *refs[n + 3 : n + 6], refs[-1])


def unpack_kernel(*refs):
    slots, (q_ref, k_ref, v_ref, buf) = refs[:-4], refs[-4:]
    members = MEMBERS
    rows = q_ref.shape[0]
    half = rows // 2
    me = member()
    for k in range(members):
        buf[me ^ k] = slots[k][...]
    for m in range(members):
        cols = slice(m * HEAD_DIM, (m + 1) * HEAD_DIM)
        k_ref[:, cols] = buf[m, 0:rows, 0:HEAD_DIM]
        v_ref[:, cols] = buf[m, 0:rows, HEAD_DIM:]
        q_ref[0:half, cols] = buf[m, rows:, 0:HEAD_DIM]
        q_ref[half:, cols] = buf[m, rows:, HEAD_DIM:]


def finish_kernel(mine_ref, tap_ref, got_ref, out_ref, grad_ref):
    own_rows, width = mine_ref.shape
    taps = grad_ref.shape[0]
    sides = width // 128
    tap_rows = tap_ref.shape[0] // sides
    tap = tap_ref[...].astype(F32) + got_ref[sides * own_rows :].astype(F32)
    for side in range(sides):
        cols = slice(side * 128, (side + 1) * 128)
        out_ref[:, cols] = mine_ref[:, cols] + got_ref[
            side * own_rows : (side + 1) * own_rows
        ].astype(F32)
        grad_ref[:, cols] = tap[side * tap_rows : side * tap_rows + taps]


def on_device(
    query_all, key_all, value_all, cotangent, conv_input, rec_lengths, out_proj, conv_weight
):
    rows, width = query_all.shape
    half = rows // 2
    members = width // HEAD_DIM
    if members != MEMBERS:
        raise ValueError(width)
    n_ctx, n_heads = lax.axis_size("ctx"), lax.axis_size("head")
    groups = n_ctx // members
    channels = out_proj.shape[0]
    own_rows = channels // n_ctx
    scale = HEAD_DIM**-0.5
    taps = conv_weight.shape[0]
    tap_rows = -(-taps // 16) * 16
    sides = width // 128
    keys = members * rows
    queries = members * rows
    pair = groups == 2
    across = [[g * members + m for g in range(groups)] for m in range(members)]
    other = [(i, (i + members) % n_ctx) for i in range(n_ctx)]

    def move(x, pairs, axis="ctx"):
        return lax.ppermute(x, axis, pairs)

    def by_xor(x, k, axis="ctx"):
        return move(x, [(i, i ^ k) for i in range(lax.axis_size(axis))], axis)

    def swap(slots):
        return [slots[0]] + [by_xor(slots[k], k) for k in range(1, members)]

    edge_rows = sides * (HALO_X + HALO_G)
    given = (query_all, key_all, value_all, conv_input, cotangent, conv_weight, rec_lengths)
    x_in, g_in, w_in, total, edge, *slots = call(
        start_kernel,
        (
            shape((rows, width), BF),
            shape((rows, width), BF),
            shape(conv_weight.shape, BF),
            shape((8, 128), jnp.int32),
            shape((edge_rows, 128), BF),
        )
        + tuple(shape((rows + half + k % 2 * edge_rows, 128), BF) for k in range(members)),
        tuple(pltpu.with_memory_space_constraint(x, pltpu.HBM) for x in given),
        hbm=len(given),
        scratch=[pltpu.VMEM((rows, width), BF)] * 3
        + [
            pltpu.SMEM(rec_lengths.shape, jnp.int32),
            pltpu.VMEM((members, rows + half, 128), BF),
            pltpu.SemaphoreType.DMA((len(given),)),
        ],
    )
    got = swap(slots)
    borders = [i for i in range(members, n_ctx, members)]
    edge = move(edge, [(i - 1, i) for i in borders] + [(i, i - 1) for i in borders])
    x_grad, x_send, grad_conv, masked = call(
        conv_kernel,
        (shape((rows, width), BF),) * 3 + (shape((sides, rows + 2 * HALO_X, 128), F32),),
        (total, x_in, g_in, w_in, got[1], got[3], edge),
        scratch=[pltpu.VMEM((sides, rows + 2 * HALO_G, 128), F32)],
    )
    xs = [x_send] + [by_xor(x_send, k, "head") for k in range(1, n_heads)]
    own_kv = call(join_kernel, shape((keys, 128), BF), got)
    if pair:
        kv = (own_kv, move(own_kv, other))
    else:
        kv = (lax.all_gather(own_kv, "ctx", axis_index_groups=across),)
    n_keys = len(kv)
    count = groups * own_rows
    aligned = own_rows % 128 == 0
    pieces = [
        [(g * members + m) * own_rows + b for g in range(groups) for b in range(0, own_rows, 128)]
        if aligned
        else list(range(m * count, (m + 1) * count, 128))
        for m in range(members)
    ]
    slot_rows = half + count // 128 * rows
    spread = call(
        functools.partial(spread_kernel, pieces),
        (shape((slot_rows, 128), BF),) * members,
        (out_proj, *xs),
        scratch=[
            pltpu.VMEM((n_heads, rows, width), BF),
            pltpu.VMEM((members, slot_rows, 128), BF),
        ],
        flops=2 * rows * channels * width,
    )
    gos = swap(spread)
    tap_part = call(
        functools.partial(taps_kernel, taps),
        shape((sides * tap_rows, 128), BF),
        (masked, grad_conv, spread[0]),
    )
    big = (12 << 20) if groups <= 2 else (60 << 20)
    flops = 2 * queries * keys * groups * 128
    fwd = call(
        functools.partial(forward_kernel, n_keys, scale),
        (
            shape((groups, keys, queries), BF),
            shape((queries // 2 + sides * tap_rows, 128), BF),
        ),
        (total, tap_part, *got, *kv),
        scratch=[
            pltpu.VMEM((groups, keys, queries), F32),
            pltpu.VMEM((1, queries), F32),
            pltpu.VMEM((1, queries), F32),
            pltpu.VMEM((128, queries), F32),
        ],
        flops=2 * flops,
        limit=big,
    )
    probs = fwd[0]
    bwd = call(
        functools.partial(backward_kernel, n_keys, scale),
        (
            (shape((keys, 128), BF), shape((keys // 2, 128), BF), shape((keys // 2, 128), BF))
            if pair
            else (shape((groups, keys, 128), BF),)
        )
        + (shape((queries // 2, 128), BF),),
        (probs, *got, *gos, *kv),
        scratch=[
            pltpu.VMEM((groups, keys, queries), F32),
            pltpu.VMEM((1, queries), F32),
            pltpu.VMEM((128, queries), F32),
        ],
        flops=4 * flops,
        limit=big,
    )
    dq = bwd[-1]
    slot = shape((rows + half, 128), BF)
    slots = [None] * members
    if pair:
        for i, blocks in enumerate(HALVES):
            theirs = move(bwd[1 + i], other)
            made = call(
                functools.partial(collect_kernel, blocks),
                (slot,) * len(blocks),
                (bwd[0], theirs, dq),
            )
            for k, one in zip(blocks, made):
                slots[k] = one
    else:
        moved = lax.all_to_all(bwd[0], "ctx", 0, 0, axis_index_groups=across)
        summed = jnp.sum(moved.astype(F32), 0).astype(BF)
        slots = call(
            functools.partial(collect_kernel, tuple(range(members))), (slot,) * members, (summed, dq)
        )
    back = swap(slots)
    shared = swap([fwd[1]] * members)
    merged = pair and own_rows % 16 == 0
    tap_shape = shape((sides * tap_rows, 128), BF)
    outs = (
        (shape((own_rows, width), F32), tap_shape, shape((sides * (own_rows + tap_rows), 128), BF))
        if merged
        else (shape((count, width), F32), tap_shape)
    )
    partial, tap_sum, *send = call(
        functools.partial(project_kernel, own_rows),
        outs,
        (*gos, *shared),
        scratch=[
            pltpu.VMEM((members * half, count), BF),
            pltpu.VMEM((members * half, width), BF),
            pltpu.VMEM((members, queries // 2, 128), BF),
        ],
        flops=2 * count * width * queries,
    )
    grads = (shape((rows, width), BF),) * 3
    buf = [pltpu.VMEM((members, rows + half, 128), BF)]
    if merged:
        q_grad, k_grad, v_grad, out_proj_grad, conv_weight_grad = call(
            end_kernel,
            grads + (shape((own_rows, width), F32), shape((taps, width), F32)),
            (*back, partial, tap_sum, move(send[0], other)),
            scratch=buf,
        )
    else:
        q_grad, k_grad, v_grad = call(unpack_kernel, grads, tuple(back), scratch=buf)
        if not aligned:
            wanted = partial.astype(BF).reshape(1, groups, own_rows, width)
            slots = jnp.zeros((members, groups, own_rows, width), BF)
            slots = lax.dynamic_update_slice(
                slots, wanted, (member(), 0, 0, 0)
            )
            moved = lax.all_to_all(slots.reshape(n_ctx, own_rows, width), "ctx", 0, 0)
        else:
            moved = lax.all_to_all(
                partial.astype(BF).reshape(groups, own_rows, width),
                "ctx",
                0,
                0,
                axis_index_groups=across,
            )
        out_proj_grad = jnp.sum(moved.astype(F32), 0)
        tap_all = jnp.sum(
            lax.all_gather(tap_sum, "ctx", axis_index_groups=across).astype(F32), 0
        ).reshape(sides, tap_rows, 128)
        conv_weight_grad = jnp.swapaxes(tap_all, 0, 1).reshape(tap_rows, width)[:taps]
    return (q_grad, k_grad, v_grad, x_grad, out_proj_grad, conv_weight_grad)


def solution(mesh):
    placed = (
        P("ctx", "head"),
        P("ctx", "head"),
        P("ctx", "head"),
        P("ctx", "head"),
        P("ctx", "head"),
        P(),
        P(None, "head"),
        P(None, "head"),
    )

    return jax.shard_map(
        on_device,
        mesh=mesh,
        in_specs=placed,
        out_specs=(
            P("ctx", "head"),
            P("ctx", "head"),
            P("ctx", "head"),
            P("ctx", "head"),
            P("ctx", "head"),
            P(None, "head"),
        ),
        check_vma=False,
    )
```

time: 56.8 us -> 50.2 us (0.88)
  starting transfers between devices: 28.6 us -> 24.2 us
  Pallas kernels: 9.63 us -> 7.91 us
  local copies, waits for them, and re-layouts: 0.66 us -> 0.01 us
    ppermute x20, starting transfers between devices: 28.6 us -> 24.2 us  [move(): return lax.ppermute(x, axis, pairs)]
    pallas_call x10 -> x11, Pallas kernels: 9.63 us -> 7.91 us  [call(): pl.pallas_call(kernel, out_shape=out_shape, in_specs=[SM] * smem + [HB] *...]
    unnamed x6 -> x2, local copies, waits for them, and re-layouts: 0.66 us -> 0.01 us
  transfers between devices with their start and end apart: 20 -> 20, of which waited for: 11 -> 9; matrix products, arithmetic and copies ran while one was open for 0% -> 0% of each run, Pallas kernels for 10% -> 12%
where the time goes in v5:
time: 50.2 us; the launch traced here: 50.1 us
  starting transfers between devices  24.2 us (48%)
  waiting for transfers between devices  17.2 us (34%)
  Pallas kernels  7.91 us (16%)
  between operations  0.72 us (1%)
    ppermute x20, starting transfers between devices, move(): return lax.ppermute(x, axis, pairs)  24.2 us
    ppermute x20, waiting for transfers between devices, move(): return lax.ppermute(x, axis, pairs)  17.2 us
    pallas_call x11, Pallas kernels, call(): pl.pallas_call(kernel, out_shape=out_shape, in_specs=[SM] * smem + [HB] *...  7.91 us
  transfers between devices with their start and end apart: 20, of which 9 were waited for; matrix products, arithmetic and copies ran while one was open for 0% of the time, Pallas kernels for 12%

profile of v5, /device:TPU:0, one launch (start us, length us, event | category | flops | bytes accessed | tf_op | source)
XLA Modules:
  0.0 50.1 jit_solution(11158321283263821398)
XLA Ops:
  0.6 1.3 %shard_map.127 = (bf16[128,256]{1,0:T(8,128)(2,1)S(1)}, bf16[128,256]{1,0:T(8,128)(2,1)S(1)}, bf16[31,256]{1,0:T(8,128)(2,1)S(1)}, s32[8,128]{1,0:T(8,128)S(1)},...) custom-call(bf16[128,256]{1,0:T(8,128)(2,1)} %refs_0_.1, ...), custom_call_target="tpu_custom_call" | custom-call | flops 1048576 | bytes 1048576 | tf_op jit(solution)/shard_map/pallas_call | solution.py:27
  1.9 3.1 %collective-permute-start = (bf16[288,128]{1,0:T(8,128)(2,1)S(1)}, bf16[288,128]{1,0:T(8,128)(2,1)S(1)}, u32[]{:S(2)}, u32[]{:S(2)}) collective-permute-start(bf16[288,128]{1,0:T(8,128)(2,1)S(1)} %get-tuple-element.45), channel_id=1, source_target_pairs={{0,4},{4,0},{8,12},{12,8},{16,20},{20,16},{24,28},{28,24},{1,5},{5... | collective-permute-start | bytes 221192 | tf_op jit(solution)/shard_map/ppermute | solution.py:437
  5.0 1.5 %collective-permute-start.1 = (bf16[288,128]{1,0:T(8,128)(2,1)S(1)}, bf16[288,128]{1,0:T(8,128)(2,1)S(1)}, u32[]{:S(2)}, u32[]{:S(2)}) collective-permute-start(bf16[288,128]{1,0:T(8,128)(2,1)S(1)} %get-tuple-element.46), channel_id=1, source_target_pairs={{0,12},{4,8},{8,4},{12,0},{16,28},{20,24},{24,20},{28,16},{1,13},{... | collective-permute-start | bytes 221192 | tf_op jit(solution)/shard_map/ppermute | solution.py:437
  7.2 3.4 %collective-permute-done.6.refs_2_.rest_2_ = bf16[192,128]{1,0:T(8,128)(2,1)S(1)} collective-permute-done((bf16[192,128]{1,0:T(8,128)(2,1)S(1)}, bf16[192,128]{1,0:T(8,128)(2,1)S(1)}, u32[]{:S(2)}, u32[]{:S(2)}) %collective-permute-start.6) | collective-permute-done | bytes 49184 | tf_op jit(solution)/shard_map/ppermute | solution.py:437
  10.7 2.7 %collective-permute-start.7 = (bf16[512,128]{1,0:T(8,128)(2,1)S(1)}, bf16[512,128]{1,0:T(8,128)(2,1)S(1)}, u32[]{:S(2)}, u32[]{:S(2)}) collective-permute-start(bf16[512,128]{1,0:T(8,128)(2,1)S(1)} %shard_map.131.rest_4_.rest_8_), channel_id=1, source_target_pairs={{0,16},{4,20},{8,24},{12,28},{16,0},{20,4},{24,8},{28,12},{1,17},{... | collective-permute-start | bytes 393224 | tf_op jit(solution)/shard_map/ppermute | solution.py:437
  13.3 1.4 %shard_map.128 = (bf16[128,256]{1,0:T(8,128)(2,1)}, bf16[128,256]{1,0:T(8,128)(2,1)S(1)}, bf16[128,256]{1,0:T(8,128)(2,1)S(1)}, f32[2,192,128]{2,1,0:T(8,128)S(1)}) custom-call(s32[8,128]{1,0:T(8,128)S(1)} %get-tuple-element.41.total_ref, bf16[128,256]{1,0:T(8,128)(2,1)S(1)} %get-tuple-element.42.x_ref, bf16[128,256]{1,0:T(8,128)(2,1)S(1)} %get-tuple-element.43.g_ref, ...), custom_call_target="tpu_custom_call" | custom-call | flops 1048576 | bytes 1048576 | tf_op jit(solution)/shard_map/pallas_call | solution.py:27
  14.8 1.5 %collective-permute-start.4 = (bf16[128,256]{1,0:T(8,128)(2,1)S(1)}, bf16[128,256]{1,0:T(8,128)(2,1)S(1)}, u32[]{:S(2)}, u32[]{:S(2)}) collective-permute-start(bf16[128,256]{1,0:T(8,128)(2,1)S(1)} %get-tuple-element.50.rest_0_), channel_id=1, source_target_pairs={{0,2},{1,3},{2,0},{3,1},{4,6},{5,7},{6,4},{7,5},{8,10},{9,11},{10,... | collective-permute-start | bytes 196616 | tf_op jit(solution)/shard_map/ppermute | solution.py:437
  16.6 2.5 %collective-permute-done.5.rest_3_ = bf16[128,256]{1,0:T(8,128)(2,1)S(1)} collective-permute-done((bf16[128,256]{1,0:T(8,128)(2,1)S(1)}, bf16[128,256]{1,0:T(8,128)(2,1)S(1)}, u32[]{:S(2)}, u32[]{:S(2)}) %collective-permute-start.5) | collective-permute-done | bytes 65568 | tf_op jit(solution)/shard_map/ppermute | solution.py:437
  19.1 1.4 %collective-permute-done.4.rest_2_ = bf16[128,256]{1,0:T(8,128)(2,1)S(1)} collective-permute-done((bf16[128,256]{1,0:T(8,128)(2,1)S(1)}, bf16[128,256]{1,0:T(8,128)(2,1)S(1)}, u32[]{:S(2)}, u32[]{:S(2)}) %collective-permute-start.4) | collective-permute-done | bytes 65568 | tf_op jit(solution)/shard_map/ppermute | solution.py:437
  20.9 1.5 %collective-permute-start.8 = (bf16[320,128]{1,0:T(8,128)(2,1)S(1)}, bf16[320,128]{1,0:T(8,128)(2,1)S(1)}, u32[]{:S(2)}, u32[]{:S(2)}) collective-permute-start(bf16[320,128]{1,0:T(8,128)(2,1)S(1)} %get-tuple-element.55), channel_id=1, source_target_pairs={{0,4},{4,0},{8,12},{12,8},{16,20},{20,16},{24,28},{28,24},{1,5},{5... | collective-permute-start | bytes 245768 | tf_op jit(solution)/shard_map/ppermute | solution.py:437
  22.4 2.5 %collective-permute-start.9 = (bf16[320,128]{1,0:T(8,128)(2,1)S(1)}, bf16[320,128]{1,0:T(8,128)(2,1)S(1)}, u32[]{:S(2)}, u32[]{:S(2)}) collective-permute-start(bf16[320,128]{1,0:T(8,128)(2,1)S(1)} %get-tuple-element.56), channel_id=1, source_target_pairs={{0,8},{4,12},{8,0},{12,4},{16,24},{20,28},{24,16},{28,20},{1,9},{5... | collective-permute-start | bytes 245768 | tf_op jit(solution)/shard_map/ppermute | solution.py:437
  25.3 1.5 %shard_map.132 = (bf16[2,512,512]{2,1,0:T(8,128)(2,1)S(1)}, bf16[320,128]{1,0:T(8,128)(2,1)S(1)}) custom-call(s32[8,128]{1,0:T(8,128)S(1)} %get-tuple-element.41.total_ref, bf16[64,128]{1,0:T(8,128)(2,1)S(1)} %shard_map.130.tap_ref, bf16[192,128]{1,0:T(8,128)(2,1)S(1)} %get-tuple-element.52.refs_0_.rest_0_, ...), custom_call_target="tpu_custom_call" | custom-call | flops 268435456 | bytes 1048576 | tf_op jit(solution)/shard_map/pallas_call | solution.py:27
  26.7 3.0 %collective-permute-start.18 = (bf16[320,128]{1,0:T(8,128)(2,1)S(1)}, bf16[320,128]{1,0:T(8,128)(2,1)S(1)}, u32[]{:S(2)}, u32[]{:S(2)}) collective-permute-start(bf16[320,128]{1,0:T(8,128)(2,1)S(1)} %get-tuple-element.66.refs_4_), channel_id=1, source_target_pairs={{0,12},{4,8},{8,4},{12,0},{16,28},{20,24},{24,20},{28,16},{1,13},{... | collective-permute-start | bytes 245768 | tf_op jit(solution)/shard_map/ppermute | solution.py:437
  30.7 1.6 %shard_map.133 = (bf16[512,128]{1,0:T(8,128)(2,1)S(1)}, bf16[256,128]{1,0:T(8,128)(2,1)S(1)}, bf16[256,128]{1,0:T(8,128)(2,1)S(1)}, bf16[256,128]{1,0:T(8,128)(2,1)S(1)}) custom-call(bf16[2,512,512]{2,1,0:T(8,128)(2,1)S(1)} %get-tuple-element.54.p_ref, bf16[192,128]{1,0:T(8,128)(2,1)S(1)} %get-tuple-element.52.refs_0_.rest_0_, ...), custom_call_target="tpu_custom_call" | custom-call | flops 536870912 | bytes 1048576 | tf_op jit(solution)/shard_map/pallas_call | solution.py:27
  32.4 2.3 %collective-permute-start.11 = (bf16[256,128]{1,0:T(8,128)(2,1)S(1)}, bf16[256,128]{1,0:T(8,128)(2,1)S(1)}, u32[]{:S(2)}, u32[]{:S(2)}) collective-permute-start(bf16[256,128]{1,0:T(8,128)(2,1)S(1)} %get-tuple-element.59), channel_id=1, source_target_pairs={{0,16},{4,20},{8,24},{12,28},{16,0},{20,4},{24,8},{28,12},{1,17},{... | collective-permute-start | bytes 196616 | tf_op jit(solution)/shard_map/ppermute | solution.py:437
  34.6 0.7 %collective-permute-start.12 = (bf16[256,128]{1,0:T(8,128)(2,1)S(1)}, bf16[256,128]{1,0:T(8,128)(2,1)S(1)}, u32[]{:S(2)}, u32[]{:S(2)}) collective-permute-start(bf16[256,128]{1,0:T(8,128)(2,1)S(1)} %get-tuple-element.62), channel_id=1, source_target_pairs={{0,16},{4,20},{8,24},{12,28},{16,0},{20,4},{24,8},{28,12},{1,17},{... | collective-permute-start | bytes 196616 | tf_op jit(solution)/shard_map/ppermute | solution.py:437
  35.9 2.3 %collective-permute-start.19 = (bf16[320,128]{1,0:T(8,128)(2,1)S(1)}, bf16[320,128]{1,0:T(8,128)(2,1)S(1)}, u32[]{:S(2)}, u32[]{:S(2)}) collective-permute-start(bf16[320,128]{1,0:T(8,128)(2,1)S(1)} %get-tuple-element.69), channel_id=1, source_target_pairs={{0,16},{4,20},{8,24},{12,28},{16,0},{20,4},{24,8},{28,12},{1,17},{... | collective-permute-start | bytes 245768 | tf_op jit(solution)/shard_map/ppermute | solution.py:437
  38.2 2.4 %collective-permute-done.11.refs_0_ = bf16[256,128]{1,0:T(8,128)(2,1)S(1)} collective-permute-done((bf16[256,128]{1,0:T(8,128)(2,1)S(1)}, bf16[256,128]{1,0:T(8,128)(2,1)S(1)}, u32[]{:S(2)}, u32[]{:S(2)}) %collective-permute-start.11) | collective-permute-done | bytes 65568 | tf_op jit(solution)/shard_map/ppermute | solution.py:437
  40.7 2.1 %collective-permute-done.12.refs_0_ = bf16[256,128]{1,0:T(8,128)(2,1)S(1)} collective-permute-done((bf16[256,128]{1,0:T(8,128)(2,1)S(1)}, bf16[256,128]{1,0:T(8,128)(2,1)S(1)}, u32[]{:S(2)}, u32[]{:S(2)}) %collective-permute-start.12) | collective-permute-done | bytes 65568 | tf_op jit(solution)/shard_map/ppermute | solution.py:437
  42.8 1.4 %collective-permute-start.13 = (bf16[192,128]{1,0:T(8,128)(2,1)S(1)}, bf16[192,128]{1,0:T(8,128)(2,1)S(1)}, u32[]{:S(2)}, u32[]{:S(2)}) collective-permute-start(bf16[192,128]{1,0:T(8,128)(2,1)S(1)} %get-tuple-element.63), channel_id=1, source_target_pairs={{0,4},{4,0},{8,12},{12,8},{16,20},{20,16},{24,28},{28,24},{1,5},{5... | collective-permute-start | bytes 147464 | tf_op jit(solution)/shard_map/ppermute | solution.py:437
  44.2 0.9 %collective-permute-done.14.refs_2_ = bf16[192,128]{1,0:T(8,128)(2,1)S(1)} collective-permute-done((bf16[192,128]{1,0:T(8,128)(2,1)S(1)}, bf16[192,128]{1,0:T(8,128)(2,1)S(1)}, u32[]{:S(2)}, u32[]{:S(2)}) %collective-permute-start.14) | collective-permute-done | bytes 49184 | tf_op jit(solution)/shard_map/ppermute | solution.py:437
  45.1 1.8 %collective-permute-done.13.refs_1_ = bf16[192,128]{1,0:T(8,128)(2,1)S(1)} collective-permute-done((bf16[192,128]{1,0:T(8,128)(2,1)S(1)}, bf16[192,128]{1,0:T(8,128)(2,1)S(1)}, u32[]{:S(2)}, u32[]{:S(2)}) %collective-permute-start.13) | collective-permute-done | bytes 49184 | tf_op jit(solution)/shard_map/ppermute | solution.py:437
  47.0 2.2 %collective-permute-done.15.refs_3_ = bf16[192,128]{1,0:T(8,128)(2,1)S(1)} collective-permute-done((bf16[192,128]{1,0:T(8,128)(2,1)S(1)}, bf16[192,128]{1,0:T(8,128)(2,1)S(1)}, u32[]{:S(2)}, u32[]{:S(2)}) %collective-permute-start.15) | collective-permute-done | bytes 49184 | tf_op jit(solution)/shard_map/ppermute | solution.py:437
  49.2 0.9 %shard_map.137 = (bf16[128,256]{1,0:T(8,128)(2,1)}, bf16[128,256]{1,0:T(8,128)(2,1)}, bf16[128,256]{1,0:T(8,128)(2,1)}, f32[128,256]{1,0:T(8,128)}, f32[31,256]{1,0:T(8,128)}) custom-call(bf16[192,128]{1,0:T(8,128)(2,1)S(1)} %get-tuple-element.61.refs_0_, bf16[192,128]{1,0:T(8,128)(2,1)S(1)} %collective-permute-done.13.refs_1_, ...), custom_call_target="tpu_custom_call" | custom-call | flops 1048576 | bytes 1048576 | tf_op jit(solution)/shard_map/pallas_call | solution.py:27
  (29 shorter events, 3.5 us)
Async XLA Ops:
  0.6 19.9 %copy-start = (bf16[1024,256]{1,0:T(8,128)(2,1)S(1)}, bf16[1024,256]{1,0:T(8,128)(2,1)}, u32[]{:S(2)}) copy-start(bf16[1024,256]{1,0:T(8,128)(2,1)} %proj_ref.1) | copy-start | bytes 1572868
  1.9 8.7 %collective-permute-start = (bf16[288,128]{1,0:T(8,128)(2,1)S(1)}, bf16[288,128]{1,0:T(8,128)(2,1)S(1)}, u32[]{:S(2)}, u32[]{:S(2)}) collective-permute-start(bf16[288,128]{1,0:T(8,128)(2,1)S(1)} %get-tuple-element.45), channel_id=1, source_target_pairs={{0,4},{4,0},{8,12},{12,8},{16,20},{20,16},{24,28},{28,24},{1,5},{5... | collective-permute-start | bytes 221192 | tf_op jit(solution)/shard_map/ppermute | solution.py:437
  5.0 5.7 %collective-permute-start.1 = (bf16[288,128]{1,0:T(8,128)(2,1)S(1)}, bf16[288,128]{1,0:T(8,128)(2,1)S(1)}, u32[]{:S(2)}, u32[]{:S(2)}) collective-permute-start(bf16[288,128]{1,0:T(8,128)(2,1)S(1)} %get-tuple-element.46), channel_id=1, source_target_pairs={{0,12},{4,8},{8,4},{12,0},{16,28},{20,24},{24,20},{28,16},{1,13},{... | collective-permute-start | bytes 221192 | tf_op jit(solution)/shard_map/ppermute | solution.py:437
  6.5 4.1 %collective-permute-start.6 = (bf16[192,128]{1,0:T(8,128)(2,1)S(1)}, bf16[192,128]{1,0:T(8,128)(2,1)S(1)}, u32[]{:S(2)}, u32[]{:S(2)}) collective-permute-start(bf16[192,128]{1,0:T(8,128)(2,1)S(1)} %get-tuple-element.53), channel_id=1, source_target_pairs={{0,8},{4,12},{8,0},{12,4},{16,24},{20,28},{24,16},{28,20},{1,9},{5... | collective-permute-start | bytes 147464 | tf_op jit(solution)/shard_map/ppermute | solution.py:437
  6.6 6.8 %collective-permute-start.2 = (bf16[96,128]{1,0:T(8,128)(2,1)S(1)}, bf16[96,128]{1,0:T(8,128)(2,1)S(1)}, u32[]{:S(2)}, u32[]{:S(2)}) collective-permute-start(bf16[96,128]{1,0:T(8,128)(2,1)S(1)} %get-tuple-element.47), channel_id=1, source_target_pairs={{12,16},{16,12},{13,17},{17,13},{14,18},{18,14},{15,19},{19,15}} | collective-permute-start | bytes 73736 | tf_op jit(solution)/shard_map/ppermute | solution.py:437
  10.7 14.6 %collective-permute-start.7 = (bf16[512,128]{1,0:T(8,128)(2,1)S(1)}, bf16[512,128]{1,0:T(8,128)(2,1)S(1)}, u32[]{:S(2)}, u32[]{:S(2)}) collective-permute-start(bf16[512,128]{1,0:T(8,128)(2,1)S(1)} %shard_map.131.rest_4_.rest_8_), channel_id=1, source_target_pairs={{0,16},{4,20},{8,24},{12,28},{16,0},{20,4},{24,8},{28,12},{1,17},{... | collective-permute-start | bytes 393224 | tf_op jit(solution)/shard_map/ppermute | solution.py:437
  14.7 4.3 %collective-permute-start.5 = (bf16[128,256]{1,0:T(8,128)(2,1)S(1)}, bf16[128,256]{1,0:T(8,128)(2,1)S(1)}, u32[]{:S(2)}, u32[]{:S(2)}) collective-permute-start(bf16[128,256]{1,0:T(8,128)(2,1)S(1)} %get-tuple-element.50.rest_0_), channel_id=1, source_target_pairs={{0,3},{1,2},{2,1},{3,0},{4,7},{5,6},{6,5},{7,4},{8,11},{9,10},{10,... | collective-permute-start | bytes 196616 | tf_op jit(solution)/shard_map/ppermute | solution.py:437
  14.8 5.8 %collective-permute-start.4 = (bf16[128,256]{1,0:T(8,128)(2,1)S(1)}, bf16[128,256]{1,0:T(8,128)(2,1)S(1)}, u32[]{:S(2)}, u32[]{:S(2)}) collective-permute-start(bf16[128,256]{1,0:T(8,128)(2,1)S(1)} %get-tuple-element.50.rest_0_), channel_id=1, source_target_pairs={{0,2},{1,3},{2,0},{3,1},{4,6},{5,7},{6,4},{7,5},{8,10},{9,11},{10,... | collective-permute-start | bytes 196616 | tf_op jit(solution)/shard_map/ppermute | solution.py:437
  16.2 4.3 %collective-permute-start.3 = (bf16[128,256]{1,0:T(8,128)(2,1)S(1)}, bf16[128,256]{1,0:T(8,128)(2,1)S(1)}, u32[]{:S(2)}, u32[]{:S(2)}) collective-permute-start(bf16[128,256]{1,0:T(8,128)(2,1)S(1)} %get-tuple-element.50.rest_0_), channel_id=1, source_target_pairs={{0,1},{1,0},{2,3},{3,2},{4,5},{5,4},{6,7},{7,6},{8,9},{9,8},{10,11... | collective-permute-start | bytes 196616 | tf_op jit(solution)/shard_map/ppermute | solution.py:437
  20.9 8.8 %collective-permute-start.8 = (bf16[320,128]{1,0:T(8,128)(2,1)S(1)}, bf16[320,128]{1,0:T(8,128)(2,1)S(1)}, u32[]{:S(2)}, u32[]{:S(2)}) collective-permute-start(bf16[320,128]{1,0:T(8,128)(2,1)S(1)} %get-tuple-element.55), channel_id=1, source_target_pairs={{0,4},{4,0},{8,12},{12,8},{16,20},{20,16},{24,28},{28,24},{1,5},{5... | collective-permute-start | bytes 245768 | tf_op jit(solution)/shard_map/ppermute | solution.py:437
  22.4 7.9 %collective-permute-start.9 = (bf16[320,128]{1,0:T(8,128)(2,1)S(1)}, bf16[320,128]{1,0:T(8,128)(2,1)S(1)}, u32[]{:S(2)}, u32[]{:S(2)}) collective-permute-start(bf16[320,128]{1,0:T(8,128)(2,1)S(1)} %get-tuple-element.56), channel_id=1, source_target_pairs={{0,8},{4,12},{8,0},{12,4},{16,24},{20,28},{24,16},{28,20},{1,9},{5... | collective-permute-start | bytes 245768 | tf_op jit(solution)/shard_map/ppermute | solution.py:437
  24.9 5.8 %collective-permute-start.10 = (bf16[320,128]{1,0:T(8,128)(2,1)S(1)}, bf16[320,128]{1,0:T(8,128)(2,1)S(1)}, u32[]{:S(2)}, u32[]{:S(2)}) collective-permute-start(bf16[320,128]{1,0:T(8,128)(2,1)S(1)} %get-tuple-element.57), channel_id=1, source_target_pairs={{0,12},{4,8},{8,4},{12,0},{16,28},{20,24},{24,20},{28,16},{1,13},{... | collective-permute-start | bytes 245768 | tf_op jit(solution)/shard_map/ppermute | solution.py:437
  26.7 8.6 %collective-permute-start.18 = (bf16[320,128]{1,0:T(8,128)(2,1)S(1)}, bf16[320,128]{1,0:T(8,128)(2,1)S(1)}, u32[]{:S(2)}, u32[]{:S(2)}) collective-permute-start(bf16[320,128]{1,0:T(8,128)(2,1)S(1)} %get-tuple-element.66.refs_4_), channel_id=1, source_target_pairs={{0,12},{4,8},{8,4},{12,0},{16,28},{20,24},{24,20},{28,16},{1,13},{... | collective-permute-start | bytes 245768 | tf_op jit(solution)/shard_map/ppermute | solution.py:437
  29.7 5.6 %collective-permute-start.17 = (bf16[320,128]{1,0:T(8,128)(2,1)S(1)}, bf16[320,128]{1,0:T(8,128)(2,1)S(1)}, u32[]{:S(2)}, u32[]{:S(2)}) collective-permute-start(bf16[320,128]{1,0:T(8,128)(2,1)S(1)} %get-tuple-element.66.refs_4_), channel_id=1, source_target_pairs={{0,8},{4,12},{8,0},{12,4},{16,24},{20,28},{24,16},{28,20},{1,9},{5... | collective-permute-start | bytes 245768 | tf_op jit(solution)/shard_map/ppermute | solution.py:437
  29.7 5.6 %collective-permute-start.16 = (bf16[320,128]{1,0:T(8,128)(2,1)S(1)}, bf16[320,128]{1,0:T(8,128)(2,1)S(1)}, u32[]{:S(2)}, u32[]{:S(2)}) collective-permute-start(bf16[320,128]{1,0:T(8,128)(2,1)S(1)} %get-tuple-element.66.refs_4_), channel_id=1, source_target_pairs={{0,4},{4,0},{8,12},{12,8},{16,20},{20,16},{24,28},{28,24},{1,5},{5... | collective-permute-start | bytes 245768 | tf_op jit(solution)/shard_map/ppermute | solution.py:437
  32.4 8.2 %collective-permute-start.11 = (bf16[256,128]{1,0:T(8,128)(2,1)S(1)}, bf16[256,128]{1,0:T(8,128)(2,1)S(1)}, u32[]{:S(2)}, u32[]{:S(2)}) collective-permute-start(bf16[256,128]{1,0:T(8,128)(2,1)S(1)} %get-tuple-element.59), channel_id=1, source_target_pairs={{0,16},{4,20},{8,24},{12,28},{16,0},{20,4},{24,8},{28,12},{1,17},{... | collective-permute-start | bytes 196616 | tf_op jit(solution)/shard_map/ppermute | solution.py:437
  34.6 8.2 %collective-permute-start.12 = (bf16[256,128]{1,0:T(8,128)(2,1)S(1)}, bf16[256,128]{1,0:T(8,128)(2,1)S(1)}, u32[]{:S(2)}, u32[]{:S(2)}) collective-permute-start(bf16[256,128]{1,0:T(8,128)(2,1)S(1)} %get-tuple-element.62), channel_id=1, source_target_pairs={{0,16},{4,20},{8,24},{12,28},{16,0},{20,4},{24,8},{28,12},{1,17},{... | collective-permute-start | bytes 196616 | tf_op jit(solution)/shard_map/ppermute | solution.py:437
  35.9 13.3 %collective-permute-start.19 = (bf16[320,128]{1,0:T(8,128)(2,1)S(1)}, bf16[320,128]{1,0:T(8,128)(2,1)S(1)}, u32[]{:S(2)}, u32[]{:S(2)}) collective-permute-start(bf16[320,128]{1,0:T(8,128)(2,1)S(1)} %get-tuple-element.69), channel_id=1, source_target_pairs={{0,16},{4,20},{8,24},{12,28},{16,0},{20,4},{24,8},{28,12},{1,17},{... | collective-permute-start | bytes 245768 | tf_op jit(solution)/shard_map/ppermute | solution.py:437
  40.6 4.6 %collective-permute-start.14 = (bf16[192,128]{1,0:T(8,128)(2,1)S(1)}, bf16[192,128]{1,0:T(8,128)(2,1)S(1)}, u32[]{:S(2)}, u32[]{:S(2)}) collective-permute-start(bf16[192,128]{1,0:T(8,128)(2,1)S(1)} %get-tuple-element.64), channel_id=1, source_target_pairs={{0,8},{4,12},{8,0},{12,4},{16,24},{20,28},{24,16},{28,20},{1,9},{5... | collective-permute-start | bytes 147464 | tf_op jit(solution)/shard_map/ppermute | solution.py:437
  42.8 4.2 %collective-permute-start.13 = (bf16[192,128]{1,0:T(8,128)(2,1)S(1)}, bf16[192,128]{1,0:T(8,128)(2,1)S(1)}, u32[]{:S(2)}, u32[]{:S(2)}) collective-permute-start(bf16[192,128]{1,0:T(8,128)(2,1)S(1)} %get-tuple-element.63), channel_id=1, source_target_pairs={{0,4},{4,0},{8,12},{12,8},{16,20},{20,16},{24,28},{28,24},{1,5},{5... | collective-permute-start | bytes 147464 | tf_op jit(solution)/shard_map/ppermute | solution.py:437
  44.2 5.0 %collective-permute-start.15 = (bf16[192,128]{1,0:T(8,128)(2,1)S(1)}, bf16[192,128]{1,0:T(8,128)(2,1)S(1)}, u32[]{:S(2)}, u32[]{:S(2)}) collective-permute-start(bf16[192,128]{1,0:T(8,128)(2,1)S(1)} %get-tuple-element.65), channel_id=1, source_target_pairs={{0,12},{4,8},{8,4},{12,0},{16,28},{20,24},{24,20},{28,16},{1,13},{... | collective-permute-start | bytes 147464 | tf_op jit(solution)/shard_map/ppermute | solution.py:437

commit v6 on v5

--- a/solution.py
+++ b/solution.py
@@ -104,27 +104,58 @@
         out_ref[k * rows : (k + 1) * rows] = ref[0:rows]
 
 
+def slope_of(acc):
+    s = jax.nn.sigmoid(acc)
+    return s * (1.0 + acc * (1.0 - s))
+
+
+def window(w, ref, c, first, count, step):
+    acc = jnp.zeros((count, 128), F32)
+    for j in range(w.shape[0]):
+        at = first + step * j
+        acc = acc + w[j : j + 1] * ref[c, at : at + count]
+    return acc
+
+
+def interior_kernel(total_ref, x_ref, g_ref, w_ref, after_ref, xs, gs, sums):
+    rows = x_ref.shape[0]
+    half = w_ref.shape[0] // 2
+    shift = HALO_X - HALO_G - half
+    inner = 2 * HALO_G
+    first = lax.axis_index("ctx") * rows
+    for c in range(xs.shape[0]):
+        cols = slice(c * 128, (c + 1) * 128)
+        own = slice(HALO_X, HALO_X + rows)
+        pos = first + lax.broadcasted_iota(jnp.int32, (rows, 128), 0)
+        xs[c, own] = jnp.where(pos < total_ref[0:1], x_ref[:, cols].astype(F32), 0.0)
+        w = w_ref[:, cols].astype(F32)
+        slope = slope_of(window(w, xs, c, shift + inner, rows - inner, 1))
+        grad = g_ref[HALO_G : rows - HALO_G, cols].astype(F32) * slope
+        gs[c, inner:rows] = grad.astype(BF).astype(F32)
+        sums[c] = window(w, gs, c, inner + HALO_G + half, rows - 2 * inner, -1)
+
+
 def conv_kernel(
     total_ref,
-    x_ref,
     g_ref,
     w_ref,
     one_ref,
     three_ref,
     edge_ref,
+    xs_in,
+    gs_in,
+    sums,
     out_ref,
     send_ref,
     mine_ref,
     xs,
     gs,
 ):
-    rows = x_ref.shape[0]
-    taps = w_ref.shape[0]
-    half = taps // 2
-    wide = rows + 2 * HALO_G
+    rows = g_ref.shape[0]
+    half = w_ref.shape[0] // 2
     shift = HALO_X - HALO_G - half
-    size = edge_ref.shape[0]
-    start = one_ref.shape[0] - size
+    inner = 2 * HALO_G
+    start = one_ref.shape[0] - edge_ref.shape[0]
     me = member()
     one, three, edge = (
         one_ref[start:].astype(F32),
@@ -134,30 +165,35 @@
     low = jnp.where(me == 0, edge, jnp.where(me == 2, three, one))
     high = jnp.where(me == 3, edge, jnp.where(me == 1, three, one))
     first = lax.axis_index("ctx") * rows
+    total = total_ref[0:1]
     for c in range(xs.shape[0]):
         cols = slice(c * 128, (c + 1) * 128)
         at = c * (HALO_X + HALO_G)
-        xs[c, 0:HALO_X] = low[at : at + HALO_X]
-        xs[c, HALO_X : HALO_X + rows] = x_ref[:, cols].astype(F32)
-        xs[c, HALO_X + rows :] = high[at : at + HALO_X]
-        pos = first - HALO_X + lax.broadcasted_iota(jnp.int32, xs.shape[1:], 0)
-        xs[c] = jnp.where(pos < total_ref[0:1], xs[c], 0.0)
+        step = lax.broadcasted_iota(jnp.int32, (HALO_X, 128), 0)
+        xs[c, 0:HALO_X] = jnp.where(first - HALO_X + step < total, low[at : at + HALO_X], 0.0)
+        xs[c, HALO_X : HALO_X + rows] = xs_in[c, HALO_X : HALO_X + rows]
+        xs[c, HALO_X + rows :] = jnp.where(first + rows + step < total, high[at : at + HALO_X], 0.0)
         w = w_ref[:, cols].astype(F32)
-        acc = jnp.zeros((wide, 128), F32)
-        for j in range(taps):
-            acc = acc + w[j : j + 1] * xs[c, shift + j : shift + j + wide]
-        s = jax.nn.sigmoid(acc)
-        slope = s * (1.0 + acc * (1.0 - s))
-        gs[c, 0:HALO_G] = low[at + HALO_X : at + HALO_X + HALO_G]
-        gs[c, HALO_G : HALO_G + rows] = g_ref[:, cols].astype(F32)
-        gs[c, HALO_G + rows :] = high[at + HALO_X : at + HALO_X + HALO_G]
-        gs[c] = (gs[c] * slope).astype(BF).astype(F32)
-        acc = jnp.zeros((rows, 128), F32)
-        for j in range(taps):
-            to = HALO_G + half - j
-            acc = acc + w[j : j + 1] * gs[c, to : to + rows]
+        gs[c, inner:rows] = gs_in[c, inner:rows]
+        g_low = low[at + HALO_X : at + HALO_X + HALO_G]
+        g_high = high[at + HALO_X : at + HALO_X + HALO_G]
+        for to, parts in (
+            (0, (g_low, g_ref[0:HALO_G, cols].astype(F32))),
+            (rows, (g_ref[rows - HALO_G :, cols].astype(F32), g_high)),
+        ):
+            slope = slope_of(window(w, xs, c, shift + to, inner, 1))
+            grad = jnp.concatenate(parts, 0) * slope
+            gs[c, to : to + inner] = grad.astype(BF).astype(F32)
+        acc = jnp.concatenate(
+            [
+                window(w, gs, c, HALO_G + half, inner, -1),
+                sums[c],
+                window(w, gs, c, rows - inner + HALO_G + half, inner, -1),
+            ],
+            0,
+        )
         pos = first + lax.broadcasted_iota(jnp.int32, acc.shape, 0)
-        acc = jnp.where(pos < total_ref[0:1], acc, 0.0)
+        acc = jnp.where(pos < total, acc, 0.0)
         out = (g_ref[:, cols].astype(F32) + acc).astype(BF)
         out_ref[:, cols] = out
         send_ref[:, cols] = out
@@ -284,7 +320,7 @@
     got, gos, rest = rest[:MEMBERS], rest[MEMBERS : 2 * MEMBERS], rest[2 * MEMBERS :]
     kv, rest = rest[:n_keys], rest[n_keys:]
     dkv, (dq_ref, s_ref, d_ref, acc_ref) = rest[:-4], rest[-4:]
-    groups, keys, queries = s_ref.shape
+    groups, _, queries = s_ref.shape
     q = queries_of(got, scale)
     half = queries // MEMBERS // 2
     go = widened(jnp.concatenate([r[0:half] for r in gos], 0), True).astype(BF)
@@ -303,18 +339,52 @@
         ds = (p.astype(F32) * (s_ref[g] - d_ref[...])).astype(BF)
         acc_ref[...] += dot(key_block(kv, g), ds, ((0,), (0,)))
         out = (dot(ds, q, ((1,), (0,))) + dot(p, go, ((1,), (0,)))).astype(BF)
-        if len(dkv) == 1:
-            dkv[0][g] = out
-        elif g == 0:
-            dkv[0][...] = out
-        else:
-            rows = keys // MEMBERS
-            for half, ref in zip(HALVES, dkv[1:]):
-                for i, k in enumerate(half):
-                    ref[i * rows : (i + 1) * rows] = out[k * rows : (k + 1) * rows]
+        dkv[0][g] = out
 
     over(groups, grads)
     dq = (acc_ref[0:HEAD_DIM, :] * scale).T.astype(BF)
+    half = queries // 2
+    dq_ref[:, 0:HEAD_DIM] = dq[0:half]
+    dq_ref[:, HEAD_DIM:] = dq[half:]
+
+
+def send_kernel(scale, p_ref, *rest):
+    got, gos, rest = rest[:MEMBERS], rest[MEMBERS : 2 * MEMBERS], rest[2 * MEMBERS :]
+    own_ref, other_ref, *dkv, s_ref, d_ref = rest
+    _, keys, queries = s_ref.shape
+    q = queries_of(got, scale)
+    half = queries // MEMBERS // 2
+    go = widened(jnp.concatenate([r[0:half] for r in gos], 0), True).astype(BF)
+    delta = jnp.zeros((1, queries), F32)
+    for g, kv in enumerate((own_ref, other_ref)):
+        s = dot(kv[...], go, ((1,), (1,)))
+        s_ref[g] = s
+        delta = delta + jnp.sum(s * p_ref[g].astype(F32), axis=0, keepdims=True)
+    d_ref[...] = jnp.broadcast_to(delta, d_ref.shape)
+    p = p_ref[1]
+    ds = (p.astype(F32) * (s_ref[1] - delta)).astype(BF)
+    out = (dot(ds, q, ((1,), (0,))) + dot(p, go, ((1,), (0,)))).astype(BF)
+    rows = keys // MEMBERS
+    for blocks, ref in zip(HALVES, dkv):
+        for i, k in enumerate(blocks):
+            ref[i * rows : (i + 1) * rows] = out[k * rows : (k + 1) * rows]
+
+
+def own_kernel(scale, p_ref, s_ref, d_ref, *rest):
+    got, gos, rest = rest[:MEMBERS], rest[MEMBERS : 2 * MEMBERS], rest[2 * MEMBERS :]
+    own_ref, other_ref, dkv_ref, dq_ref = rest
+    queries = s_ref.shape[2]
+    q = queries_of(got, scale)
+    half = queries // MEMBERS // 2
+    go = widened(jnp.concatenate([r[0:half] for r in gos], 0), True).astype(BF)
+    acc = jnp.zeros((128, queries), F32)
+    for g, kv in enumerate((own_ref, other_ref)):
+        p = p_ref[g]
+        ds = (p.astype(F32) * (s_ref[g] - d_ref[0:1])).astype(BF)
+        acc = acc + dot(kv[...], ds, ((0,), (0,)))
+        if g == 0:
+            dkv_ref[...] = (dot(ds, q, ((1,), (0,))) + dot(p, go, ((1,), (0,)))).astype(BF)
+    dq = (acc[0:HEAD_DIM, :] * scale).T.astype(BF)
     half = queries // 2
     dq_ref[:, 0:HEAD_DIM] = dq[0:half]
     dq_ref[:, HEAD_DIM:] = dq[half:]
@@ -466,11 +536,18 @@
     got = swap(slots)
     borders = [i for i in range(members, n_ctx, members)]
     edge = move(edge, [(i - 1, i) for i in borders] + [(i, i - 1) for i in borders])
+    wide_x = shape((sides, rows + 2 * HALO_X, 128), F32)
+    wide_g = shape((sides, rows + 2 * HALO_G, 128), F32)
+    inside = call(
+        interior_kernel,
+        (wide_x, wide_g, shape((sides, rows - 4 * HALO_G, 128), F32)),
+        (total, x_in, g_in, w_in, slots[2]),
+    )
     x_grad, x_send, grad_conv, masked = call(
         conv_kernel,
-        (shape((rows, width), BF),) * 3 + (shape((sides, rows + 2 * HALO_X, 128), F32),),
-        (total, x_in, g_in, w_in, got[1], got[3], edge),
-        scratch=[pltpu.VMEM((sides, rows + 2 * HALO_G, 128), F32)],
+        (shape((rows, width), BF),) * 3 + (wide_x,),
+        (total, g_in, w_in, got[1], got[3], edge, *inside),
+        scratch=[pltpu.VMEM(wide_g.shape, F32)],
     )
     xs = [x_send] + [by_xor(x_send, k, "head") for k in range(1, n_heads)]
     own_kv = call(join_kernel, shape((keys, 128), BF), got)
@@ -523,24 +600,37 @@
         limit=big,
     )
     probs = fwd[0]
-    bwd = call(
-        functools.partial(backward_kernel, n_keys, scale),
-        (
-            (shape((keys, 128), BF), shape((keys // 2, 128), BF), shape((keys // 2, 128), BF))
-            if pair
-            else (shape((groups, keys, 128), BF),)
+    if pair:
+        *leaving, slopes, delta = call(
+            functools.partial(send_kernel, scale),
+            tuple(shape((len(h) * rows, 128), BF) for h in HALVES)
+            + (shape((groups, keys, queries), F32), shape((8, queries), F32)),
+            (probs, *got, *gos, *kv),
+            flops=2 * flops,
+            limit=big,
         )
-        + (shape((queries // 2, 128), BF),),
-        (probs, *got, *gos, *kv),
-        scratch=[
-            pltpu.VMEM((groups, keys, queries), F32),
-            pltpu.VMEM((1, queries), F32),
-            pltpu.VMEM((128, queries), F32),
-        ],
-        flops=4 * flops,
-        limit=big,
-    )
-    dq = bwd[-1]
+        own, dq = call(
+            functools.partial(own_kernel, scale),
+            (shape((keys, 128), BF), shape((queries // 2, 128), BF)),
+            (probs, slopes, delta, *got, *gos, *kv),
+            flops=2 * flops,
+            limit=big,
+        )
+        bwd = (own, *leaving)
+    else:
+        bwd = call(
+            functools.partial(backward_kernel, n_keys, scale),
+            (shape((groups, keys, 128), BF), shape((queries // 2, 128), BF)),
+            (probs, *got, *gos, *kv),
+            scratch=[
+                pltpu.VMEM((groups, keys, queries), F32),
+                pltpu.VMEM((1, queries), F32),
+                pltpu.VMEM((128, queries), F32),
+            ],
+            flops=4 * flops,
+            limit=big,
+        )
+        dq = bwd[1]
     slot = shape((rows + half, 128), BF)
     slots = [None] * members
     if pair:

time: 50.2 us -> 49.2 us (0.980)
  waiting for transfers between devices: 17.2 us -> 13.9 us
  local copies, waits for them, and re-layouts: 0.01 us -> 1.04 us
  starting transfers between devices: 24.2 us -> 25.2 us
    ppermute x20, waiting for transfers between devices: 17.2 us -> 13.9 us  [move(): return lax.ppermute(x, axis, pairs)]
    unnamed x2, local copies, waits for them, and re-layouts: 0.01 us -> 1.04 us
    ppermute x20, starting transfers between devices: 24.2 us -> 25.2 us  [move(): return lax.ppermute(x, axis, pairs)]
    pallas_call x11 -> x13, Pallas kernels: 7.91 us -> 8.06 us  [call(): pl.pallas_call(kernel, out_shape=out_shape, in_specs=[SM] * smem + [HB] *...]
where the time goes in v6:
time: 49.2 us; the launch traced here: 49 us
  starting transfers between devices  25.2 us (51%)
  waiting for transfers between devices  13.9 us (28%)
  Pallas kernels  8.06 us (16%)
  local copies, waits for them, and re-layouts  1.04 us (2%)
  between operations  0.73 us (1%)
    ppermute x20, starting transfers between devices, move(): return lax.ppermute(x, axis, pairs)  25.2 us
    ppermute x20, waiting for transfers between devices, move(): return lax.ppermute(x, axis, pairs)  13.9 us
    pallas_call x13, Pallas kernels, call(): pl.pallas_call(kernel, out_shape=out_shape, in_specs=[SM] * smem + [HB] *...  8.06 us
    unnamed x2, local copies, waits for them, and re-layouts  1.04 us
  transfers between devices with their start and end apart: 20, of which 9 were waited for; matrix products, arithmetic and copies ran while one was open for 0% of the time, Pallas kernels for 12%

profile of v6, /device:TPU:0, one launch (start us, length us, event | category | flops | bytes accessed | tf_op | source)
XLA Modules:
  0.0 49.0 jit_solution(4070366406180187929)
XLA Ops:
  0.6 1.2 %shard_map.127 = (bf16[128,256]{1,0:T(8,128)(2,1)S(1)}, bf16[128,256]{1,0:T(8,128)(2,1)S(1)}, bf16[31,256]{1,0:T(8,128)(2,1)S(1)}, s32[8,128]{1,0:T(8,128)S(1)},...) custom-call(bf16[128,256]{1,0:T(8,128)(2,1)} %refs_0_.1, ...), custom_call_target="tpu_custom_call" | custom-call | flops 1048576 | bytes 1048576 | tf_op jit(solution)/shard_map/pallas_call | solution.py:27
  1.9 3.1 %collective-permute-start = (bf16[288,128]{1,0:T(8,128)(2,1)S(1)}, bf16[288,128]{1,0:T(8,128)(2,1)S(1)}, u32[]{:S(2)}, u32[]{:S(2)}) collective-permute-start(bf16[288,128]{1,0:T(8,128)(2,1)S(1)} %get-tuple-element.49), channel_id=1, source_target_pairs={{0,4},{4,0},{8,12},{12,8},{16,20},{20,16},{24,28},{28,24},{1,5},{5... | collective-permute-start | bytes 221192 | tf_op jit(solution)/shard_map/ppermute | solution.py:507
  4.9 1.5 %collective-permute-start.1 = (bf16[288,128]{1,0:T(8,128)(2,1)S(1)}, bf16[288,128]{1,0:T(8,128)(2,1)S(1)}, u32[]{:S(2)}, u32[]{:S(2)}) collective-permute-start(bf16[288,128]{1,0:T(8,128)(2,1)S(1)} %get-tuple-element.50), channel_id=1, source_target_pairs={{0,12},{4,8},{8,4},{12,0},{16,28},{20,24},{24,20},{28,16},{1,13},{... | collective-permute-start | bytes 221192 | tf_op jit(solution)/shard_map/ppermute | solution.py:507
  7.2 3.4 %collective-permute-done.6.refs_2_.rest_2_ = bf16[192,128]{1,0:T(8,128)(2,1)S(1)} collective-permute-done((bf16[192,128]{1,0:T(8,128)(2,1)S(1)}, bf16[192,128]{1,0:T(8,128)(2,1)S(1)}, u32[]{:S(2)}, u32[]{:S(2)}) %collective-permute-start.6) | collective-permute-done | bytes 49184 | tf_op jit(solution)/shard_map/ppermute | solution.py:507
  10.6 2.7 %collective-permute-start.7 = (bf16[512,128]{1,0:T(8,128)(2,1)S(1)}, bf16[512,128]{1,0:T(8,128)(2,1)S(1)}, u32[]{:S(2)}, u32[]{:S(2)}) collective-permute-start(bf16[512,128]{1,0:T(8,128)(2,1)S(1)} %shard_map.132.rest_4_.rest_8_), channel_id=1, source_target_pairs={{0,16},{4,20},{8,24},{12,28},{16,0},{20,4},{24,8},{28,12},{1,17},{... | collective-permute-start | bytes 393224 | tf_op jit(solution)/shard_map/ppermute | solution.py:507
  13.7 1.0 %shard_map.129 = (bf16[128,256]{1,0:T(8,128)(2,1)}, bf16[128,256]{1,0:T(8,128)(2,1)S(1)}, bf16[128,256]{1,0:T(8,128)(2,1)S(1)}, f32[2,192,128]{2,1,0:T(8,128)S(1)}) custom-call(s32[8,128]{1,0:T(8,128)S(1)} %get-tuple-element.46.total_ref, bf16[128,256]{1,0:T(8,128)(2,1)S(1)} %get-tuple-element.47.g_ref, bf16[31,256]{1,0:T(8,128)(2,1)S(1)} %get-tuple-element.48.w_ref, ...), custom_call_target="tpu_custom_call" | custom-call | flops 1048576 | bytes 1048576 | tf_op jit(solution)/shard_map/pallas_call | solution.py:27
  14.7 1.5 %collective-permute-start.4 = (bf16[128,256]{1,0:T(8,128)(2,1)S(1)}, bf16[128,256]{1,0:T(8,128)(2,1)S(1)}, u32[]{:S(2)}, u32[]{:S(2)}) collective-permute-start(bf16[128,256]{1,0:T(8,128)(2,1)S(1)} %get-tuple-element.59.rest_0_), channel_id=1, source_target_pairs={{0,2},{1,3},{2,0},{3,1},{4,6},{5,7},{6,4},{7,5},{8,10},{9,11},{10,... | collective-permute-start | bytes 196616 | tf_op jit(solution)/shard_map/ppermute | solution.py:507
  16.6 2.7 %collective-permute-done.4.rest_2_ = bf16[128,256]{1,0:T(8,128)(2,1)S(1)} collective-permute-done((bf16[128,256]{1,0:T(8,128)(2,1)S(1)}, bf16[128,256]{1,0:T(8,128)(2,1)S(1)}, u32[]{:S(2)}, u32[]{:S(2)}) %collective-permute-start.4) | collective-permute-done | bytes 65568 | tf_op jit(solution)/shard_map/ppermute | solution.py:507
  19.3 1.0 %collective-permute-done.5.rest_3_ = bf16[128,256]{1,0:T(8,128)(2,1)S(1)} collective-permute-done((bf16[128,256]{1,0:T(8,128)(2,1)S(1)}, bf16[128,256]{1,0:T(8,128)(2,1)S(1)}, u32[]{:S(2)}, u32[]{:S(2)}) %collective-permute-start.5) | collective-permute-done | bytes 65568 | tf_op jit(solution)/shard_map/ppermute | solution.py:507
  20.3 1.0 %copy-done = bf16[1024,256]{1,0:T(8,128)(2,1)S(1)} copy-done((bf16[1024,256]{1,0:T(8,128)(2,1)S(1)}, bf16[1024,256]{1,0:T(8,128)(2,1)}, u32[]{:S(2)}) %copy-start) | copy-done | bytes 524312
  21.6 1.5 %collective-permute-start.8 = (bf16[320,128]{1,0:T(8,128)(2,1)S(1)}, bf16[320,128]{1,0:T(8,128)(2,1)S(1)}, u32[]{:S(2)}, u32[]{:S(2)}) collective-permute-start(bf16[320,128]{1,0:T(8,128)(2,1)S(1)} %get-tuple-element.63), channel_id=1, source_target_pairs={{0,4},{4,0},{8,12},{12,8},{16,20},{20,16},{24,28},{28,24},{1,5},{5... | collective-permute-start | bytes 245768 | tf_op jit(solution)/shard_map/ppermute | solution.py:507
  23.2 2.0 %collective-permute-start.9 = (bf16[320,128]{1,0:T(8,128)(2,1)S(1)}, bf16[320,128]{1,0:T(8,128)(2,1)S(1)}, u32[]{:S(2)}, u32[]{:S(2)}) collective-permute-start(bf16[320,128]{1,0:T(8,128)(2,1)S(1)} %get-tuple-element.64), channel_id=1, source_target_pairs={{0,8},{4,12},{8,0},{12,4},{16,24},{20,28},{24,16},{28,20},{1,9},{5... | collective-permute-start | bytes 245768 | tf_op jit(solution)/shard_map/ppermute | solution.py:507
  25.6 1.5 %shard_map.133 = (bf16[2,512,512]{2,1,0:T(8,128)(2,1)S(1)}, bf16[320,128]{1,0:T(8,128)(2,1)S(1)}) custom-call(s32[8,128]{1,0:T(8,128)S(1)} %get-tuple-element.46.total_ref, bf16[64,128]{1,0:T(8,128)(2,1)S(1)} %shard_map.131.tap_ref, bf16[192,128]{1,0:T(8,128)(2,1)S(1)} %get-tuple-element.61.refs_0_.rest_0_, ...), custom_call_target="tpu_custom_call" | custom-call | flops 268435456 | bytes 1048576 | tf_op jit(solution)/shard_map/pallas_call | solution.py:27
  27.0 1.5 %collective-permute-start.16 = (bf16[320,128]{1,0:T(8,128)(2,1)S(1)}, bf16[320,128]{1,0:T(8,128)(2,1)S(1)}, u32[]{:S(2)}, u32[]{:S(2)}) collective-permute-start(bf16[320,128]{1,0:T(8,128)(2,1)S(1)} %get-tuple-element.76.refs_4_), channel_id=1, source_target_pairs={{0,4},{4,0},{8,12},{12,8},{16,20},{20,16},{24,28},{28,24},{1,5},{5... | collective-permute-start | bytes 245768 | tf_op jit(solution)/shard_map/ppermute | solution.py:507
  28.6 2.0 %collective-permute-start.17 = (bf16[320,128]{1,0:T(8,128)(2,1)S(1)}, bf16[320,128]{1,0:T(8,128)(2,1)S(1)}, u32[]{:S(2)}, u32[]{:S(2)}) collective-permute-start(bf16[320,128]{1,0:T(8,128)(2,1)S(1)} %get-tuple-element.76.refs_4_), channel_id=1, source_target_pairs={{0,8},{4,12},{8,0},{12,4},{16,24},{20,28},{24,16},{28,20},{1,9},{5... | collective-permute-start | bytes 245768 | tf_op jit(solution)/shard_map/ppermute | solution.py:507
  30.7 1.0 %shard_map.134 = (bf16[256,128]{1,0:T(8,128)(2,1)S(1)}, bf16[256,128]{1,0:T(8,128)(2,1)S(1)}, f32[2,512,512]{2,1,0:T(8,128)S(1)}, f32[8,512]{1,0:T(8,128)S(1)}) custom-call(bf16[2,512,512]{2,1,0:T(8,128)(2,1)S(1)} %get-tuple-element.62.p_ref, bf16[192,128]{1,0:T(8,128)(2,1)S(1)} %get-tuple-element.61.refs_0_.rest_0_, ...), custom_call_target="tpu_custom_call" | custom-call | flops 268435456 | bytes 1048576 | tf_op jit(solution)/shard_map/pallas_call | solution.py:27
  31.7 2.6 %collective-permute-start.12 = (bf16[256,128]{1,0:T(8,128)(2,1)S(1)}, bf16[256,128]{1,0:T(8,128)(2,1)S(1)}, u32[]{:S(2)}, u32[]{:S(2)}) collective-permute-start(bf16[256,128]{1,0:T(8,128)(2,1)S(1)} %get-tuple-element.72), channel_id=1, source_target_pairs={{0,16},{4,20},{8,24},{12,28},{16,0},{20,4},{24,8},{28,12},{1,17},{... | collective-permute-start | bytes 196616 | tf_op jit(solution)/shard_map/ppermute | solution.py:507
  34.7 2.1 %collective-permute-done.18.refs_7_ = bf16[320,128]{1,0:T(8,128)(2,1)S(1)} collective-permute-done((bf16[320,128]{1,0:T(8,128)(2,1)S(1)}, bf16[320,128]{1,0:T(8,128)(2,1)S(1)}, u32[]{:S(2)}, u32[]{:S(2)}) %collective-permute-start.18) | collective-permute-done | bytes 81952 | tf_op jit(solution)/shard_map/ppermute | solution.py:507
  38.6 1.5 %collective-permute-done.12.refs_0_ = bf16[256,128]{1,0:T(8,128)(2,1)S(1)} collective-permute-done((bf16[256,128]{1,0:T(8,128)(2,1)S(1)}, bf16[256,128]{1,0:T(8,128)(2,1)S(1)}, u32[]{:S(2)}, u32[]{:S(2)}) %collective-permute-start.12) | collective-permute-done | bytes 65568 | tf_op jit(solution)/shard_map/ppermute | solution.py:507
  40.2 1.7 %collective-permute-start.13 = (bf16[192,128]{1,0:T(8,128)(2,1)S(1)}, bf16[192,128]{1,0:T(8,128)(2,1)S(1)}, u32[]{:S(2)}, u32[]{:S(2)}) collective-permute-start(bf16[192,128]{1,0:T(8,128)(2,1)S(1)} %get-tuple-element.73), channel_id=1, source_target_pairs={{0,4},{4,0},{8,12},{12,8},{16,20},{20,16},{24,28},{28,24},{1,5},{5... | collective-permute-start | bytes 147464 | tf_op jit(solution)/shard_map/ppermute | solution.py:507
  42.6 3.0 %collective-permute-start.15 = (bf16[192,128]{1,0:T(8,128)(2,1)S(1)}, bf16[192,128]{1,0:T(8,128)(2,1)S(1)}, u32[]{:S(2)}, u32[]{:S(2)}) collective-permute-start(bf16[192,128]{1,0:T(8,128)(2,1)S(1)} %get-tuple-element.75), channel_id=1, source_target_pairs={{0,12},{4,8},{8,4},{12,0},{16,28},{20,24},{24,20},{28,16},{1,13},{... | collective-permute-start | bytes 147464 | tf_op jit(solution)/shard_map/ppermute | solution.py:507
  45.5 1.1 %collective-permute-done.14.refs_2_ = bf16[192,128]{1,0:T(8,128)(2,1)S(1)} collective-permute-done((bf16[192,128]{1,0:T(8,128)(2,1)S(1)}, bf16[192,128]{1,0:T(8,128)(2,1)S(1)}, u32[]{:S(2)}, u32[]{:S(2)}) %collective-permute-start.14) | collective-permute-done | bytes 49184 | tf_op jit(solution)/shard_map/ppermute | solution.py:507
  46.6 1.5 %collective-permute-done.15.refs_3_ = bf16[192,128]{1,0:T(8,128)(2,1)S(1)} collective-permute-done((bf16[192,128]{1,0:T(8,128)(2,1)S(1)}, bf16[192,128]{1,0:T(8,128)(2,1)S(1)}, u32[]{:S(2)}, u32[]{:S(2)}) %collective-permute-start.15) | collective-permute-done | bytes 49184 | tf_op jit(solution)/shard_map/ppermute | solution.py:507
  48.1 0.9 %shard_map.139 = (bf16[128,256]{1,0:T(8,128)(2,1)}, bf16[128,256]{1,0:T(8,128)(2,1)}, bf16[128,256]{1,0:T(8,128)(2,1)}, f32[128,256]{1,0:T(8,128)}, f32[31,256]{1,0:T(8,128)}) custom-call(bf16[192,128]{1,0:T(8,128)(2,1)S(1)} %get-tuple-element.71.refs_0_, bf16[192,128]{1,0:T(8,128)(2,1)S(1)} %collective-permute-done.13.refs_1_, ...), custom_call_target="tpu_custom_call" | custom-call | flops 1048576 | bytes 1048576 | tf_op jit(solution)/shard_map/pallas_call | solution.py:27
  (31 shorter events, 5.2 us)
Async XLA Ops:
  1.9 8.7 %collective-permute-start = (bf16[288,128]{1,0:T(8,128)(2,1)S(1)}, bf16[288,128]{1,0:T(8,128)(2,1)S(1)}, u32[]{:S(2)}, u32[]{:S(2)}) collective-permute-start(bf16[288,128]{1,0:T(8,128)(2,1)S(1)} %get-tuple-element.49), channel_id=1, source_target_pairs={{0,4},{4,0},{8,12},{12,8},{16,20},{20,16},{24,28},{28,24},{1,5},{5... | collective-permute-start | bytes 221192 | tf_op jit(solution)/shard_map/ppermute | solution.py:507
  4.9 5.7 %collective-permute-start.1 = (bf16[288,128]{1,0:T(8,128)(2,1)S(1)}, bf16[288,128]{1,0:T(8,128)(2,1)S(1)}, u32[]{:S(2)}, u32[]{:S(2)}) collective-permute-start(bf16[288,128]{1,0:T(8,128)(2,1)S(1)} %get-tuple-element.50), channel_id=1, source_target_pairs={{0,12},{4,8},{8,4},{12,0},{16,28},{20,24},{24,20},{28,16},{1,13},{... | collective-permute-start | bytes 221192 | tf_op jit(solution)/shard_map/ppermute | solution.py:507
  6.4 4.1 %collective-permute-start.6 = (bf16[192,128]{1,0:T(8,128)(2,1)S(1)}, bf16[192,128]{1,0:T(8,128)(2,1)S(1)}, u32[]{:S(2)}, u32[]{:S(2)}) collective-permute-start(bf16[192,128]{1,0:T(8,128)(2,1)S(1)} %get-tuple-element.53.after_ref), channel_id=1, source_target_pairs={{0,8},{4,12},{8,0},{12,4},{16,24},{20,28},{24,16},{28,20},{1,9},{5... | collective-permute-start | bytes 147464 | tf_op jit(solution)/shard_map/ppermute | solution.py:507
  6.5 7.2 %collective-permute-start.2 = (bf16[96,128]{1,0:T(8,128)(2,1)S(1)}, bf16[96,128]{1,0:T(8,128)(2,1)S(1)}, u32[]{:S(2)}, u32[]{:S(2)}) collective-permute-start(bf16[96,128]{1,0:T(8,128)(2,1)S(1)} %get-tuple-element.51), channel_id=1, source_target_pairs={{12,16},{16,12},{13,17},{17,13},{14,18},{18,14},{15,19},{19,15}} | collective-permute-start | bytes 73736 | tf_op jit(solution)/shard_map/ppermute | solution.py:507
  10.6 15.0 %collective-permute-start.7 = (bf16[512,128]{1,0:T(8,128)(2,1)S(1)}, bf16[512,128]{1,0:T(8,128)(2,1)S(1)}, u32[]{:S(2)}, u32[]{:S(2)}) collective-permute-start(bf16[512,128]{1,0:T(8,128)(2,1)S(1)} %shard_map.132.rest_4_.rest_8_), channel_id=1, source_target_pairs={{0,16},{4,20},{8,24},{12,28},{16,0},{20,4},{24,8},{28,12},{1,17},{... | collective-permute-start | bytes 393224 | tf_op jit(solution)/shard_map/ppermute | solution.py:507
  14.7 1.9 %collective-permute-start.3 = (bf16[128,256]{1,0:T(8,128)(2,1)S(1)}, bf16[128,256]{1,0:T(8,128)(2,1)S(1)}, u32[]{:S(2)}, u32[]{:S(2)}) collective-permute-start(bf16[128,256]{1,0:T(8,128)(2,1)S(1)} %get-tuple-element.59.rest_0_), channel_id=1, source_target_pairs={{0,1},{1,0},{2,3},{3,2},{4,5},{5,4},{6,7},{7,6},{8,9},{9,8},{10,11... | collective-permute-start | bytes 196616 | tf_op jit(solution)/shard_map/ppermute | solution.py:507
  14.7 4.5 %collective-permute-start.4 = (bf16[128,256]{1,0:T(8,128)(2,1)S(1)}, bf16[128,256]{1,0:T(8,128)(2,1)S(1)}, u32[]{:S(2)}, u32[]{:S(2)}) collective-permute-start(bf16[128,256]{1,0:T(8,128)(2,1)S(1)} %get-tuple-element.59.rest_0_), channel_id=1, source_target_pairs={{0,2},{1,3},{2,0},{3,1},{4,6},{5,7},{6,4},{7,5},{8,10},{9,11},{10,... | collective-permute-start | bytes 196616 | tf_op jit(solution)/shard_map/ppermute | solution.py:507
  16.2 4.0 %collective-permute-start.5 = (bf16[128,256]{1,0:T(8,128)(2,1)S(1)}, bf16[128,256]{1,0:T(8,128)(2,1)S(1)}, u32[]{:S(2)}, u32[]{:S(2)}) collective-permute-start(bf16[128,256]{1,0:T(8,128)(2,1)S(1)} %get-tuple-element.59.rest_0_), channel_id=1, source_target_pairs={{0,3},{1,2},{2,1},{3,0},{4,7},{5,6},{6,5},{7,4},{8,11},{9,10},{10,... | collective-permute-start | bytes 196616 | tf_op jit(solution)/shard_map/ppermute | solution.py:507
  20.3 1.0 %copy-start = (bf16[1024,256]{1,0:T(8,128)(2,1)S(1)}, bf16[1024,256]{1,0:T(8,128)(2,1)}, u32[]{:S(2)}) copy-start(bf16[1024,256]{1,0:T(8,128)(2,1)} %proj_ref.1) | copy-start | bytes 1572868
  21.6 9.0 %collective-permute-start.8 = (bf16[320,128]{1,0:T(8,128)(2,1)S(1)}, bf16[320,128]{1,0:T(8,128)(2,1)S(1)}, u32[]{:S(2)}, u32[]{:S(2)}) collective-permute-start(bf16[320,128]{1,0:T(8,128)(2,1)S(1)} %get-tuple-element.63), channel_id=1, source_target_pairs={{0,4},{4,0},{8,12},{12,8},{16,20},{20,16},{24,28},{28,24},{1,5},{5... | collective-permute-start | bytes 245768 | tf_op jit(solution)/shard_map/ppermute | solution.py:507
  23.2 7.4 %collective-permute-start.9 = (bf16[320,128]{1,0:T(8,128)(2,1)S(1)}, bf16[320,128]{1,0:T(8,128)(2,1)S(1)}, u32[]{:S(2)}, u32[]{:S(2)}) collective-permute-start(bf16[320,128]{1,0:T(8,128)(2,1)S(1)} %get-tuple-element.64), channel_id=1, source_target_pairs={{0,8},{4,12},{8,0},{12,4},{16,24},{20,28},{24,16},{28,20},{1,9},{5... | collective-permute-start | bytes 245768 | tf_op jit(solution)/shard_map/ppermute | solution.py:507
  25.2 5.4 %collective-permute-start.10 = (bf16[320,128]{1,0:T(8,128)(2,1)S(1)}, bf16[320,128]{1,0:T(8,128)(2,1)S(1)}, u32[]{:S(2)}, u32[]{:S(2)}) collective-permute-start(bf16[320,128]{1,0:T(8,128)(2,1)S(1)} %get-tuple-element.65), channel_id=1, source_target_pairs={{0,12},{4,8},{8,4},{12,0},{16,28},{20,24},{24,20},{28,16},{1,13},{... | collective-permute-start | bytes 245768 | tf_op jit(solution)/shard_map/ppermute | solution.py:507
  27.0 7.6 %collective-permute-start.16 = (bf16[320,128]{1,0:T(8,128)(2,1)S(1)}, bf16[320,128]{1,0:T(8,128)(2,1)S(1)}, u32[]{:S(2)}, u32[]{:S(2)}) collective-permute-start(bf16[320,128]{1,0:T(8,128)(2,1)S(1)} %get-tuple-element.76.refs_4_), channel_id=1, source_target_pairs={{0,4},{4,0},{8,12},{12,8},{16,20},{20,16},{24,28},{28,24},{1,5},{5... | collective-permute-start | bytes 245768 | tf_op jit(solution)/shard_map/ppermute | solution.py:507
  28.6 6.1 %collective-permute-start.17 = (bf16[320,128]{1,0:T(8,128)(2,1)S(1)}, bf16[320,128]{1,0:T(8,128)(2,1)S(1)}, u32[]{:S(2)}, u32[]{:S(2)}) collective-permute-start(bf16[320,128]{1,0:T(8,128)(2,1)S(1)} %get-tuple-element.76.refs_4_), channel_id=1, source_target_pairs={{0,8},{4,12},{8,0},{12,4},{16,24},{20,28},{24,16},{28,20},{1,9},{5... | collective-permute-start | bytes 245768 | tf_op jit(solution)/shard_map/ppermute | solution.py:507
  30.6 6.2 %collective-permute-start.18 = (bf16[320,128]{1,0:T(8,128)(2,1)S(1)}, bf16[320,128]{1,0:T(8,128)(2,1)S(1)}, u32[]{:S(2)}, u32[]{:S(2)}) collective-permute-start(bf16[320,128]{1,0:T(8,128)(2,1)S(1)} %get-tuple-element.76.refs_4_), channel_id=1, source_target_pairs={{0,12},{4,8},{8,4},{12,0},{16,28},{20,24},{24,20},{28,16},{1,13},{... | collective-permute-start | bytes 245768 | tf_op jit(solution)/shard_map/ppermute | solution.py:507
  31.7 8.5 %collective-permute-start.12 = (bf16[256,128]{1,0:T(8,128)(2,1)S(1)}, bf16[256,128]{1,0:T(8,128)(2,1)S(1)}, u32[]{:S(2)}, u32[]{:S(2)}) collective-permute-start(bf16[256,128]{1,0:T(8,128)(2,1)S(1)} %get-tuple-element.72), channel_id=1, source_target_pairs={{0,16},{4,20},{8,24},{12,28},{16,0},{20,4},{24,8},{28,12},{1,17},{... | collective-permute-start | bytes 196616 | tf_op jit(solution)/shard_map/ppermute | solution.py:507
  34.3 8.1 %collective-permute-start.11 = (bf16[256,128]{1,0:T(8,128)(2,1)S(1)}, bf16[256,128]{1,0:T(8,128)(2,1)S(1)}, u32[]{:S(2)}, u32[]{:S(2)}) collective-permute-start(bf16[256,128]{1,0:T(8,128)(2,1)S(1)} %get-tuple-element.69), channel_id=1, source_target_pairs={{0,16},{4,20},{8,24},{12,28},{16,0},{20,4},{24,8},{28,12},{1,17},{... | collective-permute-start | bytes 196616 | tf_op jit(solution)/shard_map/ppermute | solution.py:507
  37.3 10.8 %collective-permute-start.19 = (bf16[320,128]{1,0:T(8,128)(2,1)S(1)}, bf16[320,128]{1,0:T(8,128)(2,1)S(1)}, u32[]{:S(2)}, u32[]{:S(2)}) collective-permute-start(bf16[320,128]{1,0:T(8,128)(2,1)S(1)} %get-tuple-element.79), channel_id=1, source_target_pairs={{0,16},{4,20},{8,24},{12,28},{16,0},{20,4},{24,8},{28,12},{1,17},{... | collective-permute-start | bytes 245768 | tf_op jit(solution)/shard_map/ppermute | solution.py:507
  40.2 5.3 %collective-permute-start.13 = (bf16[192,128]{1,0:T(8,128)(2,1)S(1)}, bf16[192,128]{1,0:T(8,128)(2,1)S(1)}, u32[]{:S(2)}, u32[]{:S(2)}) collective-permute-start(bf16[192,128]{1,0:T(8,128)(2,1)S(1)} %get-tuple-element.73), channel_id=1, source_target_pairs={{0,4},{4,0},{8,12},{12,8},{16,20},{20,16},{24,28},{28,24},{1,5},{5... | collective-permute-start | bytes 147464 | tf_op jit(solution)/shard_map/ppermute | solution.py:507
  42.5 4.2 %collective-permute-start.14 = (bf16[192,128]{1,0:T(8,128)(2,1)S(1)}, bf16[192,128]{1,0:T(8,128)(2,1)S(1)}, u32[]{:S(2)}, u32[]{:S(2)}) collective-permute-start(bf16[192,128]{1,0:T(8,128)(2,1)S(1)} %get-tuple-element.74), channel_id=1, source_target_pairs={{0,8},{4,12},{8,0},{12,4},{16,24},{20,28},{24,16},{28,20},{1,9},{5... | collective-permute-start | bytes 147464 | tf_op jit(solution)/shard_map/ppermute | solution.py:507
  42.6 5.6 %collective-permute-start.15 = (bf16[192,128]{1,0:T(8,128)(2,1)S(1)}, bf16[192,128]{1,0:T(8,128)(2,1)S(1)}, u32[]{:S(2)}, u32[]{:S(2)}) collective-permute-start(bf16[192,128]{1,0:T(8,128)(2,1)S(1)} %get-tuple-element.75), channel_id=1, source_target_pairs={{0,12},{4,8},{8,4},{12,0},{16,28},{20,24},{24,20},{28,16},{1,13},{... | collective-permute-start | bytes 147464 | tf_op jit(solution)/shard_map/ppermute | solution.py:507
